TPU v7x, 32 devices: a whole 2x2x4 slice. The times are simulated.
32 devices in a mesh: row: 8 (over y, x, core), col: 4 (over z).
Axes of the slice: x: 2, y: 2, z: 4, core: 2. Of those that a mesh axis runs over, the one named last changes fastest.
Arguments:
- panel: bfloat16 [24576, 256], P('row', 'col'), as said below
- trailing: bfloat16 [24576, 16384], P('row', 'col'), may hold values from -6 to 6
- tile_list: int32 [176], P('row'), may hold values from 0 to 23, as said below
Outputs:
- triangle: float32 [256, 256], replicated
- top_rows: float32 [16384, 256], P('col')
- updated: bfloat16 [22528, 16384], P('row', 'col')
Inputs may be any that keep to these rules, and one draw needn't show every extreme that they name: `tile_list`: each aligned block of 22 entries (the entries of one index of row) lists distinct tile numbers of that group's 24 tiles in increasing order and always includes tile 24 - 1. `panel`: the active rows of every row group, and all active rows together, have full column rank with a condition number under 100.
All inputs are finite; a program needn't handle non-finite values.
Results may differ from a plain program's by a relative error of at most 0.0065.
Values may be sent and summed in bfloat16 or wider, within the bound.
No kernel may reach another device: no remote copies, remote signals or barrier semaphores. Data moves between devices by JAX's collectives and lax.ppermute only.
A program may use at most 128 MiB of HBM per device.

v0:
```python
import jax
import jax.numpy as jnp
from jax import lax
from jax.sharding import PartitionSpec as P

TILE = 128


def pick_tiles(whole, tile_list):
    tiled = whole.reshape(-1, TILE, whole.shape[1])
    return jnp.take(tiled, tile_list, axis=0).reshape(-1, whole.shape[1])


def local(panel, trailing, tile_list):
    panel_full = lax.all_gather(panel, "col", axis=1, tiled=True)
    act_panel = pick_tiles(panel_full, tile_list)
    act_trail = pick_tiles(trailing, tile_list)
    local_gram = lax.dot_general(
        act_panel, act_panel, (((0,), (0,)), ((), ())), preferred_element_type=jnp.float32
    )
    gram_matrix = lax.psum(local_gram.astype(jnp.bfloat16), "row").astype(jnp.float32)
    lower_factor = jnp.linalg.cholesky(gram_matrix)
    triangle = lower_factor.T
    local_cross = lax.dot_general(
        act_trail, act_panel, (((0,), (0,)), ((), ())), preferred_element_type=jnp.float32
    )
    cross_sum = lax.psum(local_cross, "row")
    top_rows = jax.scipy.linalg.solve_triangular(lower_factor, cross_sum.T, lower=True).T
    coeff = jax.scipy.linalg.solve_triangular(
        lower_factor, top_rows.T, lower=True, trans=1
    ).T.astype(jnp.bfloat16)
    product = lax.dot_general(
        act_panel, coeff, (((1,), (1,)), ((), ())), preferred_element_type=jnp.float32
    )
    updated = (act_trail.astype(jnp.float32) - product).astype(jnp.bfloat16)
    return (triangle, top_rows, updated)


def solution(mesh):
    return jax.shard_map(
        local,
        mesh=mesh,
        in_specs=(P("row", "col"), P("row", "col"), P("row")),
        out_specs=(P(), P("col", None), P("row", "col")),
        check_vma=False,
    )
```

profile of v0, /device:TPU:17, one launch (start us, length us, event | category | flops | bytes accessed | tf_op | source)
XLA Modules:
  0.0 237.7 jit_solution(15465657170109536758)
XLA Ops:
  9.4 17.7 %gather_fusion.1 = bf16[22,128,4096]{2,1,0:T(8,128)(2,1)} fusion(bf16[24,128,4096]{2,1,0:T(8,128)(2,1)} %bitcast.57, s32[1024]{0:T(1024)S(1)} %pad_clamp_fusion), kind=kCustom, calls=%fused_computation.1 | custom fusion | bytes 46137432 | tf_op jit(solution)/shard_map/jit(_take)/gather | solution.py:11
  27.1 20.6 %bitcast_select_fusion = bf16[2816,4096]{1,0:T(8,128)(2,1)} fusion(bf16[22,128,4096]{2,1,0:T(8,128)(2,1)} %gather_fusion.1, pred[2816]{0:T(1024)(128)(4,1)S(1)} %broadcast_bitcast_fusion), kind=kLoop, calls=%fused_computation.5 | loop fusion | flops 11534336 | bytes 46140160 | tf_op jit(solution)/shard_map/jit(_take)/select_n | solution.py:11
  47.7 1.7 copy.11
  50.0 1.5 fusion.12
  51.6 12.2 %fusion.4 = f32[256,4096]{1,0:T(8,128)} fusion(bf16[22,128,4096]{2,1,0:T(8,128)(2,1)} %gather_fusion.1, pred[22]{0:T(512)(128)(4,1)S(1)} %compare_and_fusion, bf16[22,128,256]{2,1,0:T(8,128)(2,1)S(1)} %gather_fusion), kind=kOutput, calls=%fused_computation.10 | convolution fusion | flops 5917835264 | bytes 28704790 | tf_op jit(solution)/shard_map/dot_general | solution.py:24
  63.8 1.7 bitcast_select_fusion.1
  65.4 40.0 %all-reduce.4.cloned.1.call-done = bf16[256,256]{0,1:T(8,128)(2,1)} async-done(((bf16[256,256]{0,1:T(8,128)(2,1)}), bf16[256,256]{0,1:T(8,128)(2,1)}) %all-reduce.4.cloned.1.call-update) | async-done | bytes 131088 | tf_op jit(solution)/shard_map/psum | solution.py:21
  107.4 11.7 %cholesky.50 = f32[128,128]{1,0:T(8,128)S(1)} custom-call(f32[128,128]{1,0:T(8,128)S(1)} %cholesky.118), custom_call_target="Cholesky" | custom-call | tf_op jit(solution)/shard_map/jit(cholesky)/cholesky | solution.py:22
  119.2 9.8 %custom-call.18 = f32[1,128,128]{1,2,0:T(8,128)S(1)} custom-call(f32[1,128,128]{2,1,0:T(8,128)S(1)} %get-tuple-element.32), custom_call_target="InvertDiagBlocksLowerTriangular" | custom-call | tf_op jit(solution)/shard_map/jit(cholesky)/cholesky | solution.py:22
  129.5 11.7 %cholesky.105 = f32[128,128]{1,0:T(8,128)S(1)} custom-call(f32[128,128]{1,0:T(8,128)S(1)} %convolution_subtract_fusion.2), custom_call_target="Cholesky" | custom-call | tf_op jit(solution)/shard_map/jit(cholesky)/cholesky | solution.py:22
  144.1 4.0 %while.1 = (s32[]{:T(128)}, f32[256,256]{1,0:T(8,128)S(1)}, s32[2,2]{1,0:T(2,128)S(1)}, f32[2,128,128]{2,1,0:T(8,128)S(1)}, s32[]{:T(128)}) while((s32[]{:T(128)}, f32[256,256]{1,0:T(8,128)S(1)}, s32[2,2]{1,0:T(2,128)S(1)}, f32[2,128,128]{2,1,0:T(8,128)S(1)}, s32[]{:T(128)}) %tuple.31), condition=%wide.while_cond, body=%wide.while_body.sunk | while | flops 2 | bytes 131189 | solution.py:28
  144.7 1.4 bitcast_dynamic-update-slice_fusion.2
  146.8 1.4 bitcast_dynamic-update-slice_fusion.2
  148.2 19.9 %custom-call.19 = f32[2,128,128]{1,2,0:T(8,128)S(1)} custom-call(f32[2,128,128]{2,1,0:T(8,128)S(1)} %get-tuple-element.10), custom_call_target="InvertDiagBlocksLowerTriangular" | custom-call | tf_op jit(solution)/shard_map/jit(_solve_triangular)/triangular_solve | solution.py:28
  168.1 22.2 %all-reduce.6.cloned.1.call-done = f32[256,4096]{1,0:T(8,128)} async-done(((f32[256,4096]{1,0:T(8,128)}), f32[256,4096]{1,0:T(8,128)}) %all-reduce.6.cloned.1.call-update) | async-done | bytes 4194320 | tf_op jit(solution)/shard_map/psum | solution.py:27
  190.3 3.6 %fusion.7 = f32[128,4096]{1,0:T(8,128)S(1)} fusion(f32[256,4096]{1,0:T(8,128)} %all-reduce.6.cloned.1.call-done, f32[2,128,128]{1,2,0:T(8,128)S(1)} %custom-call.19), kind=kOutput, calls=%fused_computation.15 | convolution fusion | flops 805306368 | bytes 4259840 | tf_op jit(solution)/shard_map/jit(_solve_triangular)/triangular_solve | solution.py:28
  194.0 1.9 convolution_subtract_fusion.1
  195.9 1.9 fusion.20
  197.9 1.9 fusion.27
  199.8 2.5 %maximum_bitcast_fusion = f32[4096,256]{0,1:T(8,128)} fusion(f32[128,4096]{1,0:T(8,128)S(1)} %fusion.20, f32[128,4096]{1,0:T(8,128)S(1)} %fusion.7), kind=kLoop, calls=%fused_computation.14 | loop fusion | flops 1048576 | bytes 8388608 | tf_op jit(solution)/shard_map/transpose | solution.py:28
  202.3 2.0 convolution_subtract_fusion
  204.3 1.9 convolution_convert_fusion
  206.2 5.9 %copy.17 = f32[4096,256]{1,0:T(8,128)} copy(f32[4096,256]{0,1:T(8,128)} %maximum_bitcast_fusion) | data formatting | bytes 8388608
  212.0 19.1 %subtract_convert_fusion = bf16[2816,4096]{1,0:T(8,128)(2,1)} fusion(bf16[2816,4096]{1,0:T(8,128)(2,1)} %bitcast_select_fusion, bf16[2816,256]{1,0:T(8,128)(2,1)S(1)} %bitcast_select_fusion.1, bf16[128,4096]{1,0:T(8,128)(2,1)S(1)} %get-tuple-element.35, bf16[128,4096]{1,0:T(8,128)(2,1)S(1)} %convolution_convert_fusion), kind=kOutput, calls=%fused_computation.4 | convolution fusion | flops 5944377344 | bytes 49676288 | tf_op jit(solution)/shard_map/dot_general | solution.py:32
  (36 shorter events, 8.2 us)
Async XLA Ops:
  7.2 40.5 %all-gather.2.cloned.1.call-start = ((), (), s32[]{:S(2)}) async-start(), calls=%async_computation | async-start | bytes 1966080 | tf_op jit(solution)/shard_map/all_gather | solution.py:15
  7.9 97.6 %all-reduce.4.cloned.1.call-start = ((), (), s32[]{:S(2)}) async-start(), calls=%async_computation.1 | async-start | bytes 262144 | tf_op jit(solution)/shard_map/psum | solution.py:21
  51.5 138.8 %all-reduce.6.cloned.1.call-start = ((), (), s32[]{:S(2)}) async-start(), calls=%async_computation.2 | async-start | bytes 8388608 | tf_op jit(solution)/shard_map/psum | solution.py:27
  168.1 29.8 %copy-start.1 = (f32[2,128,128]{1,2,0:T(8,128)}, f32[2,128,128]{1,2,0:T(8,128)S(1)}, u32[]{:S(2)}) copy-start(f32[2,128,128]{1,2,0:T(8,128)S(1)} %custom-call.19) | copy-start | bytes 393220
  190.3 3.7 %copy-start = (f32[256,4096]{1,0:T(8,128)S(1)}, f32[256,4096]{1,0:T(8,128)}, u32[]{:S(2)}) copy-start(f32[256,4096]{1,0:T(8,128)} %all-reduce.6.cloned.1.call-done) | copy-start | bytes 12582916
  202.3 2.0 copy-start.2
Sparse Core Ops, SparseCore 0:
  9.5 36.7 all-gather.1
  51.6 53.7 all-reduce.3
  109.3 80.9 all-reduce.5
where the time goes:
time: 240 us; the launch traced here: 238 us
  other arithmetic  80.9 us (34%)
  waiting for transfers between devices  63 us (26%)
  matrix products  46.5 us (19%)
  local copies, waits for them, and re-layouts  31.9 us (13%)
  between operations  15.2 us (6%)
    psum x1, waiting for transfers between devices, local(): lax.psum(local_gram.astype(jnp.bfloat16), 'row').astype(jnp.float32)  40 us
    another operation x6, other arithmetic, local(): lower_factor = jnp.linalg.cholesky(gram_matrix)  34 us
    select_n x3, other arithmetic, pick_tiles(): return jnp.take(tiled, tile_list, axis=0).reshape(-1, whole.shape[1])  22.9 us
    psum x1, waiting for transfers between devices, local(): cross_sum = lax.psum(local_cross, 'row')  22.2 us
    another operation x3, other arithmetic, local(): jax.scipy.linalg.solve_triangular(lower_factor, cross_sum.T, lower=True)  19.9 us
    dot_general x1, matrix products, local(): lax.dot_general(act_panel, coeff, (((1,), (1,)), ((), ())), preferred_ele...  19.1 us
    gather x2, local copies, waits for them, and re-layouts, pick_tiles(): return jnp.take(tiled, tile_list, axis=0).reshape(-1, whole.shape[1])  18.4 us
    dot_general x1, matrix products, local(): lax.dot_general(act_trail, act_panel, (((0,), (0,)), ((), ())), preferred...  12.2 us
  transfers between devices with their start and end apart: 3, of which 2 were waited for; matrix products, arithmetic and copies ran while one was open for 48% of the time, Pallas kernels for 0%

commit v1 on v0

v1 whole, which is shorter than its diff:
```python
import functools
import jax
import jax.numpy as jnp
from jax import lax
from jax.sharding import PartitionSpec as P
from jax.experimental import pallas as pl
from jax.experimental.pallas import tpu as pltpu

TILE = 128
F32 = jnp.float32
BF16 = jnp.bfloat16
VMEM = pl.BlockSpec(memory_space=pltpu.VMEM)
SMEM = pl.BlockSpec(memory_space=pltpu.SMEM)
ANY = pl.BlockSpec(memory_space=pl.ANY)
MIB = 1 << 20


def shape(dims, kind):
    return jax.ShapeDtypeStruct(dims, kind)


def call(body, name, out_shape, in_specs, out_specs, grant, flops=0, moved=0, scratch=()):
    return pl.pallas_call(
        body,
        name=name,
        out_shape=out_shape,
        in_specs=in_specs,
        out_specs=out_specs,
        scratch_shapes=list(scratch),
        cost_estimate=pl.CostEstimate(flops=flops, bytes_accessed=moved, transcendentals=0),
        compiler_params=pltpu.CompilerParams(vmem_limit_bytes=grant * MIB),
    )


def dot(a, b, contract):
    return lax.dot_general(a, b, (contract, ((), ())), preferred_element_type=F32)


def exact(a, b, contract):
    return lax.dot_general(
        a, b, (contract, ((), ())), precision=lax.Precision.HIGHEST, preferred_element_type=F32
    )


def split(value):
    high = value.astype(BF16)
    return high, (value - high.astype(F32)).astype(BF16)


def pick_kernel(tiles, panel, out):
    for k in range(tiles.shape[0]):
        start = pl.multiple_of(tiles[k] * TILE, TILE)
        block = panel[pl.ds(start, TILE), :].astype(F32)
        out[:, k * TILE : (k + 1) * TILE] = block.T.astype(BF16)


def pick(tile_list, panel):
    rows = tile_list.shape[0] * TILE
    return call(
        pick_kernel, "pick", shape((panel.shape[1], rows), BF16), [SMEM, VMEM], VMEM, 8,
        moved=4 * rows * panel.shape[1],
    )(tile_list, panel)


def gram_kernel(parts, place, *refs):
    blocks, (full, keep, send) = refs[: 2 * parts - 1], refs[2 * parts - 1 :]
    z, core = place[0], place[1]
    wide = blocks[0].shape[0]
    full[pl.ds(pl.multiple_of(z * wide, wide), wide), :] = blocks[0][...]
    for d in range(1, parts):
        @pl.when(z >= d)
        def _(d=d):
            full[pl.ds(pl.multiple_of((z - d) * wide, wide), wide), :] = blocks[2 * d - 1][...]

        @pl.when(z + d < parts)
        def _(d=d):
            full[pl.ds(pl.multiple_of((z + d) * wide, wide), wide), :] = blocks[2 * d][...]

    half = keep.shape[0]
    everything = full[...]
    mine = full[pl.ds(pl.multiple_of(core * half, half), half), :]
    theirs = full[pl.ds(pl.multiple_of((1 - core) * half, half), half), :]
    send[...] = dot(theirs, everything, ((1,), (1,)))
    keep[...] = dot(mine, everything, ((1,), (1,)))


def gram(place, blocks, parts):
    wide, rows = blocks[0].shape
    width = parts * wide
    half = shape((width // 2, width), F32)
    return call(
        functools.partial(gram_kernel, parts), "gram", (shape((width, rows), BF16), half, half),
        [SMEM] + [VMEM] * len(blocks), (VMEM, VMEM, VMEM), 16,
        flops=2 * width * width * rows, moved=4 * width * rows,
    )(place, *blocks)


def turn_kernel(full, out):
    step = 2 * TILE
    for k in range(full.shape[1] // step):
        out[k * step : (k + 1) * step, :] = full[:, k * step : (k + 1) * step].astype(F32).T.astype(BF16)


def turn(full):
    width, rows = full.shape
    return call(turn_kernel, "turn", shape((rows, width), BF16), [VMEM], VMEM, 16, moved=4 * width * rows)(full)


def fetch(tiles, source, buffer, sems, column, slot):
    wide = buffer.shape[2]
    for k in range(tiles.shape[0]):
        start = pl.multiple_of(tiles[k] * TILE, TILE)
        pltpu.make_async_copy(
            source.at[pl.ds(start, TILE), pl.ds(column, wide)],
            buffer.at[slot, pl.ds(k * TILE, TILE), :],
            sems.at[slot],
        ).start()


def arrive(source, buffer, sems, slot):
    rows, wide = buffer.shape[1:]
    pltpu.make_async_copy(source.at[pl.ds(0, rows), pl.ds(0, wide)], buffer.at[slot], sems.at[slot]).wait()


def cross_kernel(prepare, steps, tiles, place, *refs):
    *sources, trailing, keep, send, lhs, buffer, sems = refs
    core = place[1]
    half = keep.shape[1]
    wide = buffer.shape[2]

    def column(i):
        side = jnp.where(i < steps // 2, 1 - core, core)
        return pl.multiple_of(side * half + lax.rem(i, steps // 2) * wide, wide)

    fetch(tiles, trailing, buffer, sems, column(0), 0)
    prepare(place, sources, lhs)

    def body(i, _):
        slot = lax.rem(i, 2)

        @pl.when(i + 1 < steps)
        def _():
            fetch(tiles, trailing, buffer, sems, column(i + 1), 1 - slot)

        arrive(trailing, buffer, sems, slot)
        value = dot(lhs[...], buffer[slot], ((1,), (0,)))
        where = pl.ds(pl.multiple_of(lax.rem(i, steps // 2) * wide, wide), wide)

        @pl.when(i < steps // 2)
        def _():
            send[:, where] = value.astype(BF16)

        @pl.when(i >= steps // 2)
        def _():
            keep[:, where] = value

        return 0

    lax.fori_loop(0, steps, body, 0)


def cross(name, prepare, deep, tile_list, place, sources, trailing):
    rows = tile_list.shape[0] * TILE
    columns = trailing.shape[1]
    steps = 8
    wide = columns // steps
    return call(
        functools.partial(cross_kernel, prepare, steps), name,
        (shape((deep, columns // 2), F32), shape((deep, columns // 2), BF16)),
        [SMEM, SMEM] + [VMEM] * len(sources) + [ANY], (VMEM, VMEM), 24,
        flops=2 * deep * rows * columns, moved=2 * rows * columns,
        scratch=(
            pltpu.VMEM((deep, rows), BF16),
            pltpu.VMEM((2, rows, wide), BF16),
            pltpu.SemaphoreType.DMA((2,)),
        ),
    )(tile_list, place, *sources, trailing)


def pair_lhs(place, sources, lhs):
    own, below, above = sources
    wide = own.shape[0]

    @pl.when(lax.rem(place[0], 2) == 0)
    def _():
        lhs[:wide, :] = own[...]
        lhs[wide:, :] = above[...]

    @pl.when(lax.rem(place[0], 2) == 1)
    def _():
        lhs[:wide, :] = below[...]
        lhs[wide:, :] = own[...]


def other_lhs(place, sources, lhs):
    (full,) = sources
    pair = lax.div(place[0], 2)
    wide = full.shape[0] - lhs.shape[0]
    for k in range(lhs.shape[0] // wide):
        q = k + (k >= pair).astype(jnp.int32)
        lhs[k * wide : (k + 1) * wide, :] = full[pl.ds(pl.multiple_of(q * wide, wide), wide), :]


def share_kernel(place, keep, got, own, *outs):
    chip = place[2]
    wide = own.shape[1]

    def total(where):
        return keep[:, where] + got[:, where].astype(F32)

    own[...] = total(pl.ds(pl.multiple_of(chip * wide, wide), wide))
    for s, out in enumerate(outs, 1):
        out[...] = total(pl.ds(pl.multiple_of((chip ^ s) * wide, wide), wide)).astype(BF16)


def share(place, keep, got, chips):
    deep, columns = keep.shape
    wide = columns // chips
    return call(
        share_kernel, "share", [shape((deep, wide), F32)] + [shape((deep, wide), BF16)] * (chips - 1),
        [SMEM, VMEM, VMEM], [VMEM] * chips, 8, moved=8 * deep * columns,
    )(place, keep, got)


def swap(value, bit, rows):
    return lax.ppermute(value, "row", [(i, i ^ bit) for i in range(rows)])


def tree(values):
    values = [v.astype(F32) for v in values]
    while len(values) > 1:
        values = [a + b for a, b in zip(values[::2], values[1::2])]
    return values[0]


def reduce_cross(place, keep, send, rows):
    chips = rows // 2
    got = swap(send, 1, rows)
    own, *outs = share(place, keep, got, chips)
    parts = [own] + [swap(v, 2 * s, rows) for s, v in enumerate(outs, 1)]
    mine = tree(parts).astype(BF16)
    stack = jnp.stack([mine] + [swap(mine, 2 * s, rows) for s in range(1, chips)])
    return stack, swap(stack, 1, rows)


def reduce_gram(keep, send, rows):
    own = keep + swap(send, 1, rows)
    total = tree([own] + [swap(own, 2 * s, rows) for s in range(1, rows // 2)])
    return total, swap(total, 1, rows)


def eliminate(tiles, size):
    sub = lax.broadcasted_iota(jnp.int32, (8, 1), 0)
    done = []
    for t in range(size // 8):
        for r in range(8):
            j = t * 8 + r
            row = tiles[t][r : r + 1, :]
            scale = lax.rsqrt(row[:, j : j + 1])
            pivot = row * scale
            done.append(pivot)
            for q in range(t, size // 8):
                lead = tiles[q][:, j : j + 1] * scale
                if q == t:
                    lead = jnp.where(sub > r, lead, 0.0)
                tiles[q] = tiles[q] - lead * pivot
    return jnp.concatenate(done, 0)


def factor_kernel(place, mine, theirs, triangle, inverse, turned, whole):
    core = place[1]
    h = mine.shape[0]
    whole[pl.ds(pl.multiple_of(core * h, h), h), :] = mine[...]
    whole[pl.ds(pl.multiple_of((1 - core) * h, h), h), :] = theirs[...]
    line = lax.broadcasted_iota(jnp.int32, (h, h), 0)
    lane = lax.broadcasted_iota(jnp.int32, (h, h), 1)
    eye = (line == lane).astype(F32)
    zero = jnp.zeros((h, h), F32)
    first = jnp.concatenate([whole[:h, :], eye], 1)
    first = eliminate([first[8 * t : 8 * t + 8] for t in range(h // 8)], h)
    r11, r12, i11 = first[:, :h], first[:, h : 2 * h], first[:, 2 * h :]
    second = jnp.concatenate([whole[h:, h:] - exact(r12, r12, ((0,), (0,))), eye], 1)
    second = eliminate([second[8 * t : 8 * t + 8] for t in range(h // 8)], h)
    r22, i22 = second[:, :h], second[:, h:]
    i11 = jnp.where(lane <= line, i11, 0.0)
    i22 = jnp.where(lane <= line, i22, 0.0)
    i21 = -exact(i22, exact(r12, i11, ((0,), (0,))), ((1,), (0,)))
    triangle[:h, :h] = jnp.where(lane >= line, r11, 0.0)
    triangle[:h, h:] = r12
    triangle[h:, :h] = zero
    triangle[h:, h:] = jnp.where(lane >= line, r22, 0.0)
    full = jnp.concatenate([jnp.concatenate([i11, zero], 1), jnp.concatenate([i21, i22], 1)], 0)
    inverse[0], inverse[1] = split(full)
    turned[0], turned[1] = split(full.T)


def factor(place, mine, theirs):
    size = mine.shape[1]
    both = shape((2, size, size), BF16)
    return call(
        factor_kernel, "factor", (shape((size, size), F32), both, both), [SMEM, VMEM, VMEM], (VMEM,) * 3, 16,
        flops=10 * size**3, moved=30 * MIB, scratch=(pltpu.VMEM((size, size), F32),),
    )(place, mine, theirs)


def update_kernel(
    chips, tiles, place, inverse, turned, panel, near_one, far_one, near_two, far_two, trailing,
    top_out, out, cross_buf, tops, buffer, results, in_sems, top_sems, out_sems,
):
    z, core, chip = place[0], place[1], place[2]
    pair = lax.div(z, 2)
    wide = buffer.shape[2]
    steps = 2 * chips
    two = near_one.shape[1]
    rest = near_two.shape[1] // two
    rows = buffer.shape[1]
    block = 2 * TILE

    def column(i):
        side = jnp.where(i < chips, core, 1 - core)
        return pl.multiple_of((side * chips + (chip ^ lax.rem(i, chips))) * wide, wide)

    fetch(tiles, trailing, buffer, in_sems, column(0), 0)

    def top_copy(slot, where):
        return pltpu.make_async_copy(tops.at[slot], top_out.at[pl.ds(where, wide), :], top_sems.at[slot])

    def out_copy(slot, where):
        return pltpu.make_async_copy(results.at[slot], out.at[:, pl.ds(where, wide)], out_sems.at[slot])

    def body(i, _):
        slot = lax.rem(i, 2)
        where = column(i)
        s = lax.rem(i, chips)

        @pl.when(i + 1 < steps)
        def _():
            fetch(tiles, trailing, buffer, in_sems, column(i + 1), 1 - slot)

        def place_cross(one, several):
            cross_buf[pl.ds(pl.multiple_of(pair * two, two), two), :] = one[s]
            for k in range(rest):
                q = k + (k >= pair).astype(jnp.int32)
                cross_buf[pl.ds(pl.multiple_of(q * two, two), two), :] = several[s, k * two : (k + 1) * two, :]

        @pl.when(i < chips)
        def _():
            place_cross(near_one, near_two)

        @pl.when(i >= chips)
        def _():
            place_cross(far_one, far_two)

        sums = cross_buf[...]
        turn_ = ((1,), (0,))
        top = dot(inverse[0], sums, turn_) + dot(inverse[1], sums, turn_)
        high, low = split(top)
        coeff = (dot(turned[0], high, turn_) + (dot(turned[0], low, turn_) + dot(turned[1], high, turn_))).astype(BF16)

        @pl.when(i >= 2)
        def _():
            top_copy(slot, 0).wait()
            out_copy(slot, 0).wait()

        tops[slot] = top.T
        top_copy(slot, where).start()
        arrive(trailing, buffer, in_sems, slot)

        def rows_body(k, _):
            part = pl.ds(pl.multiple_of(k * block, block), block)
            product = dot(panel[part, :], coeff, turn_)
            results[slot, part, :] = (buffer[slot, part, :].astype(F32) - product).astype(BF16)
            return 0

        lax.fori_loop(0, rows // block, rows_body, 0, unroll=True)
        out_copy(slot, where).start()
        return 0

    lax.fori_loop(0, steps, body, 0)
    for slot in range(2):
        top_copy(slot, 0).wait()
        out_copy(slot, 0).wait()


def update(tile_list, place, inverse, turned, panel, one, two, trailing, chips):
    rows, size = panel.shape
    columns = trailing.shape[1]
    wide = columns // (2 * chips)
    return call(
        functools.partial(update_kernel, chips), "update",
        (shape((columns, size), F32), shape((rows, columns), BF16)),
        [SMEM, SMEM] + [VMEM] * 7 + [ANY], (ANY, ANY), 40,
        flops=2 * rows * size * columns, moved=4 * rows * columns,
        scratch=(
            pltpu.VMEM((size, wide), BF16),
            pltpu.VMEM((2, wide, size), F32),
            pltpu.VMEM((2, rows, wide), BF16),
            pltpu.VMEM((2, rows, wide), BF16),
            pltpu.SemaphoreType.DMA((2,)),
            pltpu.SemaphoreType.DMA((2,)),
            pltpu.SemaphoreType.DMA((2,)),
        ),
    )(tile_list, place, inverse, turned, panel, *one, *two, trailing)


def local(nrow, ncol, panel, trailing, tile_list):
    row = lax.axis_index("row")
    place = jnp.stack([lax.axis_index("col"), row % 2, row // 2]).astype(jnp.int32)
    own = pick(tile_list, panel)
    below, above = [own], [own]
    for s in range(1, ncol):
        below.append(lax.ppermute(below[-1], "col", [(i, i + 1) for i in range(s - 1, ncol - 1)]))
        above.append(lax.ppermute(above[-1], "col", [(i + 1, i) for i in range(ncol - s)]))
    wide = panel.shape[1]
    one = cross("cross_pair", pair_lhs, 2 * wide, tile_list, place, [own, below[1], above[1]], trailing)
    one = reduce_cross(place, *one, nrow)
    blocks = [own]
    for s in range(1, ncol):
        blocks += [below[s], above[s]]
    full, keep, send = gram(place, blocks, ncol)
    sums = reduce_gram(keep, send, nrow)
    two = cross("cross_rest", other_lhs, (ncol - 2) * wide, tile_list, place, [full], trailing)
    two = reduce_cross(place, *two, nrow)
    triangle, inverse, turned = factor(place, *sums)
    top_rows, updated = update(
        tile_list, place, inverse, turned, turn(full), one, two, trailing, nrow // 2
    )
    return triangle, top_rows, updated


def solution(mesh):
    return jax.shard_map(
        functools.partial(local, mesh.shape["row"], mesh.shape["col"]),
        mesh=mesh,
        in_specs=(P("row", "col"), P("row", "col"), P("row")),
        out_specs=(P(), P("col", None), P("row", "col")),
        check_vma=False,
    )
```

time: 240 us -> 155 us (0.65)
  other arithmetic: 80.9 us -> 0.41 us
  Pallas kernels: 0 us -> 67 us
  matrix products: 46.5 us -> 0 us
  starting transfers between devices: 0.12 us -> 40.5 us
  waiting for transfers between devices: 63 us -> 26.7 us
  between operations: 15.2 us -> 1.02 us
  local copies, waits for them, and re-layouts: 31.9 us -> 19 us
    pallas_call x0 -> x9, Pallas kernels: none -> 67 us  [the longest x1 23.1 us: factor(): call(factor_kernel, 'factor', (shape((size, size), F32), both, both), [SM...]
    psum x2 -> x0, waiting for transfers between devices: 62.3 us -> none  [the longest x1 40 us: local(): lax.psum(local_gram.astype(jnp.bfloat16), 'row').astype(jnp.float32)]
    another operation x9 -> x3, other arithmetic: 53.9 us -> 0.21 us  [the longest x2 0.14 us: reduce_cross(): jnp.stack([mine] + [swap(mine, 2 * s, rows) for s in range(1, chips)])]
    ppermute x0 -> x27, starting transfers between devices: none -> 40.5 us  [the longest x21 26.6 us: swap(): return lax.ppermute(value, 'row', [(i, i ^ bit) for i in range(rows)])]
    dot_general x3 -> x0, matrix products: 32.7 us -> none  [the longest x1 19.1 us: local(): lax.dot_general(act_panel, coeff, (((1,), (1,)), ((), ())), preferred_ele...]
    ppermute x0 -> x27, waiting for transfers between devices: none -> 26.7 us  [the longest x21 14.4 us: swap(): return lax.ppermute(value, 'row', [(i, i ^ bit) for i in range(rows)])]
    select_n x3 -> x0, other arithmetic: 22.9 us -> none  [pick_tiles(): return jnp.take(tiled, tile_list, axis=0).reshape(-1, whole.shape[1])]
    gather x2 -> x0, local copies, waits for them, and re-layouts: 18.4 us -> none  [pick_tiles(): return jnp.take(tiled, tile_list, axis=0).reshape(-1, whole.shape[1])]
  transfers between devices with their start and end apart: 3 -> 27, of which waited for: 2 -> 11; matrix products, arithmetic and copies ran while one was open for 48% -> 0% of each run, Pallas kernels for 0% -> 30%
where the time goes in v1:
time: 155 us
  Pallas kernels  67 us (43%)
  starting transfers between devices  40.5 us (26%)
  waiting for transfers between devices  26.7 us (17%)
  local copies, waits for them, and re-layouts  19 us (12%)
    ppermute x21, starting transfers between devices, swap(): return lax.ppermute(value, 'row', [(i, i ^ bit) for i in range(rows)])  26.6 us
    pallas_call x1, Pallas kernels, factor(): call(factor_kernel, 'factor', (shape((size, size), F32), both, both), [SM...  23.1 us
    pallas_call x1, Pallas kernels, update(): call(functools.partial(update_kernel, chips), 'update', (shape((columns,...  20.5 us
    pallas_call x2, Pallas kernels, cross(): call(functools.partial(cross_kernel, prepare, steps), name, (shape((deep,...  19.2 us
    unnamed x11, local copies, waits for them, and re-layouts  19 us
    ppermute x21, waiting for transfers between devices, swap(): return lax.ppermute(value, 'row', [(i, i ^ bit) for i in range(rows)])  14.4 us
    ppermute x3, waiting for transfers between devices, local(): lax.ppermute(above[-1], 'col', [(i + 1, i) for i in range(ncol - s)])  9.13 us
    ppermute x3, starting transfers between devices, local(): lax.ppermute(below[-1], 'col', [(i, i + 1) for i in range(s - 1, ncol - 1)])  9.06 us
  transfers between devices with their start and end apart: 27, of which 11 were waited for; matrix products, arithmetic and copies ran while one was open for 0% of the time, Pallas kernels for 30%

profile of v1, /device:TPU:17, one launch (start us, length us, event | category | flops | bytes accessed | tf_op | source)
XLA Modules:
  0.0 154.6 jit_solution(10242919013728854981)
XLA Ops:
  3.5 2.1 %collective-permute-start.1 = (bf16[64,2816]{1,0:T(8,128)(2,1)S(1)}, bf16[64,2816]{1,0:T(8,128)(2,1)S(1)}, u32[]{:S(2)}, u32[]{:S(2)}) collective-permute-start(bf16[64,2816]{1,0:T(8,128)(2,1)S(1)} %pick.1.refs_0_), channel_id=1, source_target_pairs={{1,0},{2,1},{3,2},{5,4},{6,5},{7,6},{9,8},{10,9},{11,10},{13,12},{... | collective-permute-start | bytes 1081352 | tf_op jit(solution)/shard_map/ppermute | solution.py:413
  5.6 3.2 %collective-permute-start = (bf16[64,2816]{1,0:T(8,128)(2,1)S(1)}, bf16[64,2816]{1,0:T(8,128)(2,1)S(1)}, u32[]{:S(2)}, u32[]{:S(2)}) collective-permute-start(bf16[64,2816]{1,0:T(8,128)(2,1)S(1)} %pick.1.refs_0_), channel_id=1, source_target_pairs={{0,1},{1,2},{2,3},{4,5},{5,6},{6,7},{8,9},{9,10},{10,11},{12,13},{... | collective-permute-start | bytes 1081352 | tf_op jit(solution)/shard_map/ppermute | solution.py:412
  8.8 5.9 %collective-permute-done.1.refs_2_ = bf16[64,2816]{1,0:T(8,128)(2,1)S(1)} collective-permute-done((bf16[64,2816]{1,0:T(8,128)(2,1)S(1)}, bf16[64,2816]{1,0:T(8,128)(2,1)S(1)}, u32[]{:S(2)}, u32[]{:S(2)}) %collective-permute-start.1) | collective-permute-done | bytes 360480 | tf_op jit(solution)/shard_map/ppermute | solution.py:413
  14.7 2.1 %collective-permute-start.3 = (bf16[64,2816]{1,0:T(8,128)(2,1)S(1)}, bf16[64,2816]{1,0:T(8,128)(2,1)S(1)}, u32[]{:S(2)}, u32[]{:S(2)}) collective-permute-start(bf16[64,2816]{1,0:T(8,128)(2,1)S(1)} %collective-permute-done.1.refs_2_), channel_id=1, source_target_pairs={{1,0},{2,1},{5,4},{6,5},{9,8},{10,9},{13,12},{14,13},{17,16},{18,1... | collective-permute-start | bytes 1081352 | tf_op jit(solution)/shard_map/ppermute | solution.py:413
  16.8 2.9 %collective-permute-start.2 = (bf16[64,2816]{1,0:T(8,128)(2,1)S(1)}, bf16[64,2816]{1,0:T(8,128)(2,1)S(1)}, u32[]{:S(2)}, u32[]{:S(2)}) collective-permute-start(bf16[64,2816]{1,0:T(8,128)(2,1)S(1)} %collective-permute-done.refs_1_), channel_id=1, source_target_pairs={{1,2},{2,3},{5,6},{6,7},{9,10},{10,11},{13,14},{14,15},{17,18},{18... | collective-permute-start | bytes 1081352 | tf_op jit(solution)/shard_map/ppermute | solution.py:412
  19.7 3.2 %collective-permute-done.3.refs_4_ = bf16[64,2816]{1,0:T(8,128)(2,1)S(1)} collective-permute-done((bf16[64,2816]{1,0:T(8,128)(2,1)S(1)}, bf16[64,2816]{1,0:T(8,128)(2,1)S(1)}, u32[]{:S(2)}, u32[]{:S(2)}) %collective-permute-start.3) | collective-permute-done | bytes 360480 | tf_op jit(solution)/shard_map/ppermute | solution.py:413
  23.6 3.2 %collective-permute-done.2.refs_3_ = bf16[64,2816]{1,0:T(8,128)(2,1)S(1)} collective-permute-done((bf16[64,2816]{1,0:T(8,128)(2,1)S(1)}, bf16[64,2816]{1,0:T(8,128)(2,1)S(1)}, u32[]{:S(2)}, u32[]{:S(2)}) %collective-permute-start.2) | collective-permute-done | bytes 360480 | tf_op jit(solution)/shard_map/ppermute | solution.py:412
  26.8 2.9 %collective-permute-start.4 = (bf16[64,2816]{1,0:T(8,128)(2,1)S(1)}, bf16[64,2816]{1,0:T(8,128)(2,1)S(1)}, u32[]{:S(2)}, u32[]{:S(2)}) collective-permute-start(bf16[64,2816]{1,0:T(8,128)(2,1)S(1)} %collective-permute-done.2.refs_3_), channel_id=1, source_target_pairs={{2,3},{6,7},{10,11},{14,15},{18,19},{22,23},{26,27},{30,31}} | collective-permute-start | bytes 1081352 | tf_op jit(solution)/shard_map/ppermute | solution.py:412
  29.8 8.2 %copy-done = bf16[3072,4096]{1,0:T(8,128)(2,1)S(1)} copy-done((bf16[3072,4096]{1,0:T(8,128)(2,1)S(1)}, bf16[3072,4096]{1,0:T(8,128)(2,1)}, u32[]{:S(2)}) %copy-start) | copy-done | bytes 25165848
  38.6 9.5 %cross_pair.1 = (f32[128,2048]{1,0:T(8,128)S(1)}, bf16[128,2048]{1,0:T(8,128)(2,1)S(1)}) custom-call(s32[22]{0:T(128)S(1)} %copy-done.3, s32[3]{0:T(128)S(1)} %pad_add_fusion.place, bf16[64,2816]{1,0:T(8,128)(2,1)S(1)} %pick.1.refs_0_, bf16[64,2816]{1,0:T(8,128)(2,1)S(1)} %collective-permute-done.refs_1_, ...), custom_call_target="tpu_custom_call" | custom-call | flops 2952790016 | bytes 23068672 | tf_op jit(solution)/shard_map/cross_pair/pallas_call | solution.py:167
  48.2 3.0 %collective-permute-start.11 = (bf16[128,2048]{1,0:T(8,128)(2,1)S(1)}, bf16[128,2048]{1,0:T(8,128)(2,1)S(1)}, u32[]{:S(2)}, u32[]{:S(2)}) collective-permute-start(bf16[128,2048]{1,0:T(8,128)(2,1)S(1)} %get-tuple-element.30), channel_id=1, source_target_pairs={{0,4},{4,0},{8,12},{12,8},{16,20},{20,16},{24,28},{28,24},{1,5},{5... | collective-permute-start | bytes 1572872 | tf_op jit(solution)/shard_map/ppermute | solution.py:226
  51.2 1.7 %gram.1 = (bf16[256,2816]{1,0:T(8,128)(2,1)S(1)}, f32[128,256]{1,0:T(8,128)S(1)}, f32[128,256]{1,0:T(8,128)S(1)}) custom-call(s32[3]{0:T(128)S(1)} %pad_add_fusion.place, bf16[64,2816]{1,0:T(8,128)(2,1)S(1)} %pick.1.refs_0_, bf16[64,2816]{1,0:T(8,128)(2,1)S(1)} %collective-permute-done.refs_1_, bf16[64,2816]{1,0:T(8,128)(2,1)S(1)} %collective-permute-done.1.refs_2_, ...), custom_call_target="tpu_custom_call" | custom-call | flops 369098752 | bytes 2883584 | tf_op jit(solution)/shard_map/gram/pallas_call | solution.py:91
  52.9 8.1 %copy-done.1 = bf16[3072,4096]{1,0:T(8,128)(2,1)S(1)} copy-done((bf16[3072,4096]{1,0:T(8,128)(2,1)S(1)}, bf16[3072,4096]{1,0:T(8,128)(2,1)}, u32[]{:S(2)}) %copy-start.1) | copy-done | bytes 25165848
  61.1 9.7 %cross_rest.1 = (f32[128,2048]{1,0:T(8,128)S(1)}, bf16[128,2048]{1,0:T(8,128)(2,1)S(1)}) custom-call(s32[22]{0:T(128)S(1)} %copy-done.4, s32[3]{0:T(128)S(1)} %pad_add_fusion.place, bf16[256,2816]{1,0:T(8,128)(2,1)S(1)} %get-tuple-element.28.full.refs_0_, bf16[3072,4096]{1,0:T(8,128)(2,1)S(1)} %copy-done.1), custom_call_target="tpu_custom_call" | custom-call | flops 2952790016 | bytes 23068672 | tf_op jit(solution)/shard_map/cross_rest/pallas_call | solution.py:167
  78.3 1.5 collective-permute-done.14
  83.0 1.5 collective-permute-done.21
  89.6 3.3 %collective-permute-done.16 = bf16[128,512]{1,0:T(8,128)(2,1)S(1)} collective-permute-done((bf16[128,512]{1,0:T(8,128)(2,1)S(1)}, bf16[128,512]{1,0:T(8,128)(2,1)S(1)}, u32[]{:S(2)}, u32[]{:S(2)}) %collective-permute-start.16) | collective-permute-done | bytes 131104 | tf_op jit(solution)/shard_map/ppermute | solution.py:226
  92.9 2.7 %collective-permute-start.6 = (f32[128,256]{1,0:T(8,128)S(1)}, f32[128,256]{1,0:T(8,128)S(1)}, u32[]{:S(2)}, u32[]{:S(2)}) collective-permute-start(f32[128,256]{1,0:T(8,128)S(1)} %get-tuple-element.24), channel_id=1, source_target_pairs={{0,4},{4,0},{8,12},{12,8},{16,20},{20,16},{24,28},{28,24},{1,5},{5... | collective-permute-start | bytes 393224 | tf_op jit(solution)/shard_map/ppermute | solution.py:226
  95.9 4.3 %collective-permute-start.26 = (bf16[4,128,512]{2,1,0:T(8,128)(2,1)S(1)}, bf16[4,128,512]{2,1,0:T(8,128)(2,1)S(1)}, u32[]{:S(2)}, u32[]{:S(2)}) collective-permute-start(bf16[4,128,512]{2,1,0:T(8,128)(2,1)S(1)} %pad_maximum_fusion.1.near_two), channel_id=1, source_target_pairs={{0,4},{4,0},{8,12},{12,8},{16,20},{20,16},{24,28},{28,24},{1,5},{5... | collective-permute-start | bytes 1572872 | tf_op jit(solution)/shard_map/ppermute | solution.py:226
  100.1 1.8 %collective-permute-start.9 = (f32[128,256]{1,0:T(8,128)S(1)}, f32[128,256]{1,0:T(8,128)S(1)}, u32[]{:S(2)}, u32[]{:S(2)}) collective-permute-start(f32[128,256]{1,0:T(8,128)S(1)} %add.36), channel_id=1, source_target_pairs={{0,24},{4,28},{8,16},{12,20},{16,8},{20,12},{24,0},{28,4},{1,25},{... | collective-permute-start | bytes 393224 | tf_op jit(solution)/shard_map/ppermute | solution.py:226
  102.9 3.3 %collective-permute-done.9 = f32[128,256]{1,0:T(8,128)S(1)} collective-permute-done((f32[128,256]{1,0:T(8,128)S(1)}, f32[128,256]{1,0:T(8,128)S(1)}, u32[]{:S(2)}, u32[]{:S(2)}) %collective-permute-start.9) | collective-permute-done | bytes 131104 | tf_op jit(solution)/shard_map/ppermute | solution.py:226
  106.1 3.2 %collective-permute-done.8 = f32[128,256]{1,0:T(8,128)S(1)} collective-permute-done((f32[128,256]{1,0:T(8,128)S(1)}, f32[128,256]{1,0:T(8,128)S(1)}, u32[]{:S(2)}, u32[]{:S(2)}) %collective-permute-start.8) | collective-permute-done | bytes 131104 | tf_op jit(solution)/shard_map/ppermute | solution.py:226
  110.9 23.1 %factor.1 = (f32[256,256]{1,0:T(8,128)}, bf16[2,256,256]{2,1,0:T(8,128)(2,1)S(1)}, bf16[2,256,256]{2,1,0:T(8,128)(2,1)S(1)}) custom-call(s32[3]{0:T(128)S(1)} %pad_add_fusion.place, f32[128,256]{1,0:T(8,128)S(1)} %add_add_fusion.mine, f32[128,256]{1,0:T(8,128)S(1)} %collective-permute-done.10.theirs), custom_call_target="tpu_custom_call" | custom-call | flops 167772160 | bytes 31457280 | tf_op jit(solution)/shard_map/factor/pallas_call | solution.py:300
  134.0 20.5 %update.1 = (f32[4096,256]{1,0:T(8,128)}, bf16[2816,4096]{1,0:T(8,128)(2,1)}) custom-call(s32[22]{0:T(128)S(1)} %copy-done.4, s32[3]{0:T(128)S(1)} %pad_add_fusion.place, bf16[2,256,256]{2,1,0:T(8,128)(2,1)S(1)} %get-tuple-element.26.inverse, bf16[2,256,256]{2,1,0:T(8,128)(2,1)S(1)} %get-tuple-element.27.turned, bf16[2816,256]{1,0:T(8,128)(2,1)S(1)} %turn.1.panel, ...), custom_call_target="tpu_custom_call" | custom-call | flops 5905580032 | bytes 46137344 | tf_op jit(solution)/shard_map/update/pallas_call | solution.py:389
  (57 shorter events, 22.7 us)
Async XLA Ops:
  3.5 11.2 %collective-permute-start.1 = (bf16[64,2816]{1,0:T(8,128)(2,1)S(1)}, bf16[64,2816]{1,0:T(8,128)(2,1)S(1)}, u32[]{:S(2)}, u32[]{:S(2)}) collective-permute-start(bf16[64,2816]{1,0:T(8,128)(2,1)S(1)} %pick.1.refs_0_), channel_id=1, source_target_pairs={{1,0},{2,1},{3,2},{5,4},{6,5},{7,6},{9,8},{10,9},{11,10},{13,12},{... | collective-permute-start | bytes 1081352 | tf_op jit(solution)/shard_map/ppermute | solution.py:413
  5.6 11.2 %collective-permute-start = (bf16[64,2816]{1,0:T(8,128)(2,1)S(1)}, bf16[64,2816]{1,0:T(8,128)(2,1)S(1)}, u32[]{:S(2)}, u32[]{:S(2)}) collective-permute-start(bf16[64,2816]{1,0:T(8,128)(2,1)S(1)} %pick.1.refs_0_), channel_id=1, source_target_pairs={{0,1},{1,2},{2,3},{4,5},{5,6},{6,7},{8,9},{9,10},{10,11},{12,13},{... | collective-permute-start | bytes 1081352 | tf_op jit(solution)/shard_map/ppermute | solution.py:412
  14.7 8.3 %collective-permute-start.3 = (bf16[64,2816]{1,0:T(8,128)(2,1)S(1)}, bf16[64,2816]{1,0:T(8,128)(2,1)S(1)}, u32[]{:S(2)}, u32[]{:S(2)}) collective-permute-start(bf16[64,2816]{1,0:T(8,128)(2,1)S(1)} %collective-permute-done.1.refs_2_), channel_id=1, source_target_pairs={{1,0},{2,1},{5,4},{6,5},{9,8},{10,9},{13,12},{14,13},{17,16},{18,1... | collective-permute-start | bytes 1081352 | tf_op jit(solution)/shard_map/ppermute | solution.py:413
  16.8 10.1 %collective-permute-start.2 = (bf16[64,2816]{1,0:T(8,128)(2,1)S(1)}, bf16[64,2816]{1,0:T(8,128)(2,1)S(1)}, u32[]{:S(2)}, u32[]{:S(2)}) collective-permute-start(bf16[64,2816]{1,0:T(8,128)(2,1)S(1)} %collective-permute-done.refs_1_), channel_id=1, source_target_pairs={{1,2},{2,3},{5,6},{6,7},{9,10},{10,11},{13,14},{14,15},{17,18},{18... | collective-permute-start | bytes 1081352 | tf_op jit(solution)/shard_map/ppermute | solution.py:412
  23.0 28.2 %collective-permute-start.5 = (bf16[64,2816]{1,0:T(8,128)(2,1)S(1)}, bf16[64,2816]{1,0:T(8,128)(2,1)S(1)}, u32[]{:S(2)}, u32[]{:S(2)}) collective-permute-start(bf16[64,2816]{1,0:T(8,128)(2,1)S(1)} %collective-permute-done.3.refs_4_), channel_id=1, source_target_pairs={{1,0},{5,4},{9,8},{13,12},{17,16},{21,20},{25,24},{29,28}} | collective-permute-start | bytes 1081352 | tf_op jit(solution)/shard_map/ppermute | solution.py:413
  26.8 24.4 %collective-permute-start.4 = (bf16[64,2816]{1,0:T(8,128)(2,1)S(1)}, bf16[64,2816]{1,0:T(8,128)(2,1)S(1)}, u32[]{:S(2)}, u32[]{:S(2)}) collective-permute-start(bf16[64,2816]{1,0:T(8,128)(2,1)S(1)} %collective-permute-done.2.refs_3_), channel_id=1, source_target_pairs={{2,3},{6,7},{10,11},{14,15},{18,19},{22,23},{26,27},{30,31}} | collective-permute-start | bytes 1081352 | tf_op jit(solution)/shard_map/ppermute | solution.py:412
  48.2 22.7 %collective-permute-start.11 = (bf16[128,2048]{1,0:T(8,128)(2,1)S(1)}, bf16[128,2048]{1,0:T(8,128)(2,1)S(1)}, u32[]{:S(2)}, u32[]{:S(2)}) collective-permute-start(bf16[128,2048]{1,0:T(8,128)(2,1)S(1)} %get-tuple-element.30), channel_id=1, source_target_pairs={{0,4},{4,0},{8,12},{12,8},{16,20},{20,16},{24,28},{28,24},{1,5},{5... | collective-permute-start | bytes 1572872 | tf_op jit(solution)/shard_map/ppermute | solution.py:226
  71.5 5.9 %collective-permute-start.12 = (bf16[128,512]{1,0:T(8,128)(2,1)S(1)}, bf16[128,512]{1,0:T(8,128)(2,1)S(1)}, u32[]{:S(2)}, u32[]{:S(2)}) collective-permute-start(bf16[128,512]{1,0:T(8,128)(2,1)S(1)} %get-tuple-element.32), channel_id=1, source_target_pairs={{0,8},{4,12},{8,0},{12,4},{16,24},{20,28},{24,16},{28,20},{1,9},{5... | collective-permute-start | bytes 393224 | tf_op jit(solution)/shard_map/ppermute | solution.py:226
  74.0 5.8 %collective-permute-start.14 = (bf16[128,512]{1,0:T(8,128)(2,1)S(1)}, bf16[128,512]{1,0:T(8,128)(2,1)S(1)}, u32[]{:S(2)}, u32[]{:S(2)}) collective-permute-start(bf16[128,512]{1,0:T(8,128)(2,1)S(1)} %get-tuple-element.34), channel_id=1, source_target_pairs={{0,24},{4,28},{8,16},{12,20},{16,8},{20,12},{24,0},{28,4},{1,25},{... | collective-permute-start | bytes 393224 | tf_op jit(solution)/shard_map/ppermute | solution.py:226
  74.9 7.6 %collective-permute-start.20 = (bf16[128,512]{1,0:T(8,128)(2,1)S(1)}, bf16[128,512]{1,0:T(8,128)(2,1)S(1)}, u32[]{:S(2)}, u32[]{:S(2)}) collective-permute-start(bf16[128,512]{1,0:T(8,128)(2,1)S(1)} %get-tuple-element.38), channel_id=1, source_target_pairs={{0,8},{4,12},{8,0},{12,4},{16,24},{20,28},{24,16},{28,20},{1,9},{5... | collective-permute-start | bytes 393224 | tf_op jit(solution)/shard_map/ppermute | solution.py:226
  76.2 8.4 %collective-permute-start.21 = (bf16[128,512]{1,0:T(8,128)(2,1)S(1)}, bf16[128,512]{1,0:T(8,128)(2,1)S(1)}, u32[]{:S(2)}, u32[]{:S(2)}) collective-permute-start(bf16[128,512]{1,0:T(8,128)(2,1)S(1)} %get-tuple-element.39), channel_id=1, source_target_pairs={{0,16},{4,20},{8,24},{12,28},{16,0},{20,4},{24,8},{28,12},{1,17},{... | collective-permute-start | bytes 393224 | tf_op jit(solution)/shard_map/ppermute | solution.py:226
  77.4 8.0 %collective-permute-start.22 = (bf16[128,512]{1,0:T(8,128)(2,1)S(1)}, bf16[128,512]{1,0:T(8,128)(2,1)S(1)}, u32[]{:S(2)}, u32[]{:S(2)}) collective-permute-start(bf16[128,512]{1,0:T(8,128)(2,1)S(1)} %get-tuple-element.40), channel_id=1, source_target_pairs={{0,24},{4,28},{8,16},{12,20},{16,8},{20,12},{24,0},{28,4},{1,25},{... | collective-permute-start | bytes 393224 | tf_op jit(solution)/shard_map/ppermute | solution.py:226
  79.9 8.4 %collective-permute-start.17 = (bf16[128,512]{1,0:T(8,128)(2,1)S(1)}, bf16[128,512]{1,0:T(8,128)(2,1)S(1)}, u32[]{:S(2)}, u32[]{:S(2)}) collective-permute-start(bf16[128,512]{1,0:T(8,128)(2,1)S(1)} %add_convert_fusion.1), channel_id=1, source_target_pairs={{0,24},{4,28},{8,16},{12,20},{16,8},{20,12},{24,0},{28,4},{1,25},{... | collective-permute-start | bytes 393224 | tf_op jit(solution)/shard_map/ppermute | solution.py:226
  81.2 11.7 %collective-permute-start.16 = (bf16[128,512]{1,0:T(8,128)(2,1)S(1)}, bf16[128,512]{1,0:T(8,128)(2,1)S(1)}, u32[]{:S(2)}, u32[]{:S(2)}) collective-permute-start(bf16[128,512]{1,0:T(8,128)(2,1)S(1)} %add_convert_fusion.1), channel_id=1, source_target_pairs={{0,16},{4,20},{8,24},{12,28},{16,0},{20,4},{24,8},{28,12},{1,17},{... | collective-permute-start | bytes 393224 | tf_op jit(solution)/shard_map/ppermute | solution.py:226
  82.5 13.1 %collective-permute-start.15 = (bf16[128,512]{1,0:T(8,128)(2,1)S(1)}, bf16[128,512]{1,0:T(8,128)(2,1)S(1)}, u32[]{:S(2)}, u32[]{:S(2)}) collective-permute-start(bf16[128,512]{1,0:T(8,128)(2,1)S(1)} %add_convert_fusion.1), channel_id=1, source_target_pairs={{0,8},{4,12},{8,0},{12,4},{16,24},{20,28},{24,16},{28,20},{1,9},{5... | collective-permute-start | bytes 393224 | tf_op jit(solution)/shard_map/ppermute | solution.py:226
  85.5 10.3 %collective-permute-start.25 = (bf16[128,512]{1,0:T(8,128)(2,1)S(1)}, bf16[128,512]{1,0:T(8,128)(2,1)S(1)}, u32[]{:S(2)}, u32[]{:S(2)}) collective-permute-start(bf16[128,512]{1,0:T(8,128)(2,1)S(1)} %add_convert_fusion), channel_id=1, source_target_pairs={{0,24},{4,28},{8,16},{12,20},{16,8},{20,12},{24,0},{28,4},{1,25},{... | collective-permute-start | bytes 393224 | tf_op jit(solution)/shard_map/ppermute | solution.py:226
  86.8 8.9 %collective-permute-start.24 = (bf16[128,512]{1,0:T(8,128)(2,1)S(1)}, bf16[128,512]{1,0:T(8,128)(2,1)S(1)}, u32[]{:S(2)}, u32[]{:S(2)}) collective-permute-start(bf16[128,512]{1,0:T(8,128)(2,1)S(1)} %add_convert_fusion), channel_id=1, source_target_pairs={{0,16},{4,20},{8,24},{12,28},{16,0},{20,4},{24,8},{28,12},{1,17},{... | collective-permute-start | bytes 393224 | tf_op jit(solution)/shard_map/ppermute | solution.py:226
  88.3 7.5 %collective-permute-start.23 = (bf16[128,512]{1,0:T(8,128)(2,1)S(1)}, bf16[128,512]{1,0:T(8,128)(2,1)S(1)}, u32[]{:S(2)}, u32[]{:S(2)}) collective-permute-start(bf16[128,512]{1,0:T(8,128)(2,1)S(1)} %add_convert_fusion), channel_id=1, source_target_pairs={{0,8},{4,12},{8,0},{12,4},{16,24},{20,28},{24,16},{28,20},{1,9},{5... | collective-permute-start | bytes 393224 | tf_op jit(solution)/shard_map/ppermute | solution.py:226
  92.9 7.2 %collective-permute-start.6 = (f32[128,256]{1,0:T(8,128)S(1)}, f32[128,256]{1,0:T(8,128)S(1)}, u32[]{:S(2)}, u32[]{:S(2)}) collective-permute-start(f32[128,256]{1,0:T(8,128)S(1)} %get-tuple-element.24), channel_id=1, source_target_pairs={{0,4},{4,0},{8,12},{12,8},{16,20},{20,16},{24,28},{28,24},{1,5},{5... | collective-permute-start | bytes 393224 | tf_op jit(solution)/shard_map/ppermute | solution.py:226
  95.7 38.3 %collective-permute-start.18 = (bf16[4,128,512]{2,1,0:T(8,128)(2,1)S(1)}, bf16[4,128,512]{2,1,0:T(8,128)(2,1)S(1)}, u32[]{:S(2)}, u32[]{:S(2)}) collective-permute-start(bf16[4,128,512]{2,1,0:T(8,128)(2,1)S(1)} %pad_maximum_fusion.near_one), channel_id=1, source_target_pairs={{0,4},{4,0},{8,12},{12,8},{16,20},{20,16},{24,28},{28,24},{1,5},{5... | collective-permute-start | bytes 1572872 | tf_op jit(solution)/shard_map/ppermute | solution.py:226
  95.9 38.1 %collective-permute-start.26 = (bf16[4,128,512]{2,1,0:T(8,128)(2,1)S(1)}, bf16[4,128,512]{2,1,0:T(8,128)(2,1)S(1)}, u32[]{:S(2)}, u32[]{:S(2)}) collective-permute-start(bf16[4,128,512]{2,1,0:T(8,128)(2,1)S(1)} %pad_maximum_fusion.1.near_two), channel_id=1, source_target_pairs={{0,4},{4,0},{8,12},{12,8},{16,20},{20,16},{24,28},{28,24},{1,5},{5... | collective-permute-start | bytes 1572872 | tf_op jit(solution)/shard_map/ppermute | solution.py:226
  100.1 6.0 %collective-permute-start.9 = (f32[128,256]{1,0:T(8,128)S(1)}, f32[128,256]{1,0:T(8,128)S(1)}, u32[]{:S(2)}, u32[]{:S(2)}) collective-permute-start(f32[128,256]{1,0:T(8,128)S(1)} %add.36), channel_id=1, source_target_pairs={{0,24},{4,28},{8,16},{12,20},{16,8},{20,12},{24,0},{28,4},{1,25},{... | collective-permute-start | bytes 393224 | tf_op jit(solution)/shard_map/ppermute | solution.py:226
  102.0 7.4 %collective-permute-start.8 = (f32[128,256]{1,0:T(8,128)S(1)}, f32[128,256]{1,0:T(8,128)S(1)}, u32[]{:S(2)}, u32[]{:S(2)}) collective-permute-start(f32[128,256]{1,0:T(8,128)S(1)} %add.36), channel_id=1, source_target_pairs={{0,16},{4,20},{8,24},{12,28},{16,0},{20,4},{24,8},{28,12},{1,17},{... | collective-permute-start | bytes 393224 | tf_op jit(solution)/shard_map/ppermute | solution.py:226
  102.0 7.4 %collective-permute-start.7 = (f32[128,256]{1,0:T(8,128)S(1)}, f32[128,256]{1,0:T(8,128)S(1)}, u32[]{:S(2)}, u32[]{:S(2)}) collective-permute-start(f32[128,256]{1,0:T(8,128)S(1)} %add.36), channel_id=1, source_target_pairs={{0,8},{4,12},{8,0},{12,4},{16,24},{20,28},{24,16},{28,20},{1,9},{5... | collective-permute-start | bytes 393224 | tf_op jit(solution)/shard_map/ppermute | solution.py:226
  (8 other events, 42.4 us)

commit v2 on v1

v2 whole, which is shorter than its diff:
```python
import functools
import jax
import jax.numpy as jnp
from jax import lax
from jax.sharding import PartitionSpec as P
from jax.experimental import pallas as pl
from jax.experimental.pallas import tpu as pltpu

TILE = 128
F32 = jnp.float32
BF16 = jnp.bfloat16
VMEM = pl.BlockSpec(memory_space=pltpu.VMEM)
SMEM = pl.BlockSpec(memory_space=pltpu.SMEM)
ANY = pl.BlockSpec(memory_space=pl.ANY)
MIB = 1 << 20


def shape(dims, kind):
    return jax.ShapeDtypeStruct(dims, kind)


def call(body, out_shape, in_specs, out_specs, grant, flops=0, moved=0, scratch=()):
    return pl.pallas_call(
        body,
        out_shape=out_shape,
        in_specs=in_specs,
        out_specs=out_specs,
        scratch_shapes=list(scratch),
        cost_estimate=pl.CostEstimate(flops=flops, bytes_accessed=moved, transcendentals=0),
        compiler_params=pltpu.CompilerParams(vmem_limit_bytes=grant * MIB),
    )


def dot(a, b, contract):
    return lax.dot_general(a, b, (contract, ((), ())), preferred_element_type=F32)


def exact(a, b, contract):
    return lax.dot_general(
        a, b, (contract, ((), ())), precision=lax.Precision.HIGHEST, preferred_element_type=F32
    )


def split(value):
    high = value.astype(BF16)
    return high, (value - high.astype(F32)).astype(BF16)


def pick_kernel(tiles, panel, out):
    for k in range(tiles.shape[0]):
        start = pl.multiple_of(tiles[k] * TILE, TILE)
        out[:, k * TILE : (k + 1) * TILE] = panel[:, pl.ds(start, TILE)]


def pick(tile_list, panel):
    rows = tile_list.shape[0] * TILE
    return call(
        pick_kernel, shape((panel.shape[0], rows), BF16), [SMEM, VMEM], VMEM, 8,
        moved=4 * rows * panel.shape[0],
    )(tile_list, panel)


def gram_kernel(place, *refs):
    *blocks, full, keep, send = refs
    z, core = place[0], place[1]
    wide = blocks[0].shape[0]
    for s, block in enumerate(blocks):
        full[pl.ds(pl.multiple_of((z ^ s) * wide, wide), wide), :] = block[...]
    half = keep.shape[0]
    everything = full[...]
    mine = full[pl.ds(pl.multiple_of(core * half, half), half), :]
    theirs = full[pl.ds(pl.multiple_of((1 - core) * half, half), half), :]
    send[...] = dot(theirs, everything, ((1,), (1,)))
    keep[...] = dot(mine, everything, ((1,), (1,)))


def gram(place, blocks):
    wide, rows = blocks[0].shape
    width = len(blocks) * wide
    half = shape((width // 2, width), F32)
    return call(
        gram_kernel, (shape((width, rows), BF16), half, half),
        [SMEM] + [VMEM] * len(blocks), (VMEM, VMEM, VMEM), 16,
        flops=2 * width * width * rows, moved=4 * width * rows,
    )(place, *blocks)


def turn_kernel(full, out):
    step = 2 * TILE
    for k in range(full.shape[1] // step):
        out[k * step : (k + 1) * step, :] = full[:, k * step : (k + 1) * step].astype(F32).T.astype(BF16)


def turn(full):
    width, rows = full.shape
    return call(turn_kernel, shape((rows, width), BF16), [VMEM], VMEM, 16, moved=4 * width * rows)(full)


def cross_pair_kernel(steps, tiles, place, own, other, trailing, active, keep, send, lhs, sems):
    core, odd = place[1], lax.rem(place[0], 2)
    half = keep.shape[1]
    wide = active.shape[1] // steps
    deep = own.shape[0]

    def column(i):
        side = jnp.where(i < steps // 2, 1 - core, core)
        return pl.multiple_of(side * half + lax.rem(i, steps // 2) * wide, wide)

    def issue(i, _):
        for k in range(tiles.shape[0]):
            start = pl.multiple_of(tiles[k] * TILE, TILE)
            where = pl.ds(column(i), wide)
            pltpu.make_async_copy(
                trailing.at[pl.ds(start, TILE), where], active.at[pl.ds(k * TILE, TILE), where], sems.at[i]
            ).start()
        return 0

    lax.fori_loop(0, steps, issue, 0)
    lhs[pl.ds(pl.multiple_of(odd * deep, deep), deep), :] = own[...]
    lhs[pl.ds(pl.multiple_of((1 - odd) * deep, deep), deep), :] = other[...]

    def body(i, _):
        source = pl.ds(column(i), wide)
        rows = active.shape[0]
        pltpu.make_async_copy(trailing.at[pl.ds(0, rows), source], active.at[:, source], sems.at[i]).wait()
        value = dot(lhs[...], active[:, source], ((1,), (0,)))
        where = pl.ds(pl.multiple_of(lax.rem(i, steps // 2) * wide, wide), wide)

        @pl.when(i < steps // 2)
        def _():
            send[:, where] = value.astype(BF16)

        @pl.when(i >= steps // 2)
        def _():
            keep[:, where] = value

        return 0

    lax.fori_loop(0, steps, body, 0)


def cross_pair(tile_list, place, own, other, trailing):
    deep, rows = own.shape
    columns = trailing.shape[1]
    steps = 8
    return call(
        functools.partial(cross_pair_kernel, steps),
        (pltpu.VMEM((rows, columns), BF16), shape((2 * deep, columns // 2), F32), shape((2 * deep, columns // 2), BF16)),
        [SMEM, SMEM, VMEM, VMEM, ANY], (VMEM,) * 3, 8,
        flops=4 * deep * rows * columns, moved=2 * rows * columns,
        scratch=(pltpu.VMEM((2 * deep, rows), BF16), pltpu.SemaphoreType.DMA((steps,))),
    )(tile_list, place, own, other, trailing)


def cross_rest_kernel(steps, mine, place, full, active, out, lhs):
    pair = lax.div(place[0], 2)
    side = place[1] if mine else 1 - place[1]
    across = full.shape[0] - lhs.shape[0]
    wide = out.shape[1] // steps
    for k in range(lhs.shape[0] // across):
        q = k + (k >= pair).astype(jnp.int32)
        lhs[k * across : (k + 1) * across, :] = full[pl.ds(pl.multiple_of(q * across, across), across), :]

    def body(i, _):
        source = pl.ds(pl.multiple_of(side * out.shape[1] + i * wide, wide), wide)
        where = pl.ds(pl.multiple_of(i * wide, wide), wide)
        out[:, where] = dot(lhs[...], active[:, source], ((1,), (0,))).astype(out.dtype)
        return 0

    lax.fori_loop(0, steps, body, 0)


def cross_rest(mine, place, full, active, across):
    deep = full.shape[0] - across
    rows, columns = active.shape
    return call(
        functools.partial(cross_rest_kernel, 4, mine),
        shape((deep, columns // 2), F32 if mine else BF16), [SMEM, VMEM, VMEM], VMEM, 8,
        flops=deep * rows * columns, moved=rows * columns,
        scratch=(pltpu.VMEM((deep, rows), BF16),),
    )(place, full, active)


def share_kernel(place, keep, got, own, *outs):
    chip = place[2]
    wide = own.shape[1]

    def total(where):
        return keep[:, where] + got[:, where].astype(F32)

    own[...] = total(pl.ds(pl.multiple_of(chip * wide, wide), wide))
    for s, out in enumerate(outs, 1):
        out[...] = total(pl.ds(pl.multiple_of((chip ^ s) * wide, wide), wide)).astype(BF16)


def share(place, keep, got, chips):
    deep, columns = keep.shape
    wide = columns // chips
    return call(
        share_kernel, [shape((deep, wide), F32)] + [shape((deep, wide), BF16)] * (chips - 1),
        [SMEM, VMEM, VMEM], [VMEM] * chips, 8, moved=8 * deep * columns,
    )(place, keep, got)


def swap(value, bit, rows):
    return lax.ppermute(value, "row", [(i, i ^ bit) for i in range(rows)])


def tree(values):
    values = [v.astype(F32) for v in values]
    while len(values) > 1:
        values = [a + b for a, b in zip(values[::2], values[1::2])]
    return values[0]


def reduce_cross(place, keep, got, rows):
    chips = rows // 2
    own, *outs = share(place, keep, got, chips)
    parts = [own] + [swap(v, 2 * s, rows) for s, v in enumerate(outs, 1)]
    mine = tree(parts).astype(BF16)
    stack = jnp.stack([mine] + [swap(mine, 2 * s, rows) for s in range(1, chips)])
    return stack, swap(stack, 1, rows)


def reduce_gram(keep, send, rows):
    own = keep + swap(send, 1, rows)
    total = tree([own] + [swap(own, 2 * s, rows) for s in range(1, rows // 2)])
    return total, swap(total, 1, rows)


def eliminate(tiles, size):
    sub = lax.broadcasted_iota(jnp.int32, (8, 1), 0)
    done = []
    for t in range(size // 8):
        for r in range(8):
            j = t * 8 + r
            row = tiles[t][r : r + 1, :]
            scale = lax.rsqrt(row[:, j : j + 1])
            pivot = row * scale
            done.append(pivot)
            for q in range(t, size // 8):
                lead = tiles[q][:, j : j + 1] * scale
                if q == t:
                    lead = jnp.where(sub > r, lead, 0.0)
                tiles[q] = tiles[q] - lead * pivot
    return jnp.concatenate(done, 0)


def rows_of(value):
    return [value[8 * t : 8 * t + 8] for t in range(value.shape[0] // 8)]


def factor_first_kernel(place, mine, theirs, first, rest, whole):
    core = place[1]
    h = mine.shape[0]
    whole[pl.ds(pl.multiple_of(core * h, h), h), :] = mine[...]
    whole[pl.ds(pl.multiple_of((1 - core) * h, h), h), :] = theirs[...]
    line = lax.broadcasted_iota(jnp.int32, (h, h), 0)
    lane = lax.broadcasted_iota(jnp.int32, (h, h), 1)
    eye = (line == lane).astype(F32)
    value = eliminate(rows_of(jnp.concatenate([whole[:h, :], eye], 1)), h)
    first[...] = value
    r12 = value[:, h : 2 * h]
    rest[...] = whole[h:, h:] - exact(r12, r12, ((0,), (0,)))


def factor_last_kernel(first, rest, triangle, inverse, turned):
    h = first.shape[0]
    line = lax.broadcasted_iota(jnp.int32, (h, h), 0)
    lane = lax.broadcasted_iota(jnp.int32, (h, h), 1)
    eye = (line == lane).astype(F32)
    zero = jnp.zeros((h, h), F32)
    second = eliminate(rows_of(jnp.concatenate([rest[...], eye], 1)), h)
    r11, r12, i11 = first[:, :h], first[:, h : 2 * h], first[:, 2 * h :]
    r22, i22 = second[:, :h], second[:, h:]
    i11 = jnp.where(lane <= line, i11, 0.0)
    i22 = jnp.where(lane <= line, i22, 0.0)
    i21 = -exact(i22, exact(r12, i11, ((0,), (0,))), ((1,), (0,)))
    triangle[:h, :h] = jnp.where(lane >= line, r11, 0.0)
    triangle[:h, h:] = r12
    triangle[h:, :h] = zero
    triangle[h:, h:] = jnp.where(lane >= line, r22, 0.0)
    full = jnp.concatenate([jnp.concatenate([i11, zero], 1), jnp.concatenate([i21, i22], 1)], 0)
    inverse[0], inverse[1] = split(full)
    turned[0], turned[1] = split(full.T)


def factor_first(place, mine, theirs):
    h, size = mine.shape
    return call(
        factor_first_kernel, (shape((h, 3 * h), F32), shape((h, h), F32)), [SMEM, VMEM, VMEM],
        (VMEM,) * 2, 8, flops=10 * size**3, moved=20 * MIB, scratch=(pltpu.VMEM((size, size), F32),),
    )(place, mine, theirs)


def factor_last(first, rest):
    size = 2 * first.shape[0]
    both = shape((2, size, size), BF16)
    return call(
        factor_last_kernel, (shape((size, size), F32), both, both), [VMEM, VMEM], (VMEM,) * 3, 8,
        flops=10 * size**3, moved=20 * MIB,
    )(first, rest)


def update_kernel(
    chips, place, inverse, turned, panel, near_one, far_one, near_two, far_two, active,
    top_out, out, cross_buf, tops, results, top_sems, out_sems,
):
    z, core, chip = place[0], place[1], place[2]
    pair = lax.div(z, 2)
    wide = results.shape[2]
    steps = 2 * chips
    two = near_one.shape[1]
    rest = near_two.shape[1] // two
    rows = results.shape[1]
    block = 2 * TILE

    def column(i):
        side = jnp.where(i < chips, core, 1 - core)
        return pl.multiple_of((side * chips + (chip ^ lax.rem(i, chips))) * wide, wide)

    def top_copy(slot, where):
        return pltpu.make_async_copy(tops.at[slot], top_out.at[pl.ds(where, wide), :], top_sems.at[slot])

    def out_copy(slot, where):
        return pltpu.make_async_copy(results.at[slot], out.at[:, pl.ds(where, wide)], out_sems.at[slot])

    def body(i, _):
        slot = lax.rem(i, 2)
        where = column(i)
        s = lax.rem(i, chips)

        def place_cross(one, several):
            cross_buf[pl.ds(pl.multiple_of(pair * two, two), two), :] = one[s]
            for k in range(rest):
                q = k + (k >= pair).astype(jnp.int32)
                cross_buf[pl.ds(pl.multiple_of(q * two, two), two), :] = several[s, k * two : (k + 1) * two, :]

        @pl.when(i < chips)
        def _():
            place_cross(near_one, near_two)

        @pl.when(i >= chips)
        def _():
            place_cross(far_one, far_two)

        sums = cross_buf[...]
        turn_ = ((1,), (0,))
        top = dot(inverse[0], sums, turn_) + dot(inverse[1], sums, turn_)
        high, low = split(top)
        coeff = (dot(turned[0], high, turn_) + (dot(turned[0], low, turn_) + dot(turned[1], high, turn_))).astype(BF16)

        @pl.when(i >= 2)
        def _():
            top_copy(slot, 0).wait()
            out_copy(slot, 0).wait()

        tops[slot] = top.T
        top_copy(slot, where).start()

        def rows_body(k, _):
            part = pl.ds(pl.multiple_of(k * block, block), block)
            product = dot(panel[part, :], coeff, turn_)
            results[slot, part, :] = (active[part, pl.ds(where, wide)].astype(F32) - product).astype(BF16)
            return 0

        lax.fori_loop(0, rows // block, rows_body, 0, unroll=True)
        out_copy(slot, where).start()
        return 0

    lax.fori_loop(0, steps, body, 0)
    for slot in range(2):
        top_copy(slot, 0).wait()
        out_copy(slot, 0).wait()


def update(place, inverse, turned, panel, one, two, active, chips):
    rows, size = panel.shape
    columns = active.shape[1]
    wide = columns // (2 * chips)
    return call(
        functools.partial(update_kernel, chips),
        (shape((columns, size), F32), shape((rows, columns), BF16)),
        [SMEM] + [VMEM] * 8, (ANY, ANY), 12,
        flops=2 * rows * size * columns, moved=2 * rows * columns,
        scratch=(
            pltpu.VMEM((size, wide), BF16),
            pltpu.VMEM((2, wide, size), F32),
            pltpu.VMEM((2, rows, wide), BF16),
            pltpu.SemaphoreType.DMA((2,)),
            pltpu.SemaphoreType.DMA((2,)),
        ),
    )(place, inverse, turned, panel, *one, *two, active)


def local(nrow, ncol, panel, trailing, tile_list):
    row = lax.axis_index("row")
    place = jnp.stack([lax.axis_index("col"), row % 2, row // 2]).astype(jnp.int32)
    own = pick(tile_list, panel.T)
    blocks = [own]
    for s in range(1, ncol):
        blocks.append(lax.ppermute(own, "col", [(i, i ^ s) for i in range(ncol)]))
    across = 2 * panel.shape[1]
    active, keep, send = cross_pair(tile_list, place, own, blocks[1], trailing)
    one = reduce_cross(place, keep, swap(send, 1, nrow), nrow)
    full, keep, send = gram(place, blocks)
    sums = reduce_gram(keep, send, nrow)
    turned_panel = turn(full)
    send = cross_rest(False, place, full, active, across)
    send = swap(send, 1, nrow)
    keep = cross_rest(True, place, full, active, across)
    two = reduce_cross(place, keep, send, nrow)
    triangle, inverse, turned = factor_last(*factor_first(place, *sums))
    top_rows, updated = update(place, inverse, turned, turned_panel, one, two, active, nrow // 2)
    return triangle, top_rows, updated


def solution(mesh):
    nrow, ncol = mesh.shape["row"], mesh.shape["col"]

    def program(panel, trailing, tile_list):
        return local(nrow, ncol, panel, trailing, tile_list)

    return jax.shard_map(
        program,
        mesh=mesh,
        in_specs=(P("row", "col"), P("row", "col"), P("row")),
        out_specs=(P(), P("col", None), P("row", "col")),
        check_vma=False,
    )
```

time: 155 us -> 122 us (0.79)
  the two profiles are of different devices: /device:TPU:17 before, /device:TPU:0 now
where the time goes in v2:
time: 122 us
  Pallas kernels  57.6 us (47%)
  waiting for transfers between devices  34.3 us (28%)
  starting transfers between devices  26.2 us (21%)
  local copies, waits for them, and re-layouts  2.3 us (2%)
    ppermute x3, waiting for transfers between devices, local(): blocks.append(lax.ppermute(own, 'col', [(i, i ^ s) for i in range(ncol)]))  21.5 us
    ppermute x21, starting transfers between devices, swap(): return lax.ppermute(value, 'row', [(i, i ^ bit) for i in range(rows)])  20.5 us
    pallas_call x1, Pallas kernels, update(): call(functools.partial(update_kernel, chips), (shape((columns, size), F32...  15.5 us
    ppermute x21, waiting for transfers between devices, swap(): return lax.ppermute(value, 'row', [(i, i ^ bit) for i in range(rows)])  12.8 us
    pallas_call x1, Pallas kernels, factor_last(): call(factor_last_kernel, (shape((size, size), F32), both, both), [VMEM, V...  11.6 us
    pallas_call x1, Pallas kernels, factor_first(): call(factor_first_kernel, (shape((h, 3 * h), F32), shape((h, h), F32)), [...  11.5 us
    pallas_call x1, Pallas kernels, cross_pair(): call(functools.partial(cross_pair_kernel, steps), (pltpu.VMEM((rows, colu...  9.07 us
    pallas_call x2, Pallas kernels, cross_rest(): call(functools.partial(cross_rest_kernel, 4, mine), shape((deep, columns...  5.93 us
  transfers between devices with their start and end apart: 24, of which 12 were waited for; matrix products, arithmetic and copies ran while one was open for 0% of the time, Pallas kernels for 30%

profile of v2, /device:TPU:0, one launch (start us, length us, event | category | flops | bytes accessed | tf_op | source)
XLA Modules:
  0.0 121.7 jit_solution(17984722923412391341)
XLA Ops:
  2.9 3.1 %collective-permute-start = (bf16[64,2816]{1,0:T(8,128)(2,1)S(1)}, bf16[64,2816]{1,0:T(8,128)(2,1)S(1)}, u32[]{:S(2)}, u32[]{:S(2)}) collective-permute-start(bf16[64,2816]{1,0:T(8,128)(2,1)S(1)} %shard_map.58.refs_0_.own), channel_id=1, source_target_pairs={{0,1},{1,0},{2,3},{3,2},{4,5},{5,4},{6,7},{7,6},{8,9},{9,8},{10,11... | collective-permute-start | bytes 1081352 | tf_op jit(solution)/shard_map/ppermute | solution.py:402
  6.0 2.5 %collective-permute-start.2 = (bf16[64,2816]{1,0:T(8,128)(2,1)S(1)}, bf16[64,2816]{1,0:T(8,128)(2,1)S(1)}, u32[]{:S(2)}, u32[]{:S(2)}) collective-permute-start(bf16[64,2816]{1,0:T(8,128)(2,1)S(1)} %shard_map.58.refs_0_.own), channel_id=1, source_target_pairs={{0,3},{1,2},{2,1},{3,0},{4,7},{5,6},{6,5},{7,4},{8,11},{9,10},{10,... | collective-permute-start | bytes 1081352 | tf_op jit(solution)/shard_map/ppermute | solution.py:402
  8.7 6.1 %collective-permute-done.refs_1_.other = bf16[64,2816]{1,0:T(8,128)(2,1)S(1)} collective-permute-done((bf16[64,2816]{1,0:T(8,128)(2,1)S(1)}, bf16[64,2816]{1,0:T(8,128)(2,1)S(1)}, u32[]{:S(2)}, u32[]{:S(2)}) %collective-permute-start) | collective-permute-done | bytes 360480 | tf_op jit(solution)/shard_map/ppermute | solution.py:402
  15.5 9.1 %shard_map.63 = (bf16[2816,4096]{1,0:T(8,128)(2,1)S(1)}, f32[128,2048]{1,0:T(8,128)S(1)}, bf16[128,2048]{1,0:T(8,128)(2,1)S(1)}) custom-call(s32[22]{0:T(128)S(1)} %copy-done.2, s32[3]{0:T(128)S(1)} %pad_add_fusion.place, bf16[64,2816]{1,0:T(8,128)(2,1)S(1)} %shard_map.58.refs_0_.own, bf16[64,2816]{1,0:T(8,128)(2,1)S(1)} %collective-permute-done.refs_1_.other, ...), custom_call_target="tpu_custom_call" | custom-call | flops 2952790016 | bytes 23068672 | tf_op jit(solution)/shard_map/pallas_call | solution.py:146
  25.6 14.3 %collective-permute-done.1.refs_2_ = bf16[64,2816]{1,0:T(8,128)(2,1)S(1)} collective-permute-done((bf16[64,2816]{1,0:T(8,128)(2,1)S(1)}, bf16[64,2816]{1,0:T(8,128)(2,1)S(1)}, u32[]{:S(2)}, u32[]{:S(2)}) %collective-permute-start.1) | collective-permute-done | bytes 360480 | tf_op jit(solution)/shard_map/ppermute | solution.py:402
  39.9 1.7 %shard_map.59 = (bf16[256,2816]{1,0:T(8,128)(2,1)S(1)}, f32[128,256]{1,0:T(8,128)S(1)}, f32[128,256]{1,0:T(8,128)S(1)}) custom-call(s32[3]{0:T(128)S(1)} %pad_add_fusion.place, bf16[64,2816]{1,0:T(8,128)(2,1)S(1)} %shard_map.58.refs_0_.own, bf16[64,2816]{1,0:T(8,128)(2,1)S(1)} %collective-permute-done.refs_1_.other, ...), custom_call_target="tpu_custom_call" | custom-call | flops 369098752 | bytes 2883584 | tf_op jit(solution)/shard_map/pallas_call | solution.py:81
  41.6 2.9 %shard_map.66 = bf16[128,2048]{1,0:T(8,128)(2,1)S(1)} custom-call(s32[3]{0:T(128)S(1)} %pad_add_fusion.place, bf16[256,2816]{1,0:T(8,128)(2,1)S(1)} %get-tuple-element.31.full, bf16[2816,4096]{1,0:T(8,128)(2,1)S(1)} %get-tuple-element.38.active), custom_call_target="tpu_custom_call" | custom-call | flops 1476395008 | bytes 11534336 | tf_op jit(solution)/shard_map/pallas_call | solution.py:176
  45.1 3.1 %shard_map.65.keep = f32[128,2048]{1,0:T(8,128)S(1)} custom-call(s32[3]{0:T(128)S(1)} %pad_add_fusion.place, bf16[256,2816]{1,0:T(8,128)(2,1)S(1)} %get-tuple-element.31.full, bf16[2816,4096]{1,0:T(8,128)(2,1)S(1)} %get-tuple-element.38.active), custom_call_target="tpu_custom_call" | custom-call | flops 1476395008 | bytes 11534336 | tf_op jit(solution)/shard_map/pallas_call | solution.py:176
  48.8 1.6 %collective-permute-start.17 = (bf16[128,512]{1,0:T(8,128)(2,1)S(1)}, bf16[128,512]{1,0:T(8,128)(2,1)S(1)}, u32[]{:S(2)}, u32[]{:S(2)}) collective-permute-start(bf16[128,512]{1,0:T(8,128)(2,1)S(1)} %get-tuple-element.40), channel_id=1, source_target_pairs={{0,8},{4,12},{8,0},{12,4},{16,24},{20,28},{24,16},{28,20},{1,9},{5... | collective-permute-start | bytes 393224 | tf_op jit(solution)/shard_map/ppermute | solution.py:206
  50.4 1.5 %collective-permute-start.18 = (bf16[128,512]{1,0:T(8,128)(2,1)S(1)}, bf16[128,512]{1,0:T(8,128)(2,1)S(1)}, u32[]{:S(2)}, u32[]{:S(2)}) collective-permute-start(bf16[128,512]{1,0:T(8,128)(2,1)S(1)} %get-tuple-element.41), channel_id=1, source_target_pairs={{0,16},{4,20},{8,24},{12,28},{16,0},{20,4},{24,8},{28,12},{1,17},{... | collective-permute-start | bytes 393224 | tf_op jit(solution)/shard_map/ppermute | solution.py:206
  53.0 1.6 %collective-permute-start.9 = (bf16[128,512]{1,0:T(8,128)(2,1)S(1)}, bf16[128,512]{1,0:T(8,128)(2,1)S(1)}, u32[]{:S(2)}, u32[]{:S(2)}) collective-permute-start(bf16[128,512]{1,0:T(8,128)(2,1)S(1)} %get-tuple-element.35), channel_id=1, source_target_pairs={{0,8},{4,12},{8,0},{12,4},{16,24},{20,28},{24,16},{28,20},{1,9},{5... | collective-permute-start | bytes 393224 | tf_op jit(solution)/shard_map/ppermute | solution.py:206
  54.8 1.5 %collective-permute-start.10 = (bf16[128,512]{1,0:T(8,128)(2,1)S(1)}, bf16[128,512]{1,0:T(8,128)(2,1)S(1)}, u32[]{:S(2)}, u32[]{:S(2)}) collective-permute-start(bf16[128,512]{1,0:T(8,128)(2,1)S(1)} %get-tuple-element.36), channel_id=1, source_target_pairs={{0,16},{4,20},{8,24},{12,28},{16,0},{20,4},{24,8},{28,12},{1,17},{... | collective-permute-start | bytes 393224 | tf_op jit(solution)/shard_map/ppermute | solution.py:206
  56.3 1.8 %collective-permute-done.18 = bf16[128,512]{1,0:T(8,128)(2,1)S(1)} collective-permute-done((bf16[128,512]{1,0:T(8,128)(2,1)S(1)}, bf16[128,512]{1,0:T(8,128)(2,1)S(1)}, u32[]{:S(2)}, u32[]{:S(2)}) %collective-permute-start.18) | collective-permute-done | bytes 131104 | tf_op jit(solution)/shard_map/ppermute | solution.py:206
  58.0 1.6 %collective-permute-start.11 = (bf16[128,512]{1,0:T(8,128)(2,1)S(1)}, bf16[128,512]{1,0:T(8,128)(2,1)S(1)}, u32[]{:S(2)}, u32[]{:S(2)}) collective-permute-start(bf16[128,512]{1,0:T(8,128)(2,1)S(1)} %get-tuple-element.37), channel_id=1, source_target_pairs={{0,24},{4,28},{8,16},{12,20},{16,8},{20,12},{24,0},{28,4},{1,25},{... | collective-permute-start | bytes 393224 | tf_op jit(solution)/shard_map/ppermute | solution.py:206
  59.7 1.4 %collective-permute-start.22 = (bf16[128,512]{1,0:T(8,128)(2,1)S(1)}, bf16[128,512]{1,0:T(8,128)(2,1)S(1)}, u32[]{:S(2)}, u32[]{:S(2)}) collective-permute-start(bf16[128,512]{1,0:T(8,128)(2,1)S(1)} %add_convert_fusion), channel_id=1, source_target_pairs={{0,24},{4,28},{8,16},{12,20},{16,8},{20,12},{24,0},{28,4},{1,25},{... | collective-permute-start | bytes 393224 | tf_op jit(solution)/shard_map/ppermute | solution.py:206
  61.1 2.5 %collective-permute-start.21 = (bf16[128,512]{1,0:T(8,128)(2,1)S(1)}, bf16[128,512]{1,0:T(8,128)(2,1)S(1)}, u32[]{:S(2)}, u32[]{:S(2)}) collective-permute-start(bf16[128,512]{1,0:T(8,128)(2,1)S(1)} %add_convert_fusion), channel_id=1, source_target_pairs={{0,16},{4,20},{8,24},{12,28},{16,0},{20,4},{24,8},{28,12},{1,17},{... | collective-permute-start | bytes 393224 | tf_op jit(solution)/shard_map/ppermute | solution.py:206
  63.6 3.6 %collective-permute-done.10 = bf16[128,512]{1,0:T(8,128)(2,1)S(1)} collective-permute-done((bf16[128,512]{1,0:T(8,128)(2,1)S(1)}, bf16[128,512]{1,0:T(8,128)(2,1)S(1)}, u32[]{:S(2)}, u32[]{:S(2)}) %collective-permute-start.10) | collective-permute-done | bytes 131104 | tf_op jit(solution)/shard_map/ppermute | solution.py:206
  67.3 3.1 %collective-permute-start.14 = (bf16[128,512]{1,0:T(8,128)(2,1)S(1)}, bf16[128,512]{1,0:T(8,128)(2,1)S(1)}, u32[]{:S(2)}, u32[]{:S(2)}) collective-permute-start(bf16[128,512]{1,0:T(8,128)(2,1)S(1)} %add_convert_fusion.1), channel_id=1, source_target_pairs={{0,24},{4,28},{8,16},{12,20},{16,8},{20,12},{24,0},{28,4},{1,25},{... | collective-permute-start | bytes 393224 | tf_op jit(solution)/shard_map/ppermute | solution.py:206
  71.4 2.5 %collective-permute-start.6 = (f32[128,256]{1,0:T(8,128)S(1)}, f32[128,256]{1,0:T(8,128)S(1)}, u32[]{:S(2)}, u32[]{:S(2)}) collective-permute-start(f32[128,256]{1,0:T(8,128)S(1)} %add.36), channel_id=1, source_target_pairs={{0,24},{4,28},{8,16},{12,20},{16,8},{20,12},{24,0},{28,4},{1,25},{... | collective-permute-start | bytes 393224 | tf_op jit(solution)/shard_map/ppermute | solution.py:206
  75.3 3.8 %collective-permute-done.13 = bf16[128,512]{1,0:T(8,128)(2,1)S(1)} collective-permute-done((bf16[128,512]{1,0:T(8,128)(2,1)S(1)}, bf16[128,512]{1,0:T(8,128)(2,1)S(1)}, u32[]{:S(2)}, u32[]{:S(2)}) %collective-permute-start.13) | collective-permute-done | bytes 131104 | tf_op jit(solution)/shard_map/ppermute | solution.py:206
  80.2 1.3 %collective-permute-done.5 = f32[128,256]{1,0:T(8,128)S(1)} collective-permute-done((f32[128,256]{1,0:T(8,128)S(1)}, f32[128,256]{1,0:T(8,128)S(1)}, u32[]{:S(2)}, u32[]{:S(2)}) %collective-permute-start.5) | collective-permute-done | bytes 131104 | tf_op jit(solution)/shard_map/ppermute | solution.py:206
  83.0 11.5 %shard_map.60 = (f32[128,384]{1,0:T(8,128)S(1)}, f32[128,128]{1,0:T(8,128)S(1)}) custom-call(s32[3]{0:T(128)S(1)} %pad_add_fusion.place, f32[128,256]{1,0:T(8,128)S(1)} %add_add_fusion.mine, f32[128,256]{1,0:T(8,128)S(1)} %collective-permute-done.7.theirs), custom_call_target="tpu_custom_call" | custom-call | flops 167772160 | bytes 20971520 | tf_op jit(solution)/shard_map/pallas_call | solution.py:290
  94.5 11.6 %shard_map.61 = (f32[256,256]{1,0:T(8,128)}, bf16[2,256,256]{2,1,0:T(8,128)(2,1)S(1)}, bf16[2,256,256]{2,1,0:T(8,128)(2,1)S(1)}) custom-call(f32[128,384]{1,0:T(8,128)S(1)} %get-tuple-element.26.first, f32[128,128]{1,0:T(8,128)S(1)} %get-tuple-element.27.rest), custom_call_target="tpu_custom_call" | custom-call | flops 167772160 | bytes 20971520 | tf_op jit(solution)/shard_map/pallas_call | solution.py:299
  106.1 15.5 %shard_map.68 = (f32[4096,256]{1,0:T(8,128)}, bf16[2816,4096]{1,0:T(8,128)(2,1)}) custom-call(s32[3]{0:T(128)S(1)} %pad_add_fusion.place, bf16[2,256,256]{2,1,0:T(8,128)(2,1)S(1)} %get-tuple-element.29.inverse, bf16[2,256,256]{2,1,0:T(8,128)(2,1)S(1)} %get-tuple-element.30.turned, bf16[2816,256]{1,0:T(8,128)(2,1)S(1)} %shard_map.62.panel, ...), custom_call_target="tpu_custom_call" | custom-call | flops 5905580032 | bytes 23068672 | tf_op jit(solution)/shard_map/pallas_call | solution.py:381
  (48 shorter events, 11.8 us)
Async XLA Ops:
  2.9 11.9 %collective-permute-start = (bf16[64,2816]{1,0:T(8,128)(2,1)S(1)}, bf16[64,2816]{1,0:T(8,128)(2,1)S(1)}, u32[]{:S(2)}, u32[]{:S(2)}) collective-permute-start(bf16[64,2816]{1,0:T(8,128)(2,1)S(1)} %shard_map.58.refs_0_.own), channel_id=1, source_target_pairs={{0,1},{1,0},{2,3},{3,2},{4,5},{5,4},{6,7},{7,6},{8,9},{9,8},{10,11... | collective-permute-start | bytes 1081352 | tf_op jit(solution)/shard_map/ppermute | solution.py:402
  6.0 19.6 %collective-permute-start.2 = (bf16[64,2816]{1,0:T(8,128)(2,1)S(1)}, bf16[64,2816]{1,0:T(8,128)(2,1)S(1)}, u32[]{:S(2)}, u32[]{:S(2)}) collective-permute-start(bf16[64,2816]{1,0:T(8,128)(2,1)S(1)} %shard_map.58.refs_0_.own), channel_id=1, source_target_pairs={{0,3},{1,2},{2,1},{3,0},{4,7},{5,6},{6,5},{7,4},{8,11},{9,10},{10,... | collective-permute-start | bytes 1081352 | tf_op jit(solution)/shard_map/ppermute | solution.py:402
  8.5 31.4 %collective-permute-start.1 = (bf16[64,2816]{1,0:T(8,128)(2,1)S(1)}, bf16[64,2816]{1,0:T(8,128)(2,1)S(1)}, u32[]{:S(2)}, u32[]{:S(2)}) collective-permute-start(bf16[64,2816]{1,0:T(8,128)(2,1)S(1)} %shard_map.58.refs_0_.own), channel_id=1, source_target_pairs={{0,2},{1,3},{2,0},{3,1},{4,6},{5,7},{6,4},{7,5},{8,10},{9,11},{10,... | collective-permute-start | bytes 1081352 | tf_op jit(solution)/shard_map/ppermute | solution.py:402
  44.5 3.7 %collective-permute-start.16 = (bf16[128,2048]{1,0:T(8,128)(2,1)S(1)}, bf16[128,2048]{1,0:T(8,128)(2,1)S(1)}, u32[]{:S(2)}, u32[]{:S(2)}) collective-permute-start(bf16[128,2048]{1,0:T(8,128)(2,1)S(1)} %shard_map.66), channel_id=1, source_target_pairs={{0,4},{4,0},{8,12},{12,8},{16,20},{20,16},{24,28},{28,24},{1,5},{5... | collective-permute-start | bytes 1572872 | tf_op jit(solution)/shard_map/ppermute | solution.py:206
  44.6 7.8 %collective-permute-start.8 = (bf16[128,2048]{1,0:T(8,128)(2,1)S(1)}, bf16[128,2048]{1,0:T(8,128)(2,1)S(1)}, u32[]{:S(2)}, u32[]{:S(2)}) collective-permute-start(bf16[128,2048]{1,0:T(8,128)(2,1)S(1)} %get-tuple-element.33), channel_id=1, source_target_pairs={{0,4},{4,0},{8,12},{12,8},{16,20},{20,16},{24,28},{28,24},{1,5},{5... | collective-permute-start | bytes 1572872 | tf_op jit(solution)/shard_map/ppermute | solution.py:206
  48.8 6.0 %collective-permute-start.17 = (bf16[128,512]{1,0:T(8,128)(2,1)S(1)}, bf16[128,512]{1,0:T(8,128)(2,1)S(1)}, u32[]{:S(2)}, u32[]{:S(2)}) collective-permute-start(bf16[128,512]{1,0:T(8,128)(2,1)S(1)} %get-tuple-element.40), channel_id=1, source_target_pairs={{0,8},{4,12},{8,0},{12,4},{16,24},{20,28},{24,16},{28,20},{1,9},{5... | collective-permute-start | bytes 393224 | tf_op jit(solution)/shard_map/ppermute | solution.py:206
  50.4 7.7 %collective-permute-start.18 = (bf16[128,512]{1,0:T(8,128)(2,1)S(1)}, bf16[128,512]{1,0:T(8,128)(2,1)S(1)}, u32[]{:S(2)}, u32[]{:S(2)}) collective-permute-start(bf16[128,512]{1,0:T(8,128)(2,1)S(1)} %get-tuple-element.41), channel_id=1, source_target_pairs={{0,16},{4,20},{8,24},{12,28},{16,0},{20,4},{24,8},{28,12},{1,17},{... | collective-permute-start | bytes 393224 | tf_op jit(solution)/shard_map/ppermute | solution.py:206
  51.9 7.7 %collective-permute-start.19 = (bf16[128,512]{1,0:T(8,128)(2,1)S(1)}, bf16[128,512]{1,0:T(8,128)(2,1)S(1)}, u32[]{:S(2)}, u32[]{:S(2)}) collective-permute-start(bf16[128,512]{1,0:T(8,128)(2,1)S(1)} %get-tuple-element.42), channel_id=1, source_target_pairs={{0,24},{4,28},{8,16},{12,20},{16,8},{20,12},{24,0},{28,4},{1,25},{... | collective-permute-start | bytes 393224 | tf_op jit(solution)/shard_map/ppermute | solution.py:206
  52.4 18.0 %collective-permute-start.3 = (f32[128,256]{1,0:T(8,128)S(1)}, f32[128,256]{1,0:T(8,128)S(1)}, u32[]{:S(2)}, u32[]{:S(2)}) collective-permute-start(f32[128,256]{1,0:T(8,128)S(1)} %get-tuple-element.25), channel_id=1, source_target_pairs={{0,4},{4,0},{8,12},{12,8},{16,20},{20,16},{24,28},{28,24},{1,5},{5... | collective-permute-start | bytes 393224 | tf_op jit(solution)/shard_map/ppermute | solution.py:206
  53.0 8.1 %collective-permute-start.9 = (bf16[128,512]{1,0:T(8,128)(2,1)S(1)}, bf16[128,512]{1,0:T(8,128)(2,1)S(1)}, u32[]{:S(2)}, u32[]{:S(2)}) collective-permute-start(bf16[128,512]{1,0:T(8,128)(2,1)S(1)} %get-tuple-element.35), channel_id=1, source_target_pairs={{0,8},{4,12},{8,0},{12,4},{16,24},{20,28},{24,16},{28,20},{1,9},{5... | collective-permute-start | bytes 393224 | tf_op jit(solution)/shard_map/ppermute | solution.py:206
  54.8 12.4 %collective-permute-start.10 = (bf16[128,512]{1,0:T(8,128)(2,1)S(1)}, bf16[128,512]{1,0:T(8,128)(2,1)S(1)}, u32[]{:S(2)}, u32[]{:S(2)}) collective-permute-start(bf16[128,512]{1,0:T(8,128)(2,1)S(1)} %get-tuple-element.36), channel_id=1, source_target_pairs={{0,16},{4,20},{8,24},{12,28},{16,0},{20,4},{24,8},{28,12},{1,17},{... | collective-permute-start | bytes 393224 | tf_op jit(solution)/shard_map/ppermute | solution.py:206
  58.0 9.1 %collective-permute-start.11 = (bf16[128,512]{1,0:T(8,128)(2,1)S(1)}, bf16[128,512]{1,0:T(8,128)(2,1)S(1)}, u32[]{:S(2)}, u32[]{:S(2)}) collective-permute-start(bf16[128,512]{1,0:T(8,128)(2,1)S(1)} %get-tuple-element.37), channel_id=1, source_target_pairs={{0,24},{4,28},{8,16},{12,20},{16,8},{20,12},{24,0},{28,4},{1,25},{... | collective-permute-start | bytes 393224 | tf_op jit(solution)/shard_map/ppermute | solution.py:206
  59.7 11.1 %collective-permute-start.22 = (bf16[128,512]{1,0:T(8,128)(2,1)S(1)}, bf16[128,512]{1,0:T(8,128)(2,1)S(1)}, u32[]{:S(2)}, u32[]{:S(2)}) collective-permute-start(bf16[128,512]{1,0:T(8,128)(2,1)S(1)} %add_convert_fusion), channel_id=1, source_target_pairs={{0,24},{4,28},{8,16},{12,20},{16,8},{20,12},{24,0},{28,4},{1,25},{... | collective-permute-start | bytes 393224 | tf_op jit(solution)/shard_map/ppermute | solution.py:206
  61.1 10.3 %collective-permute-start.21 = (bf16[128,512]{1,0:T(8,128)(2,1)S(1)}, bf16[128,512]{1,0:T(8,128)(2,1)S(1)}, u32[]{:S(2)}, u32[]{:S(2)}) collective-permute-start(bf16[128,512]{1,0:T(8,128)(2,1)S(1)} %add_convert_fusion), channel_id=1, source_target_pairs={{0,16},{4,20},{8,24},{12,28},{16,0},{20,4},{24,8},{28,12},{1,17},{... | collective-permute-start | bytes 393224 | tf_op jit(solution)/shard_map/ppermute | solution.py:206
  67.2 6.7 %collective-permute-start.20 = (bf16[128,512]{1,0:T(8,128)(2,1)S(1)}, bf16[128,512]{1,0:T(8,128)(2,1)S(1)}, u32[]{:S(2)}, u32[]{:S(2)}) collective-permute-start(bf16[128,512]{1,0:T(8,128)(2,1)S(1)} %add_convert_fusion), channel_id=1, source_target_pairs={{0,8},{4,12},{8,0},{12,4},{16,24},{20,28},{24,16},{28,20},{1,9},{5... | collective-permute-start | bytes 393224 | tf_op jit(solution)/shard_map/ppermute | solution.py:206
  67.3 7.6 %collective-permute-start.14 = (bf16[128,512]{1,0:T(8,128)(2,1)S(1)}, bf16[128,512]{1,0:T(8,128)(2,1)S(1)}, u32[]{:S(2)}, u32[]{:S(2)}) collective-permute-start(bf16[128,512]{1,0:T(8,128)(2,1)S(1)} %add_convert_fusion.1), channel_id=1, source_target_pairs={{0,24},{4,28},{8,16},{12,20},{16,8},{20,12},{24,0},{28,4},{1,25},{... | collective-permute-start | bytes 393224 | tf_op jit(solution)/shard_map/ppermute | solution.py:206
  70.3 8.8 %collective-permute-start.13 = (bf16[128,512]{1,0:T(8,128)(2,1)S(1)}, bf16[128,512]{1,0:T(8,128)(2,1)S(1)}, u32[]{:S(2)}, u32[]{:S(2)}) collective-permute-start(bf16[128,512]{1,0:T(8,128)(2,1)S(1)} %add_convert_fusion.1), channel_id=1, source_target_pairs={{0,16},{4,20},{8,24},{12,28},{16,0},{20,4},{24,8},{28,12},{1,17},{... | collective-permute-start | bytes 393224 | tf_op jit(solution)/shard_map/ppermute | solution.py:206
  70.8 8.3 %collective-permute-start.12 = (bf16[128,512]{1,0:T(8,128)(2,1)S(1)}, bf16[128,512]{1,0:T(8,128)(2,1)S(1)}, u32[]{:S(2)}, u32[]{:S(2)}) collective-permute-start(bf16[128,512]{1,0:T(8,128)(2,1)S(1)} %add_convert_fusion.1), channel_id=1, source_target_pairs={{0,8},{4,12},{8,0},{12,4},{16,24},{20,28},{24,16},{28,20},{1,9},{5... | collective-permute-start | bytes 393224 | tf_op jit(solution)/shard_map/ppermute | solution.py:206
  71.4 8.8 %collective-permute-start.6 = (f32[128,256]{1,0:T(8,128)S(1)}, f32[128,256]{1,0:T(8,128)S(1)}, u32[]{:S(2)}, u32[]{:S(2)}) collective-permute-start(f32[128,256]{1,0:T(8,128)S(1)} %add.36), channel_id=1, source_target_pairs={{0,24},{4,28},{8,16},{12,20},{16,8},{20,12},{24,0},{28,4},{1,25},{... | collective-permute-start | bytes 393224 | tf_op jit(solution)/shard_map/ppermute | solution.py:206
  73.9 7.6 %collective-permute-start.5 = (f32[128,256]{1,0:T(8,128)S(1)}, f32[128,256]{1,0:T(8,128)S(1)}, u32[]{:S(2)}, u32[]{:S(2)}) collective-permute-start(f32[128,256]{1,0:T(8,128)S(1)} %add.36), channel_id=1, source_target_pairs={{0,16},{4,20},{8,24},{12,28},{16,0},{20,4},{24,8},{28,12},{1,17},{... | collective-permute-start | bytes 393224 | tf_op jit(solution)/shard_map/ppermute | solution.py:206
  74.9 6.7 %collective-permute-start.4 = (f32[128,256]{1,0:T(8,128)S(1)}, f32[128,256]{1,0:T(8,128)S(1)}, u32[]{:S(2)}, u32[]{:S(2)}) collective-permute-start(f32[128,256]{1,0:T(8,128)S(1)} %add.36), channel_id=1, source_target_pairs={{0,8},{4,12},{8,0},{12,4},{16,24},{20,28},{24,16},{28,20},{1,9},{5... | collective-permute-start | bytes 393224 | tf_op jit(solution)/shard_map/ppermute | solution.py:206
  79.1 27.0 %collective-permute-start.23 = (bf16[4,128,512]{2,1,0:T(8,128)(2,1)S(1)}, bf16[4,128,512]{2,1,0:T(8,128)(2,1)S(1)}, u32[]{:S(2)}, u32[]{:S(2)}) collective-permute-start(bf16[4,128,512]{2,1,0:T(8,128)(2,1)S(1)} %pad_maximum_fusion.1.near_two), channel_id=1, source_target_pairs={{0,4},{4,0},{8,12},{12,8},{16,20},{20,16},{24,28},{28,24},{1,5},{5... | collective-permute-start | bytes 1572872 | tf_op jit(solution)/shard_map/ppermute | solution.py:206
  79.2 26.9 %collective-permute-start.15 = (bf16[4,128,512]{2,1,0:T(8,128)(2,1)S(1)}, bf16[4,128,512]{2,1,0:T(8,128)(2,1)S(1)}, u32[]{:S(2)}, u32[]{:S(2)}) collective-permute-start(bf16[4,128,512]{2,1,0:T(8,128)(2,1)S(1)} %pad_maximum_fusion.near_one), channel_id=1, source_target_pairs={{0,4},{4,0},{8,12},{12,8},{16,20},{20,16},{24,28},{28,24},{1,5},{5... | collective-permute-start | bytes 1572872 | tf_op jit(solution)/shard_map/ppermute | solution.py:206
  81.6 1.4 %collective-permute-start.7 = (f32[128,256]{1,0:T(8,128)S(1)}, f32[128,256]{1,0:T(8,128)S(1)}, u32[]{:S(2)}, u32[]{:S(2)}) collective-permute-start(f32[128,256]{1,0:T(8,128)S(1)} %add_add_fusion.mine), channel_id=1, source_target_pairs={{0,4},{4,0},{8,12},{12,8},{16,20},{20,16},{24,28},{28,24},{1,5},{5... | collective-permute-start | bytes 393224 | tf_op jit(solution)/shard_map/ppermute | solution.py:206
  (3 other events, 2.3 us)

commit v3 on v2

v3 whole, which is shorter than its diff:
```python
import functools
import jax
import jax.numpy as jnp
from jax import lax
from jax.sharding import PartitionSpec as P
from jax.experimental import pallas as pl
from jax.experimental.pallas import tpu as pltpu

TILE = 128
BAND = 4
F32 = jnp.float32
BF16 = jnp.bfloat16
VMEM = pl.BlockSpec(memory_space=pltpu.VMEM)
SMEM = pl.BlockSpec(memory_space=pltpu.SMEM)
ANY = pl.BlockSpec(memory_space=pl.ANY)
HBM = pl.BlockSpec(memory_space=pltpu.HBM)
MIB = 1 << 20


def shape(dims, kind):
    return jax.ShapeDtypeStruct(dims, kind)


def call(body, out_shape, in_specs, out_specs, grant, flops=0, moved=0, scratch=()):
    return pl.pallas_call(
        body,
        out_shape=out_shape,
        in_specs=in_specs,
        out_specs=out_specs,
        scratch_shapes=list(scratch),
        cost_estimate=pl.CostEstimate(flops=flops, bytes_accessed=moved, transcendentals=0),
        compiler_params=pltpu.CompilerParams(vmem_limit_bytes=grant * MIB),
    )


def stay(value):
    return pltpu.with_memory_space_constraint(value, pltpu.HBM)


def dot(a, b, contract):
    return lax.dot_general(a, b, (contract, ((), ())), preferred_element_type=F32)


def exact(a, b, contract):
    return lax.dot_general(
        a, b, (contract, ((), ())), precision=lax.Precision.HIGHEST, preferred_element_type=F32
    )


def split(value):
    high = value.astype(BF16)
    return high, (value - high.astype(F32)).astype(BF16)


def pick_kernel(listed, source, out, tiles, panel, sems):
    copies = (
        pltpu.make_async_copy(listed, tiles, sems.at[0]),
        pltpu.make_async_copy(source, panel, sems.at[1]),
    )
    for copy in copies:
        copy.start()
    for copy in copies:
        copy.wait()
    for k in range(tiles.shape[0]):
        start = pl.multiple_of(tiles[k] * TILE, TILE)
        out[:, k * TILE : (k + 1) * TILE] = panel[:, pl.ds(start, TILE)]


def pick(tile_list, panel):
    rows = tile_list.shape[0] * TILE
    return call(
        pick_kernel, shape((panel.shape[0], rows), BF16), [HBM, HBM], VMEM, 8,
        moved=4 * rows * panel.shape[0],
        scratch=(
            pltpu.SMEM(tile_list.shape, jnp.int32),
            pltpu.VMEM(panel.shape, BF16),
            pltpu.SemaphoreType.DMA((2,)),
        ),
    )(stay(tile_list), stay(panel))


def load_kernel(listed, trailing, active, tiles, sems):
    copy = pltpu.make_async_copy(listed, tiles, sems.at[0])
    copy.start()
    copy.wait()
    for k in range(tiles.shape[0]):
        start = pl.multiple_of(tiles[k] * TILE, TILE)
        pltpu.make_async_copy(
            trailing.at[pl.ds(start, TILE), :], active.at[pl.ds(k * TILE, TILE), :], sems.at[1]
        ).start()
    pltpu.make_async_copy(trailing.at[pl.ds(0, active.shape[0]), :], active, sems.at[1]).wait()


def load(tile_list, trailing):
    rows = tile_list.shape[0] * TILE
    columns = trailing.shape[1]
    return call(
        load_kernel, pltpu.VMEM((rows, columns), BF16), [HBM, HBM], VMEM, 8,
        moved=2 * rows * columns,
        scratch=(pltpu.SMEM(tile_list.shape, jnp.int32), pltpu.SemaphoreType.DMA((2,))),
    )(stay(tile_list), trailing)


def gram_kernel(place, *refs):
    *blocks, full, keep, send = refs
    z, core = place[0], place[1]
    wide = blocks[0].shape[0]
    for s, block in enumerate(blocks):
        full[pl.ds(pl.multiple_of((z ^ s) * wide, wide), wide), :] = block[...]
    half = keep.shape[0]
    everything = full[...]
    mine = full[pl.ds(pl.multiple_of(core * half, half), half), :]
    theirs = full[pl.ds(pl.multiple_of((1 - core) * half, half), half), :]
    send[...] = dot(theirs, everything, ((1,), (1,)))
    keep[...] = dot(mine, everything, ((1,), (1,)))


def gram(place, blocks):
    wide, rows = blocks[0].shape
    width = len(blocks) * wide
    half = shape((width // 2, width), F32)
    return call(
        gram_kernel, (shape((width, rows), BF16), half, half),
        [SMEM] + [VMEM] * len(blocks), (VMEM, VMEM, VMEM), 16,
        flops=2 * width * width * rows, moved=4 * width * rows,
    )(place, *blocks)


def turn_kernel(full, out):
    step = 2 * TILE
    for k in range(full.shape[1] // step):
        out[k * step : (k + 1) * step, :] = full[:, k * step : (k + 1) * step].astype(F32).T.astype(BF16)


def turn(full):
    width, rows = full.shape
    return call(turn_kernel, shape((rows, width), BF16), [VMEM], VMEM, 16, moved=4 * width * rows)(full)


def pair_lhs(place, sources, lhs):
    odd = lax.rem(place[0], 2)
    for k, source in enumerate(sources):
        deep = source.shape[0]
        lhs[pl.ds(pl.multiple_of((odd ^ k) * deep, deep), deep), :] = source[...]


def rest_lhs(place, sources, lhs):
    (full,) = sources
    pair = lax.div(place[0], 2)
    across = full.shape[0] - lhs.shape[0]
    for k in range(lhs.shape[0] // across):
        q = k + (k >= pair).astype(jnp.int32)
        lhs[k * across : (k + 1) * across, :] = full[pl.ds(pl.multiple_of(q * across, across), across), :]


def cross_kernel(prepare, steps, mine, place, *refs):
    *sources, active, out, lhs = refs
    side = place[1] if mine else 1 - place[1]
    wide = out.shape[1] // steps
    prepare(place, sources, lhs)

    def body(i, _):
        source = pl.ds(pl.multiple_of(side * out.shape[1] + i * wide, wide), wide)
        where = pl.ds(pl.multiple_of(i * wide, wide), wide)
        out[:, where] = dot(lhs[...], active[:, source], ((1,), (0,))).astype(out.dtype)
        return 0

    lax.fori_loop(0, steps, body, 0)


def cross(prepare, mine, deep, place, sources, active):
    rows, columns = active.shape
    return call(
        functools.partial(cross_kernel, prepare, 4, mine),
        shape((deep, columns // 2), F32 if mine else BF16), [SMEM] + [VMEM] * (len(sources) + 1), VMEM, 8,
        flops=deep * rows * columns, moved=rows * columns,
        scratch=(pltpu.VMEM((deep, rows), BF16),),
    )(place, *sources, active)


def share_kernel(place, keep, got, own, *outs):
    chip = place[2]
    wide = own.shape[1]

    def total(where):
        return keep[:, where] + got[:, where].astype(F32)

    own[...] = total(pl.ds(pl.multiple_of(chip * wide, wide), wide))
    for s, out in enumerate(outs, 1):
        out[...] = total(pl.ds(pl.multiple_of((chip ^ s) * wide, wide), wide)).astype(BF16)


def share(place, keep, got, chips):
    deep, columns = keep.shape
    wide = columns // chips
    return call(
        share_kernel, [shape((deep, wide), F32)] + [shape((deep, wide), BF16)] * (chips - 1),
        [SMEM, VMEM, VMEM], [VMEM] * chips, 8, moved=8 * deep * columns,
    )(place, keep, got)


def swap(value, bit, rows):
    return lax.ppermute(value, "row", [(i, i ^ bit) for i in range(rows)])


def tree(values):
    values = [v.astype(F32) for v in values]
    while len(values) > 1:
        values = [a + b for a, b in zip(values[::2], values[1::2])]
    return values[0]


def reduce_cross(place, keep, got, rows):
    chips = rows // 2
    own, *outs = share(place, keep, got, chips)
    parts = [own] + [swap(v, 2 * s, rows) for s, v in enumerate(outs, 1)]
    mine = tree(parts).astype(BF16)
    stack = jnp.stack([mine] + [swap(mine, 2 * s, rows) for s in range(1, chips)])
    return stack, swap(stack, 1, rows)


def reduce_gram(keep, send, rows):
    own = keep + swap(send, 1, rows)
    total = tree([own] + [swap(own, 2 * s, rows) for s in range(1, rows // 2)])
    return total, swap(total, 1, rows)


def spread(value, r):
    return jnp.broadcast_to(value[r : r + 1, :], (8, 128))


def eliminate(value, size):
    sub = lax.broadcasted_iota(jnp.int32, (8, 128), 0)
    lanes = range(value.shape[1] // 128)
    count = size // 8
    span = min(BAND, count)
    x = [[value[8 * q : 8 * q + 8, 128 * n : 128 * n + 128] for n in lanes] for q in range(count)]
    done = []
    for begin in range(0, count, span):
        end = begin + span
        band = []
        for t in range(begin, end):
            group, at = divmod(8 * t, 128)
            lead = [
                [jnp.broadcast_to(x[q][group][:, at + c : at + c + 1], (8, 128)) for c in range(8)]
                for q in range(t, end)
            ]
            out = [jnp.zeros((8, 128), F32) for _ in lanes]
            for r in range(8):
                root = lax.rsqrt(spread(lead[0][r], r))
                inverse = root * root
                rows = [spread(x[t][n], r) for n in lanes]
                out = [jnp.where(sub == r, v * root, o) for v, o in zip(rows, out)]
                rows = [v * inverse for v in rows]
                later = [spread(lead[0][c], r) * inverse for c in range(r + 1, 8)]
                for k, q in enumerate(range(t, end)):
                    column = lead[k][r]
                    if k == 0:
                        column = jnp.where(sub > r, column, 0.0)
                    for c in range(r + 1, 8):
                        lead[k][c] = lead[k][c] - column * later[c - r - 1]
                    x[q] = [a - column * v for a, v in zip(x[q], rows)]
            band.append(jnp.concatenate(out, 1))
        band = jnp.concatenate(band, 0)
        done.append(band)
        if end < count:
            change = exact(band[:, :size], band, ((0,), (0,)))
            for q in range(end, count):
                x[q] = [x[q][n] - change[8 * q : 8 * q + 8, 128 * n : 128 * n + 128] for n in lanes]
    return jnp.concatenate(done, 0)


def factor_first_kernel(place, mine, theirs, first, rest, whole):
    core = place[1]
    h = mine.shape[0]
    whole[pl.ds(pl.multiple_of(core * h, h), h), :] = mine[...]
    whole[pl.ds(pl.multiple_of((1 - core) * h, h), h), :] = theirs[...]
    line = lax.broadcasted_iota(jnp.int32, (h, h), 0)
    lane = lax.broadcasted_iota(jnp.int32, (h, h), 1)
    eye = (line == lane).astype(F32)
    value = eliminate(jnp.concatenate([whole[:h, :], eye], 1), h)
    first[...] = value
    r12 = value[:, h : 2 * h]
    rest[...] = whole[h:, h:] - exact(r12, r12, ((0,), (0,)))


def factor_last_kernel(first, rest, triangle, inverse, turned):
    h = first.shape[0]
    line = lax.broadcasted_iota(jnp.int32, (h, h), 0)
    lane = lax.broadcasted_iota(jnp.int32, (h, h), 1)
    eye = (line == lane).astype(F32)
    zero = jnp.zeros((h, h), F32)
    second = eliminate(jnp.concatenate([rest[...], eye], 1), h)
    r11, r12, i11 = first[:, :h], first[:, h : 2 * h], first[:, 2 * h :]
    r22, i22 = second[:, :h], second[:, h:]
    i11 = jnp.where(lane <= line, i11, 0.0)
    i22 = jnp.where(lane <= line, i22, 0.0)
    i21 = -exact(i22, exact(r12, i11, ((0,), (0,))), ((1,), (0,)))
    triangle[:h, :h] = jnp.where(lane >= line, r11, 0.0)
    triangle[:h, h:] = r12
    triangle[h:, :h] = zero
    triangle[h:, h:] = jnp.where(lane >= line, r22, 0.0)
    full = jnp.concatenate([jnp.concatenate([i11, zero], 1), jnp.concatenate([i21, i22], 1)], 0)
    inverse[0], inverse[1] = split(full)
    turned[0], turned[1] = split(full.T)


def factor_first(place, mine, theirs):
    h, size = mine.shape
    return call(
        factor_first_kernel, (shape((h, 3 * h), F32), shape((h, h), F32)), [SMEM, VMEM, VMEM],
        (VMEM,) * 2, 8, flops=10 * size**3, moved=20 * MIB, scratch=(pltpu.VMEM((size, size), F32),),
    )(place, mine, theirs)


def factor_last(first, rest):
    size = 2 * first.shape[0]
    both = shape((2, size, size), BF16)
    return call(
        factor_last_kernel, (shape((size, size), F32), both, both), [VMEM, VMEM], (VMEM,) * 3, 8,
        flops=10 * size**3, moved=20 * MIB,
    )(first, rest)


def update_kernel(
    chips, place, inverse, turned, panel, near_one, far_one, near_two, far_two, active,
    top_out, out, sums, tops, results, top_sems, out_sems,
):
    core, chip = place[1], place[2]
    pair = lax.div(place[0], 2)
    rows, wide = results.shape[1:]
    steps = 2 * chips
    two = near_one.shape[1]
    rest = near_two.shape[1] // two
    block = rows // 4
    straight = ((1,), (0,))

    def where(i):
        side = core if i < chips else 1 - core
        return pl.ds(pl.multiple_of((side * chips + (chip ^ (i % chips))) * wide, wide), wide)

    def top_copy(i):
        return pltpu.make_async_copy(tops.at[i % 2], top_out.at[where(i), :], top_sems.at[i % 2])

    def out_copy(i):
        return pltpu.make_async_copy(results.at[i % 2], out.at[:, where(i)], out_sems.at[i % 2])

    def prepare(i):
        one, several = (near_one, near_two) if i < chips else (far_one, far_two)
        s = i % chips
        sums[i % 2, pl.ds(pl.multiple_of(pair * two, two), two), :] = one[s]
        for k in range(rest):
            q = k + (k >= pair).astype(jnp.int32)
            sums[i % 2, pl.ds(pl.multiple_of(q * two, two), two), :] = several[s, k * two : (k + 1) * two, :]
        cross = sums[i % 2]
        top = dot(inverse[0], cross, straight) + dot(inverse[1], cross, straight)
        high, low = split(top)
        tops[i % 2] = top.T
        return (
            dot(turned[0], high, straight) + (dot(turned[0], low, straight) + dot(turned[1], high, straight))
        ).astype(BF16)

    coeff = prepare(0)
    top_copy(0).start()
    for i in range(steps):
        if i >= 2:
            out_copy(i - 2).wait()
        if 1 <= i < steps - 1:
            top_copy(i - 1).wait()
        now = coeff
        if i + 1 < steps:
            coeff = prepare(i + 1)
        for k in range(0, rows, block):
            product = dot(panel[k : k + block, :], now, straight)
            results[i % 2, k : k + block, :] = (active[k : k + block, where(i)].astype(F32) - product).astype(BF16)
        if i + 1 < steps:
            top_copy(i + 1).start()
        out_copy(i).start()
    for i in (steps - 2, steps - 1):
        top_copy(i).wait()
        out_copy(i).wait()


def update(place, inverse, turned, panel, one, two, active, chips):
    rows, size = panel.shape
    columns = active.shape[1]
    wide = columns // (2 * chips)
    return call(
        functools.partial(update_kernel, chips),
        (shape((columns, size), F32), shape((rows, columns), BF16)),
        [SMEM] + [VMEM] * 8, (ANY, ANY), 12,
        flops=2 * rows * size * columns, moved=2 * rows * columns,
        scratch=(
            pltpu.VMEM((2, size, wide), BF16),
            pltpu.VMEM((2, wide, size), F32),
            pltpu.VMEM((2, rows, wide), BF16),
            pltpu.SemaphoreType.DMA((2,)),
            pltpu.SemaphoreType.DMA((2,)),
        ),
    )(place, inverse, turned, panel, *one, *two, active)


def local(nrow, ncol, panel, trailing, tile_list):
    row = lax.axis_index("row")
    place = jnp.stack([lax.axis_index("col"), row % 2, row // 2]).astype(jnp.int32)
    own = pick(tile_list, panel.T)
    blocks = [own]
    for s in range(1, ncol):
        blocks.append(lax.ppermute(own, "col", [(i, i ^ s) for i in range(ncol)]))
    across = 2 * panel.shape[1]
    active = load(tile_list, trailing)

    def both(prepare, deep, sources):
        send = swap(cross(prepare, False, deep, place, sources, active), 1, nrow)
        keep = cross(prepare, True, deep, place, sources, active)
        return reduce_cross(place, keep, send, nrow)

    one = both(pair_lhs, across, blocks[:2])
    full, keep, send = gram(place, blocks)
    sums = reduce_gram(keep, send, nrow)
    turned_panel = turn(full)
    two = both(rest_lhs, (ncol - 2) * panel.shape[1], [full])
    triangle, inverse, turned = factor_last(*factor_first(place, *sums))
    top_rows, updated = update(place, inverse, turned, turned_panel, one, two, active, nrow // 2)
    return triangle, top_rows, updated


def solution(mesh):
    nrow, ncol = mesh.shape["row"], mesh.shape["col"]

    def program(panel, trailing, tile_list):
        return local(nrow, ncol, panel, trailing, tile_list)

    return jax.shard_map(
        program,
        mesh=mesh,
        in_specs=(P("row", "col"), P("row", "col"), P("row")),
        out_specs=(P(), P("col", None), P("row", "col")),
        check_vma=False,
    )
```

time: 122 us -> 111 us (0.910)
  waiting for transfers between devices: 34.3 us -> 18 us
  local copies, waits for them, and re-layouts: 2.3 us -> 15.8 us
  Pallas kernels: 57.6 us -> 49.6 us
    ppermute x3, waiting for transfers between devices: 21.5 us -> 4.17 us  [local(): blocks.append(lax.ppermute(own, 'col', [(i, i ^ s) for i in range(ncol)]))]
    unnamed x6, local copies, waits for them, and re-layouts: 2.3 us -> 15.8 us
    pallas_call x1, Pallas kernels: 11.6 us -> 5.14 us  [factor_last(): call(factor_last_kernel, (shape((size, size), F32), both, both), [VMEM, V...]
    pallas_call x1, Pallas kernels: 11.5 us -> 5.34 us  [factor_first(): call(factor_first_kernel, (shape((h, 3 * h), F32), shape((h, h), F32)), [...]
    pallas_call x4 -> x6, Pallas kernels: 15.6 us -> 21.1 us  [the longest x4 11.7 us: cross(): call(functools.partial(cross_kernel, prepare, 4, mine), shape((deep, colu...]
  transfers between devices with their start and end apart: 24 -> 24, of which waited for: 12 -> 7; matrix products, arithmetic and copies ran while one was open for 0% -> 0% of each run, Pallas kernels for 30% -> 31%
where the time goes in v3:
time: 111 us
  Pallas kernels  49.6 us (45%)
  starting transfers between devices  26.1 us (24%)
  waiting for transfers between devices  18 us (16%)
  local copies, waits for them, and re-layouts  15.8 us (14%)
    ppermute x21, starting transfers between devices, swap(): return lax.ppermute(value, 'row', [(i, i ^ bit) for i in range(rows)])  20.3 us
    unnamed x6, local copies, waits for them, and re-layouts  15.8 us
    pallas_call x1, Pallas kernels, update(): call(functools.partial(update_kernel, chips), (shape((columns, size), F32...  14.7 us
    ppermute x21, waiting for transfers between devices, swap(): return lax.ppermute(value, 'row', [(i, i ^ bit) for i in range(rows)])  13.9 us
    pallas_call x4, Pallas kernels, cross(): call(functools.partial(cross_kernel, prepare, 4, mine), shape((deep, colu...  11.7 us
    pallas_call x1, Pallas kernels, load(): call(load_kernel, pltpu.VMEM((rows, columns), BF16), [HBM, HBM], VMEM, 8,...  8.26 us
    ppermute x3, starting transfers between devices, local(): blocks.append(lax.ppermute(own, 'col', [(i, i ^ s) for i in range(ncol)]))  5.71 us
    pallas_call x1, Pallas kernels, factor_first(): call(factor_first_kernel, (shape((h, 3 * h), F32), shape((h, h), F32)), [...  5.34 us
  transfers between devices with their start and end apart: 24, of which 7 were waited for; matrix products, arithmetic and copies ran while one was open for 0% of the time, Pallas kernels for 31%

profile of v3, /device:TPU:0, one launch (start us, length us, event | category | flops | bytes accessed | tf_op | source)
XLA Modules:
  0.0 110.9 jit_solution(8398689045885120631)
XLA Ops:
  1.7 3.1 %collective-permute-start = (bf16[64,2816]{1,0:T(8,128)(2,1)S(1)}, bf16[64,2816]{1,0:T(8,128)(2,1)S(1)}, u32[]{:S(2)}, u32[]{:S(2)}) collective-permute-start(bf16[64,2816]{1,0:T(8,128)(2,1)S(1)} %shard_map.58.refs_0_), channel_id=1, source_target_pairs={{0,1},{1,0},{2,3},{3,2},{4,5},{5,4},{6,7},{7,6},{8,9},{9,8},{10,11... | collective-permute-start | bytes 1081352 | tf_op jit(solution)/shard_map/ppermute | solution.py:409
  4.9 2.5 %collective-permute-start.2 = (bf16[64,2816]{1,0:T(8,128)(2,1)S(1)}, bf16[64,2816]{1,0:T(8,128)(2,1)S(1)}, u32[]{:S(2)}, u32[]{:S(2)}) collective-permute-start(bf16[64,2816]{1,0:T(8,128)(2,1)S(1)} %shard_map.58.refs_0_), channel_id=1, source_target_pairs={{0,3},{1,2},{2,1},{3,0},{4,7},{5,6},{6,5},{7,4},{8,11},{9,10},{10,... | collective-permute-start | bytes 1081352 | tf_op jit(solution)/shard_map/ppermute | solution.py:409
  7.5 8.3 %shard_map.63.refs_2_.refs_1_.active = bf16[2816,4096]{1,0:T(8,128)(2,1)S(1)} custom-call(s32[22]{0:T(128)} %listed.3, bf16[3072,4096]{1,0:T(8,128)(2,1)} %trailing.1), custom_call_target="tpu_custom_call" | custom-call | bytes 23068672 | tf_op jit(solution)/shard_map/pallas_call | solution.py:97
  15.7 8.2 %copy-done = bf16[2816,4096]{1,0:T(8,128)(2,1)} copy-done((bf16[2816,4096]{1,0:T(8,128)(2,1)}, bf16[2816,4096]{1,0:T(8,128)(2,1)S(1)}, u32[]{:S(2)}) %copy-start) | copy-done | bytes 23068696
  24.0 7.6 %copy-done.1 = bf16[2816,4096]{1,0:T(8,128)(2,1)S(1)} copy-done((bf16[2816,4096]{1,0:T(8,128)(2,1)S(1)}, bf16[2816,4096]{1,0:T(8,128)(2,1)}, u32[]{:S(2)}) %copy-start.1) | copy-done | bytes 23068696
  31.6 2.9 %shard_map.65 = bf16[128,2048]{1,0:T(8,128)(2,1)S(1)} custom-call(s32[3]{0:T(128)S(1)} %pad_add_fusion.place, bf16[64,2816]{1,0:T(8,128)(2,1)S(1)} %shard_map.58.refs_0_, bf16[64,2816]{1,0:T(8,128)(2,1)S(1)} %collective-permute-done.refs_1_, bf16[2816,4096]{1,0:T(8,128)(2,1)S(1)} %copy-done.1), custom_call_target="tpu_custom_call" | custom-call | flops 1476395008 | bytes 11534336 | tf_op jit(solution)/shard_map/pallas_call | solution.py:173
  34.6 4.2 %collective-permute-done.1.refs_2_ = bf16[64,2816]{1,0:T(8,128)(2,1)S(1)} collective-permute-done((bf16[64,2816]{1,0:T(8,128)(2,1)S(1)}, bf16[64,2816]{1,0:T(8,128)(2,1)S(1)}, u32[]{:S(2)}, u32[]{:S(2)}) %collective-permute-start.1) | collective-permute-done | bytes 360480 | tf_op jit(solution)/shard_map/ppermute | solution.py:409
  38.8 1.7 %shard_map.59 = (bf16[256,2816]{1,0:T(8,128)(2,1)S(1)}, f32[128,256]{1,0:T(8,128)S(1)}, f32[128,256]{1,0:T(8,128)S(1)}) custom-call(s32[3]{0:T(128)S(1)} %pad_add_fusion.place, bf16[64,2816]{1,0:T(8,128)(2,1)S(1)} %shard_map.58.refs_0_, bf16[64,2816]{1,0:T(8,128)(2,1)S(1)} %collective-permute-done.refs_1_, ...), custom_call_target="tpu_custom_call" | custom-call | flops 369098752 | bytes 2883584 | tf_op jit(solution)/shard_map/pallas_call | solution.py:122
  40.4 2.9 %shard_map.68 = bf16[128,2048]{1,0:T(8,128)(2,1)S(1)} custom-call(s32[3]{0:T(128)S(1)} %pad_add_fusion.place, bf16[256,2816]{1,0:T(8,128)(2,1)S(1)} %get-tuple-element.28.full.refs_0_, bf16[2816,4096]{1,0:T(8,128)(2,1)S(1)} %copy-done.2), custom_call_target="tpu_custom_call" | custom-call | flops 1476395008 | bytes 11534336 | tf_op jit(solution)/shard_map/pallas_call | solution.py:173
  43.9 2.9 %shard_map.64.keep = f32[128,2048]{1,0:T(8,128)S(1)} custom-call(s32[3]{0:T(128)S(1)} %pad_add_fusion.place, bf16[64,2816]{1,0:T(8,128)(2,1)S(1)} %shard_map.58.refs_0_, bf16[64,2816]{1,0:T(8,128)(2,1)S(1)} %collective-permute-done.refs_1_, bf16[2816,4096]{1,0:T(8,128)(2,1)S(1)} %copy-done.2), custom_call_target="tpu_custom_call" | custom-call | flops 1476395008 | bytes 11534336 | tf_op jit(solution)/shard_map/pallas_call | solution.py:173
  47.5 1.6 %collective-permute-start.9 = (bf16[128,512]{1,0:T(8,128)(2,1)S(1)}, bf16[128,512]{1,0:T(8,128)(2,1)S(1)}, u32[]{:S(2)}, u32[]{:S(2)}) collective-permute-start(bf16[128,512]{1,0:T(8,128)(2,1)S(1)} %get-tuple-element.30), channel_id=1, source_target_pairs={{0,8},{4,12},{8,0},{12,4},{16,24},{20,28},{24,16},{28,20},{1,9},{5... | collective-permute-start | bytes 393224 | tf_op jit(solution)/shard_map/ppermute | solution.py:203
  51.0 3.1 %shard_map.67.keep = f32[128,2048]{1,0:T(8,128)S(1)} custom-call(s32[3]{0:T(128)S(1)} %pad_add_fusion.place, bf16[256,2816]{1,0:T(8,128)(2,1)S(1)} %get-tuple-element.28.full.refs_0_, bf16[2816,4096]{1,0:T(8,128)(2,1)S(1)} %copy-done.2), custom_call_target="tpu_custom_call" | custom-call | flops 1476395008 | bytes 11534336 | tf_op jit(solution)/shard_map/pallas_call | solution.py:173
  54.7 1.5 %collective-permute-start.17 = (bf16[128,512]{1,0:T(8,128)(2,1)S(1)}, bf16[128,512]{1,0:T(8,128)(2,1)S(1)}, u32[]{:S(2)}, u32[]{:S(2)}) collective-permute-start(bf16[128,512]{1,0:T(8,128)(2,1)S(1)} %get-tuple-element.34), channel_id=1, source_target_pairs={{0,8},{4,12},{8,0},{12,4},{16,24},{20,28},{24,16},{28,20},{1,9},{5... | collective-permute-start | bytes 393224 | tf_op jit(solution)/shard_map/ppermute | solution.py:203
  56.3 1.5 %collective-permute-start.18 = (bf16[128,512]{1,0:T(8,128)(2,1)S(1)}, bf16[128,512]{1,0:T(8,128)(2,1)S(1)}, u32[]{:S(2)}, u32[]{:S(2)}) collective-permute-start(bf16[128,512]{1,0:T(8,128)(2,1)S(1)} %get-tuple-element.35), channel_id=1, source_target_pairs={{0,16},{4,20},{8,24},{12,28},{16,0},{20,4},{24,8},{28,12},{1,17},{... | collective-permute-start | bytes 393224 | tf_op jit(solution)/shard_map/ppermute | solution.py:203
  58.6 2.3 %collective-permute-start.14 = (bf16[128,512]{1,0:T(8,128)(2,1)S(1)}, bf16[128,512]{1,0:T(8,128)(2,1)S(1)}, u32[]{:S(2)}, u32[]{:S(2)}) collective-permute-start(bf16[128,512]{1,0:T(8,128)(2,1)S(1)} %add_convert_fusion.1), channel_id=1, source_target_pairs={{0,24},{4,28},{8,16},{12,20},{16,8},{20,12},{24,0},{28,4},{1,25},{... | collective-permute-start | bytes 393224 | tf_op jit(solution)/shard_map/ppermute | solution.py:203
  61.9 6.5 %collective-permute-done.18 = bf16[128,512]{1,0:T(8,128)(2,1)S(1)} collective-permute-done((bf16[128,512]{1,0:T(8,128)(2,1)S(1)}, bf16[128,512]{1,0:T(8,128)(2,1)S(1)}, u32[]{:S(2)}, u32[]{:S(2)}) %collective-permute-start.18) | collective-permute-done | bytes 131104 | tf_op jit(solution)/shard_map/ppermute | solution.py:203
  68.5 4.0 %collective-permute-start.22 = (bf16[128,512]{1,0:T(8,128)(2,1)S(1)}, bf16[128,512]{1,0:T(8,128)(2,1)S(1)}, u32[]{:S(2)}, u32[]{:S(2)}) collective-permute-start(bf16[128,512]{1,0:T(8,128)(2,1)S(1)} %add_convert_fusion), channel_id=1, source_target_pairs={{0,24},{4,28},{8,16},{12,20},{16,8},{20,12},{24,0},{28,4},{1,25},{... | collective-permute-start | bytes 393224 | tf_op jit(solution)/shard_map/ppermute | solution.py:203
  73.2 2.9 %collective-permute-start.6 = (f32[128,256]{1,0:T(8,128)S(1)}, f32[128,256]{1,0:T(8,128)S(1)}, u32[]{:S(2)}, u32[]{:S(2)}) collective-permute-start(f32[128,256]{1,0:T(8,128)S(1)} %add.36), channel_id=1, source_target_pairs={{0,24},{4,28},{8,16},{12,20},{16,8},{20,12},{24,0},{28,4},{1,25},{... | collective-permute-start | bytes 393224 | tf_op jit(solution)/shard_map/ppermute | solution.py:203
  77.0 2.2 %collective-permute-done.22 = bf16[128,512]{1,0:T(8,128)(2,1)S(1)} collective-permute-done((bf16[128,512]{1,0:T(8,128)(2,1)S(1)}, bf16[128,512]{1,0:T(8,128)(2,1)S(1)}, u32[]{:S(2)}, u32[]{:S(2)}) %collective-permute-start.22) | collective-permute-done | bytes 131104 | tf_op jit(solution)/shard_map/ppermute | solution.py:203
  80.0 2.4 %collective-permute-done.6 = f32[128,256]{1,0:T(8,128)S(1)} collective-permute-done((f32[128,256]{1,0:T(8,128)S(1)}, f32[128,256]{1,0:T(8,128)S(1)}, u32[]{:S(2)}, u32[]{:S(2)}) %collective-permute-start.6) | collective-permute-done | bytes 131104 | tf_op jit(solution)/shard_map/ppermute | solution.py:203
  82.5 1.7 %collective-permute-done.4 = f32[128,256]{1,0:T(8,128)S(1)} collective-permute-done((f32[128,256]{1,0:T(8,128)S(1)}, f32[128,256]{1,0:T(8,128)S(1)}, u32[]{:S(2)}, u32[]{:S(2)}) %collective-permute-start.4) | collective-permute-done | bytes 131104 | tf_op jit(solution)/shard_map/ppermute | solution.py:203
  85.6 5.3 %shard_map.60 = (f32[128,384]{1,0:T(8,128)S(1)}, f32[128,128]{1,0:T(8,128)S(1)}) custom-call(s32[3]{0:T(128)S(1)} %pad_add_fusion.place, f32[128,256]{1,0:T(8,128)S(1)} %add_add_fusion.mine, f32[128,256]{1,0:T(8,128)S(1)} %collective-permute-done.7.theirs), custom_call_target="tpu_custom_call" | custom-call | flops 167772160 | bytes 20971520 | tf_op jit(solution)/shard_map/pallas_call | solution.py:310
  90.9 5.1 %shard_map.61 = (f32[256,256]{1,0:T(8,128)}, bf16[2,256,256]{2,1,0:T(8,128)(2,1)S(1)}, bf16[2,256,256]{2,1,0:T(8,128)(2,1)S(1)}) custom-call(f32[128,384]{1,0:T(8,128)S(1)} %get-tuple-element.23.first, f32[128,128]{1,0:T(8,128)S(1)} %get-tuple-element.24.rest), custom_call_target="tpu_custom_call" | custom-call | flops 167772160 | bytes 20971520 | tf_op jit(solution)/shard_map/pallas_call | solution.py:319
  96.1 14.7 %shard_map.70 = (f32[4096,256]{1,0:T(8,128)}, bf16[2816,4096]{1,0:T(8,128)(2,1)}) custom-call(s32[3]{0:T(128)S(1)} %pad_add_fusion.place, bf16[2,256,256]{2,1,0:T(8,128)(2,1)S(1)} %get-tuple-element.26.inverse, bf16[2,256,256]{2,1,0:T(8,128)(2,1)S(1)} %get-tuple-element.27.turned, bf16[2816,256]{1,0:T(8,128)(2,1)S(1)} %shard_map.62.panel, ...), custom_call_target="tpu_custom_call" | custom-call | flops 5905580032 | bytes 23068672 | tf_op jit(solution)/shard_map/pallas_call | solution.py:388
  (50 shorter events, 11.1 us)
Async XLA Ops:
  1.7 22.3 %collective-permute-start = (bf16[64,2816]{1,0:T(8,128)(2,1)S(1)}, bf16[64,2816]{1,0:T(8,128)(2,1)S(1)}, u32[]{:S(2)}, u32[]{:S(2)}) collective-permute-start(bf16[64,2816]{1,0:T(8,128)(2,1)S(1)} %shard_map.58.refs_0_), channel_id=1, source_target_pairs={{0,1},{1,0},{2,3},{3,2},{4,5},{5,4},{6,7},{7,6},{8,9},{9,8},{10,11... | collective-permute-start | bytes 1081352 | tf_op jit(solution)/shard_map/ppermute | solution.py:409
  4.9 29.7 %collective-permute-start.2 = (bf16[64,2816]{1,0:T(8,128)(2,1)S(1)}, bf16[64,2816]{1,0:T(8,128)(2,1)S(1)}, u32[]{:S(2)}, u32[]{:S(2)}) collective-permute-start(bf16[64,2816]{1,0:T(8,128)(2,1)S(1)} %shard_map.58.refs_0_), channel_id=1, source_target_pairs={{0,3},{1,2},{2,1},{3,0},{4,7},{5,6},{6,5},{7,4},{8,11},{9,10},{10,... | collective-permute-start | bytes 1081352 | tf_op jit(solution)/shard_map/ppermute | solution.py:409
  7.3 31.4 %collective-permute-start.1 = (bf16[64,2816]{1,0:T(8,128)(2,1)S(1)}, bf16[64,2816]{1,0:T(8,128)(2,1)S(1)}, u32[]{:S(2)}, u32[]{:S(2)}) collective-permute-start(bf16[64,2816]{1,0:T(8,128)(2,1)S(1)} %shard_map.58.refs_0_), channel_id=1, source_target_pairs={{0,2},{1,3},{2,0},{3,1},{4,6},{5,7},{6,4},{7,5},{8,10},{9,11},{10,... | collective-permute-start | bytes 1081352 | tf_op jit(solution)/shard_map/ppermute | solution.py:409
  34.5 12.3 %collective-permute-start.8 = (bf16[128,2048]{1,0:T(8,128)(2,1)S(1)}, bf16[128,2048]{1,0:T(8,128)(2,1)S(1)}, u32[]{:S(2)}, u32[]{:S(2)}) collective-permute-start(bf16[128,2048]{1,0:T(8,128)(2,1)S(1)} %shard_map.65), channel_id=1, source_target_pairs={{0,4},{4,0},{8,12},{12,8},{16,20},{20,16},{24,28},{28,24},{1,5},{5... | collective-permute-start | bytes 1572872 | tf_op jit(solution)/shard_map/ppermute | solution.py:203
  43.3 10.8 %collective-permute-start.16 = (bf16[128,2048]{1,0:T(8,128)(2,1)S(1)}, bf16[128,2048]{1,0:T(8,128)(2,1)S(1)}, u32[]{:S(2)}, u32[]{:S(2)}) collective-permute-start(bf16[128,2048]{1,0:T(8,128)(2,1)S(1)} %shard_map.68), channel_id=1, source_target_pairs={{0,4},{4,0},{8,12},{12,8},{16,20},{20,16},{24,28},{28,24},{1,5},{5... | collective-permute-start | bytes 1572872 | tf_op jit(solution)/shard_map/ppermute | solution.py:203
  43.4 29.1 %collective-permute-start.3 = (f32[128,256]{1,0:T(8,128)S(1)}, f32[128,256]{1,0:T(8,128)S(1)}, u32[]{:S(2)}, u32[]{:S(2)}) collective-permute-start(f32[128,256]{1,0:T(8,128)S(1)} %get-tuple-element.22), channel_id=1, source_target_pairs={{0,4},{4,0},{8,12},{12,8},{16,20},{20,16},{24,28},{28,24},{1,5},{5... | collective-permute-start | bytes 393224 | tf_op jit(solution)/shard_map/ppermute | solution.py:203
  47.5 8.8 %collective-permute-start.9 = (bf16[128,512]{1,0:T(8,128)(2,1)S(1)}, bf16[128,512]{1,0:T(8,128)(2,1)S(1)}, u32[]{:S(2)}, u32[]{:S(2)}) collective-permute-start(bf16[128,512]{1,0:T(8,128)(2,1)S(1)} %get-tuple-element.30), channel_id=1, source_target_pairs={{0,8},{4,12},{8,0},{12,4},{16,24},{20,28},{24,16},{28,20},{1,9},{5... | collective-permute-start | bytes 393224 | tf_op jit(solution)/shard_map/ppermute | solution.py:203
  49.0 8.8 %collective-permute-start.10 = (bf16[128,512]{1,0:T(8,128)(2,1)S(1)}, bf16[128,512]{1,0:T(8,128)(2,1)S(1)}, u32[]{:S(2)}, u32[]{:S(2)}) collective-permute-start(bf16[128,512]{1,0:T(8,128)(2,1)S(1)} %get-tuple-element.31), channel_id=1, source_target_pairs={{0,16},{4,20},{8,24},{12,28},{16,0},{20,4},{24,8},{28,12},{1,17},{... | collective-permute-start | bytes 393224 | tf_op jit(solution)/shard_map/ppermute | solution.py:203
  50.6 7.9 %collective-permute-start.11 = (bf16[128,512]{1,0:T(8,128)(2,1)S(1)}, bf16[128,512]{1,0:T(8,128)(2,1)S(1)}, u32[]{:S(2)}, u32[]{:S(2)}) collective-permute-start(bf16[128,512]{1,0:T(8,128)(2,1)S(1)} %get-tuple-element.32), channel_id=1, source_target_pairs={{0,24},{4,28},{8,16},{12,20},{16,8},{20,12},{24,0},{28,4},{1,25},{... | collective-permute-start | bytes 393224 | tf_op jit(solution)/shard_map/ppermute | solution.py:203
  54.7 6.1 %collective-permute-start.17 = (bf16[128,512]{1,0:T(8,128)(2,1)S(1)}, bf16[128,512]{1,0:T(8,128)(2,1)S(1)}, u32[]{:S(2)}, u32[]{:S(2)}) collective-permute-start(bf16[128,512]{1,0:T(8,128)(2,1)S(1)} %get-tuple-element.34), channel_id=1, source_target_pairs={{0,8},{4,12},{8,0},{12,4},{16,24},{20,28},{24,16},{28,20},{1,9},{5... | collective-permute-start | bytes 393224 | tf_op jit(solution)/shard_map/ppermute | solution.py:203
  56.3 12.1 %collective-permute-start.18 = (bf16[128,512]{1,0:T(8,128)(2,1)S(1)}, bf16[128,512]{1,0:T(8,128)(2,1)S(1)}, u32[]{:S(2)}, u32[]{:S(2)}) collective-permute-start(bf16[128,512]{1,0:T(8,128)(2,1)S(1)} %get-tuple-element.35), channel_id=1, source_target_pairs={{0,16},{4,20},{8,24},{12,28},{16,0},{20,4},{24,8},{28,12},{1,17},{... | collective-permute-start | bytes 393224 | tf_op jit(solution)/shard_map/ppermute | solution.py:203
  57.8 10.6 %collective-permute-start.19 = (bf16[128,512]{1,0:T(8,128)(2,1)S(1)}, bf16[128,512]{1,0:T(8,128)(2,1)S(1)}, u32[]{:S(2)}, u32[]{:S(2)}) collective-permute-start(bf16[128,512]{1,0:T(8,128)(2,1)S(1)} %get-tuple-element.36), channel_id=1, source_target_pairs={{0,24},{4,28},{8,16},{12,20},{16,8},{20,12},{24,0},{28,4},{1,25},{... | collective-permute-start | bytes 393224 | tf_op jit(solution)/shard_map/ppermute | solution.py:203
  58.6 13.9 %collective-permute-start.14 = (bf16[128,512]{1,0:T(8,128)(2,1)S(1)}, bf16[128,512]{1,0:T(8,128)(2,1)S(1)}, u32[]{:S(2)}, u32[]{:S(2)}) collective-permute-start(bf16[128,512]{1,0:T(8,128)(2,1)S(1)} %add_convert_fusion.1), channel_id=1, source_target_pairs={{0,24},{4,28},{8,16},{12,20},{16,8},{20,12},{24,0},{28,4},{1,25},{... | collective-permute-start | bytes 393224 | tf_op jit(solution)/shard_map/ppermute | solution.py:203
  60.9 12.3 %collective-permute-start.13 = (bf16[128,512]{1,0:T(8,128)(2,1)S(1)}, bf16[128,512]{1,0:T(8,128)(2,1)S(1)}, u32[]{:S(2)}, u32[]{:S(2)}) collective-permute-start(bf16[128,512]{1,0:T(8,128)(2,1)S(1)} %add_convert_fusion.1), channel_id=1, source_target_pairs={{0,16},{4,20},{8,24},{12,28},{16,0},{20,4},{24,8},{28,12},{1,17},{... | collective-permute-start | bytes 393224 | tf_op jit(solution)/shard_map/ppermute | solution.py:203
  68.4 7.7 %collective-permute-start.12 = (bf16[128,512]{1,0:T(8,128)(2,1)S(1)}, bf16[128,512]{1,0:T(8,128)(2,1)S(1)}, u32[]{:S(2)}, u32[]{:S(2)}) collective-permute-start(bf16[128,512]{1,0:T(8,128)(2,1)S(1)} %add_convert_fusion.1), channel_id=1, source_target_pairs={{0,8},{4,12},{8,0},{12,4},{16,24},{20,28},{24,16},{28,20},{1,9},{5... | collective-permute-start | bytes 393224 | tf_op jit(solution)/shard_map/ppermute | solution.py:203
  68.5 10.7 %collective-permute-start.22 = (bf16[128,512]{1,0:T(8,128)(2,1)S(1)}, bf16[128,512]{1,0:T(8,128)(2,1)S(1)}, u32[]{:S(2)}, u32[]{:S(2)}) collective-permute-start(bf16[128,512]{1,0:T(8,128)(2,1)S(1)} %add_convert_fusion), channel_id=1, source_target_pairs={{0,24},{4,28},{8,16},{12,20},{16,8},{20,12},{24,0},{28,4},{1,25},{... | collective-permute-start | bytes 393224 | tf_op jit(solution)/shard_map/ppermute | solution.py:203
  72.5 6.9 %collective-permute-start.21 = (bf16[128,512]{1,0:T(8,128)(2,1)S(1)}, bf16[128,512]{1,0:T(8,128)(2,1)S(1)}, u32[]{:S(2)}, u32[]{:S(2)}) collective-permute-start(bf16[128,512]{1,0:T(8,128)(2,1)S(1)} %add_convert_fusion), channel_id=1, source_target_pairs={{0,16},{4,20},{8,24},{12,28},{16,0},{20,4},{24,8},{28,12},{1,17},{... | collective-permute-start | bytes 393224 | tf_op jit(solution)/shard_map/ppermute | solution.py:203
  72.5 6.9 %collective-permute-start.20 = (bf16[128,512]{1,0:T(8,128)(2,1)S(1)}, bf16[128,512]{1,0:T(8,128)(2,1)S(1)}, u32[]{:S(2)}, u32[]{:S(2)}) collective-permute-start(bf16[128,512]{1,0:T(8,128)(2,1)S(1)} %add_convert_fusion), channel_id=1, source_target_pairs={{0,8},{4,12},{8,0},{12,4},{16,24},{20,28},{24,16},{28,20},{1,9},{5... | collective-permute-start | bytes 393224 | tf_op jit(solution)/shard_map/ppermute | solution.py:203
  73.2 9.2 %collective-permute-start.6 = (f32[128,256]{1,0:T(8,128)S(1)}, f32[128,256]{1,0:T(8,128)S(1)}, u32[]{:S(2)}, u32[]{:S(2)}) collective-permute-start(f32[128,256]{1,0:T(8,128)S(1)} %add.36), channel_id=1, source_target_pairs={{0,24},{4,28},{8,16},{12,20},{16,8},{20,12},{24,0},{28,4},{1,25},{... | collective-permute-start | bytes 393224 | tf_op jit(solution)/shard_map/ppermute | solution.py:203
  76.1 6.4 %collective-permute-start.5 = (f32[128,256]{1,0:T(8,128)S(1)}, f32[128,256]{1,0:T(8,128)S(1)}, u32[]{:S(2)}, u32[]{:S(2)}) collective-permute-start(f32[128,256]{1,0:T(8,128)S(1)} %add.36), channel_id=1, source_target_pairs={{0,16},{4,20},{8,24},{12,28},{16,0},{20,4},{24,8},{28,12},{1,17},{... | collective-permute-start | bytes 393224 | tf_op jit(solution)/shard_map/ppermute | solution.py:203
  79.2 5.0 %collective-permute-start.4 = (f32[128,256]{1,0:T(8,128)S(1)}, f32[128,256]{1,0:T(8,128)S(1)}, u32[]{:S(2)}, u32[]{:S(2)}) collective-permute-start(f32[128,256]{1,0:T(8,128)S(1)} %add.36), channel_id=1, source_target_pairs={{0,8},{4,12},{8,0},{12,4},{16,24},{20,28},{24,16},{28,20},{1,9},{5... | collective-permute-start | bytes 393224 | tf_op jit(solution)/shard_map/ppermute | solution.py:203
  79.4 16.7 %collective-permute-start.15 = (bf16[4,128,512]{2,1,0:T(8,128)(2,1)S(1)}, bf16[4,128,512]{2,1,0:T(8,128)(2,1)S(1)}, u32[]{:S(2)}, u32[]{:S(2)}) collective-permute-start(bf16[4,128,512]{2,1,0:T(8,128)(2,1)S(1)} %pad_maximum_fusion.near_one), channel_id=1, source_target_pairs={{0,4},{4,0},{8,12},{12,8},{16,20},{20,16},{24,28},{28,24},{1,5},{5... | collective-permute-start | bytes 1572872 | tf_op jit(solution)/shard_map/ppermute | solution.py:203
  79.5 16.6 %collective-permute-start.23 = (bf16[4,128,512]{2,1,0:T(8,128)(2,1)S(1)}, bf16[4,128,512]{2,1,0:T(8,128)(2,1)S(1)}, u32[]{:S(2)}, u32[]{:S(2)}) collective-permute-start(bf16[4,128,512]{2,1,0:T(8,128)(2,1)S(1)} %pad_maximum_fusion.1.near_two), channel_id=1, source_target_pairs={{0,4},{4,0},{8,12},{12,8},{16,20},{20,16},{24,28},{28,24},{1,5},{5... | collective-permute-start | bytes 1572872 | tf_op jit(solution)/shard_map/ppermute | solution.py:203
  84.2 1.4 %collective-permute-start.7 = (f32[128,256]{1,0:T(8,128)S(1)}, f32[128,256]{1,0:T(8,128)S(1)}, u32[]{:S(2)}, u32[]{:S(2)}) collective-permute-start(f32[128,256]{1,0:T(8,128)S(1)} %add_add_fusion.mine), channel_id=1, source_target_pairs={{0,4},{4,0},{8,12},{12,8},{16,20},{20,16},{24,28},{28,24},{1,5},{5... | collective-permute-start | bytes 393224 | tf_op jit(solution)/shard_map/ppermute | solution.py:203
  (3 other events, 24.6 us)

commit v4 on v3

--- a/solution.py
+++ b/solution.py
@@ -21,13 +21,14 @@
     return jax.ShapeDtypeStruct(dims, kind)
 
 
-def call(body, out_shape, in_specs, out_specs, grant, flops=0, moved=0, scratch=()):
+def call(body, out_shape, in_specs, out_specs, grant, flops=0, moved=0, scratch=(), aliases=None):
     return pl.pallas_call(
         body,
         out_shape=out_shape,
         in_specs=in_specs,
         out_specs=out_specs,
         scratch_shapes=list(scratch),
+        input_output_aliases=aliases or {},
         cost_estimate=pl.CostEstimate(flops=flops, bytes_accessed=moved, transcendentals=0),
         compiler_params=pltpu.CompilerParams(vmem_limit_bytes=grant * MIB),
     )
@@ -101,10 +102,23 @@
     )(stay(tile_list), trailing)
 
 
-def gram_kernel(place, *refs):
+def gram_kernel(relayed, place, *refs):
     *blocks, full, keep, send = refs
     z, core = place[0], place[1]
     wide = blocks[0].shape[0]
+    if relayed:
+        *blocks, inner, outer = blocks
+        where = pl.ds(pl.multiple_of((z ^ len(blocks)) * wide, wide), wide)
+        middle = jnp.logical_or(z == 1, z == 2)
+
+        @pl.when(middle)
+        def _():
+            full[where, :] = inner[...]
+
+        @pl.when(jnp.logical_not(middle))
+        def _():
+            full[where, :] = outer[...]
+
     for s, block in enumerate(blocks):
         full[pl.ds(pl.multiple_of((z ^ s) * wide, wide), wide), :] = block[...]
     half = keep.shape[0]
@@ -115,12 +129,12 @@
     keep[...] = dot(mine, everything, ((1,), (1,)))
 
 
-def gram(place, blocks):
+def gram(place, blocks, parts):
     wide, rows = blocks[0].shape
-    width = len(blocks) * wide
+    width = parts * wide
     half = shape((width // 2, width), F32)
     return call(
-        gram_kernel, (shape((width, rows), BF16), half, half),
+        functools.partial(gram_kernel, len(blocks) > parts), (shape((width, rows), BF16), half, half),
         [SMEM] + [VMEM] * len(blocks), (VMEM, VMEM, VMEM), 16,
         flops=2 * width * width * rows, moved=4 * width * rows,
     )(place, *blocks)
@@ -210,18 +224,33 @@
     return values[0]
 
 
+def bits_of(rows):
+    return [1 << k for k in range(1, rows.bit_length() - 1)]
+
+
 def reduce_cross(place, keep, got, rows):
     chips = rows // 2
     own, *outs = share(place, keep, got, chips)
     parts = [own] + [swap(v, 2 * s, rows) for s, v in enumerate(outs, 1)]
-    mine = tree(parts).astype(BF16)
-    stack = jnp.stack([mine] + [swap(mine, 2 * s, rows) for s in range(1, chips)])
-    return stack, swap(stack, 1, rows)
+    return tree(parts).astype(BF16)
+
+
+def gather_slow(mine, rows):
+    stack = mine[None]
+    for bit in bits_of(rows):
+        other = swap(stack, bit, rows)
+        stack = jnp.concatenate([stack, other], 0)
+    return stack
+
+
+def gather_fast(mine, rows):
+    return [mine] + [swap(mine, 2 * s, rows) for s in range(1, rows // 2)]
 
 
 def reduce_gram(keep, send, rows):
     own = keep + swap(send, 1, rows)
-    total = tree([own] + [swap(own, 2 * s, rows) for s in range(1, rows // 2)])
+    parts = [own] + [swap(own, 2 * s, rows) for s in range(1, rows // 2)]
+    total = tree(parts)
     return total, swap(total, 1, rows)
 
 
@@ -322,91 +351,106 @@
     )(first, rest)
 
 
-def update_kernel(
-    chips, place, inverse, turned, panel, near_one, far_one, near_two, far_two, active,
-    top_out, out, sums, tops, results, top_sems, out_sems,
-):
-    core, chip = place[1], place[2]
+def coeff_kernel(place, inverse, turned, one, *refs):
+    *several, top_out, coeff_out, sums = refs
     pair = lax.div(place[0], 2)
-    rows, wide = results.shape[1:]
-    steps = 2 * chips
-    two = near_one.shape[1]
-    rest = near_two.shape[1] // two
-    block = rows // 4
+    two, wide = one.shape[1:]
     straight = ((1,), (0,))
-
-    def where(i):
-        side = core if i < chips else 1 - core
-        return pl.ds(pl.multiple_of((side * chips + (chip ^ (i % chips))) * wide, wide), wide)
-
-    def top_copy(i):
-        return pltpu.make_async_copy(tops.at[i % 2], top_out.at[where(i), :], top_sems.at[i % 2])
-
-    def out_copy(i):
-        return pltpu.make_async_copy(results.at[i % 2], out.at[:, where(i)], out_sems.at[i % 2])
-
-    def prepare(i):
-        one, several = (near_one, near_two) if i < chips else (far_one, far_two)
-        s = i % chips
-        sums[i % 2, pl.ds(pl.multiple_of(pair * two, two), two), :] = one[s]
-        for k in range(rest):
+    for s, other in enumerate(several):
+        sums[s % 2, pl.ds(pl.multiple_of(pair * two, two), two), :] = one[s]
+        for k in range(other.shape[0] // two):
             q = k + (k >= pair).astype(jnp.int32)
-            sums[i % 2, pl.ds(pl.multiple_of(q * two, two), two), :] = several[s, k * two : (k + 1) * two, :]
-        cross = sums[i % 2]
+            sums[s % 2, pl.ds(pl.multiple_of(q * two, two), two), :] = other[k * two : (k + 1) * two, :]
+        cross = sums[s % 2]
         top = dot(inverse[0], cross, straight) + dot(inverse[1], cross, straight)
         high, low = split(top)
-        tops[i % 2] = top.T
-        return (
+        part = slice(s * wide, (s + 1) * wide)
+        top_out[part, :] = top.T
+        coeff_out[:, part] = (
             dot(turned[0], high, straight) + (dot(turned[0], low, straight) + dot(turned[1], high, straight))
         ).astype(BF16)
 
-    coeff = prepare(0)
-    top_copy(0).start()
-    for i in range(steps):
-        if i >= 2:
-            out_copy(i - 2).wait()
-        if 1 <= i < steps - 1:
-            top_copy(i - 1).wait()
-        now = coeff
-        if i + 1 < steps:
-            coeff = prepare(i + 1)
+
+def coefficients(place, inverse, turned, one, several):
+    size = inverse.shape[1]
+    wide = one.shape[2]
+    half = wide * len(several)
+    return call(
+        coeff_kernel, (shape((half, size), F32), shape((size, half), BF16)),
+        [SMEM] + [VMEM] * (3 + len(several)), (VMEM, VMEM), 12,
+        flops=10 * size * size * half, moved=8 * size * half, scratch=(pltpu.VMEM((2, size, wide), BF16),),
+    )(place, inverse, turned, one, *several)
+
+
+def update_kernel(chips, mine, place, panel, coeff, top, active, *refs):
+    top_out, out, results, top_sem, out_sems = refs[-5:]
+    chip = place[2]
+    side = place[1] if mine else 1 - place[1]
+    rows, wide = results.shape[1:]
+    block = rows // 4
+
+    def where(s):
+        return pl.ds(pl.multiple_of((side * chips + (chip ^ s)) * wide, wide), wide)
+
+    def top_copy(s):
+        return pltpu.make_async_copy(top.at[pl.ds(s * wide, wide), :], top_out.at[where(s), :], top_sem)
+
+    def out_copy(s, part):
+        return pltpu.make_async_copy(results.at[s % 2, part, :], out.at[part, where(s)], out_sems.at[s % 2])
+
+    for s in range(chips):
+        top_copy(s).start()
+    for s in range(chips):
+        if s >= 2:
+            out_copy(s - 2, pl.ds(0, rows)).wait()
+        weights = coeff[:, s * wide : (s + 1) * wide]
         for k in range(0, rows, block):
-            product = dot(panel[k : k + block, :], now, straight)
-            results[i % 2, k : k + block, :] = (active[k : k + block, where(i)].astype(F32) - product).astype(BF16)
-        if i + 1 < steps:
-            top_copy(i + 1).start()
-        out_copy(i).start()
-    for i in (steps - 2, steps - 1):
-        top_copy(i).wait()
-        out_copy(i).wait()
-
-
-def update(place, inverse, turned, panel, one, two, active, chips):
+            product = dot(panel[k : k + block, :], weights, ((1,), (0,)))
+            results[s % 2, k : k + block, :] = (active[k : k + block, where(s)].astype(F32) - product).astype(BF16)
+            out_copy(s, pl.ds(k, block)).start()
+    for s in range(max(chips - 2, 0), chips):
+        out_copy(s, pl.ds(0, rows)).wait()
+    half = chips * wide
+    pltpu.make_async_copy(top, top_out.at[pl.ds(0, half), :], top_sem).wait()
+
+
+def update(mine, chips, place, panel, coeff, top, active, before=()):
     rows, size = panel.shape
     columns = active.shape[1]
     wide = columns // (2 * chips)
     return call(
-        functools.partial(update_kernel, chips),
+        functools.partial(update_kernel, chips, mine),
         (shape((columns, size), F32), shape((rows, columns), BF16)),
-        [SMEM] + [VMEM] * 8, (ANY, ANY), 12,
-        flops=2 * rows * size * columns, moved=2 * rows * columns,
+        [SMEM] + [VMEM] * 4 + [ANY] * len(before), (ANY, ANY), 12,
+        flops=rows * size * columns, moved=rows * columns,
         scratch=(
-            pltpu.VMEM((2, size, wide), BF16),
-            pltpu.VMEM((2, wide, size), F32),
             pltpu.VMEM((2, rows, wide), BF16),
-            pltpu.SemaphoreType.DMA((2,)),
+            pltpu.SemaphoreType.DMA(()),
             pltpu.SemaphoreType.DMA((2,)),
         ),
-    )(place, inverse, turned, panel, *one, *two, active)
+        aliases={5: 0, 6: 1} if before else None,
+    )(place, panel, coeff, top, active, *before)
+
+
+def gather_panel(own, ncol):
+    def shift(value, pairs):
+        return lax.ppermute(value, "col", pairs)
+
+    def direct(s):
+        return shift(own, [(i, i ^ s) for i in range(ncol)])
+
+    if ncol != 4:
+        return [own] + [direct(s) for s in range(1, ncol)]
+    across = direct(2)
+    return [own, direct(1), across, shift(own, [(1, 2), (2, 1)]), shift(across, [(2, 3), (1, 0)])]
 
 
 def local(nrow, ncol, panel, trailing, tile_list):
     row = lax.axis_index("row")
     place = jnp.stack([lax.axis_index("col"), row % 2, row // 2]).astype(jnp.int32)
+    chips = nrow // 2
     own = pick(tile_list, panel.T)
-    blocks = [own]
-    for s in range(1, ncol):
-        blocks.append(lax.ppermute(own, "col", [(i, i ^ s) for i in range(ncol)]))
+    blocks = gather_panel(own, ncol)
     across = 2 * panel.shape[1]
     active = load(tile_list, trailing)
 
@@ -415,13 +459,16 @@
         keep = cross(prepare, True, deep, place, sources, active)
         return reduce_cross(place, keep, send, nrow)
 
-    one = both(pair_lhs, across, blocks[:2])
-    full, keep, send = gram(place, blocks)
+    one = gather_slow(both(pair_lhs, across, blocks[:2]), nrow)
+    full, keep, send = gram(place, blocks, ncol)
     sums = reduce_gram(keep, send, nrow)
     turned_panel = turn(full)
-    two = both(rest_lhs, (ncol - 2) * panel.shape[1], [full])
+    two = gather_fast(both(rest_lhs, (ncol - 2) * panel.shape[1], [full]), nrow)
     triangle, inverse, turned = factor_last(*factor_first(place, *sums))
-    top_rows, updated = update(place, inverse, turned, turned_panel, one, two, active, nrow // 2)
+    top, coeff = coefficients(place, inverse, turned, one, two)
+    outs = update(True, chips, place, turned_panel, coeff, top, active)
+    coeff, top = swap(coeff, 1, nrow), swap(top, 1, nrow)
+    top_rows, updated = update(False, chips, place, turned_panel, coeff, top, active, outs)
     return triangle, top_rows, updated
 
 

time: 111 us -> 99.2 us (0.89)
  the two profiles are of different devices: /device:TPU:0 before, /device:TPU:17 now
where the time goes in v4:
time: 99.2 us; the launch traced here: 98.9 us
  Pallas kernels  49.7 us (50%)
  starting transfers between devices  29.4 us (30%)
  waiting for transfers between devices  18.3 us (18%)
  between operations  1.06 us (1%)
    ppermute x20, starting transfers between devices, swap(): return lax.ppermute(value, 'row', [(i, i ^ bit) for i in range(rows)])  17.9 us
    pallas_call x2, Pallas kernels, update(): call(functools.partial(update_kernel, chips, mine), (shape((columns, size...  12 us
    pallas_call x4, Pallas kernels, cross(): call(functools.partial(cross_kernel, prepare, 4, mine), shape((deep, colu...  11.7 us
    ppermute x4, starting transfers between devices, shift(): return lax.ppermute(value, 'col', pairs)  11.5 us
    ppermute x4, waiting for transfers between devices, shift(): return lax.ppermute(value, 'col', pairs)  10.6 us
    pallas_call x1, Pallas kernels, load(): call(load_kernel, pltpu.VMEM((rows, columns), BF16), [HBM, HBM], VMEM, 8,...  8.27 us
    ppermute x20, waiting for transfers between devices, swap(): return lax.ppermute(value, 'row', [(i, i ^ bit) for i in range(rows)])  7.75 us
    pallas_call x1, Pallas kernels, factor_first(): call(factor_first_kernel, (shape((h, 3 * h), F32), shape((h, h), F32)), [...  5.35 us
  transfers between devices with their start and end apart: 24, of which 5 were waited for; matrix products, arithmetic and copies ran while one was open for 0% of the time, Pallas kernels for 40%

profile of v4, /device:TPU:17, one launch (start us, length us, event | category | flops | bytes accessed | tf_op | source)
XLA Modules:
  0.0 98.9 jit_solution(6125938455541188035)
XLA Ops:
  1.8 1.4 %collective-permute-start = (bf16[64,2816]{1,0:T(8,128)(2,1)S(1)}, bf16[64,2816]{1,0:T(8,128)(2,1)S(1)}, u32[]{:S(2)}, u32[]{:S(2)}) collective-permute-start(bf16[64,2816]{1,0:T(8,128)(2,1)S(1)} %shard_map.58.refs_0_), channel_id=1, source_target_pairs={{0,1},{1,0},{2,3},{3,2},{4,5},{5,4},{6,7},{7,6},{8,9},{9,8},{10,11... | collective-permute-start | bytes 1081352 | tf_op jit(solution)/shard_map/ppermute | solution.py:437
  3.2 3.2 %collective-permute-start.2 = (bf16[64,2816]{1,0:T(8,128)(2,1)S(1)}, bf16[64,2816]{1,0:T(8,128)(2,1)S(1)}, u32[]{:S(2)}, u32[]{:S(2)}) collective-permute-start(bf16[64,2816]{1,0:T(8,128)(2,1)S(1)} %shard_map.58.refs_0_), channel_id=1, source_target_pairs={{1,2},{2,1},{5,6},{6,5},{9,10},{10,9},{13,14},{14,13},{17,18},{18,... | collective-permute-start | bytes 1081352 | tf_op jit(solution)/shard_map/ppermute | solution.py:437
  6.4 10.6 %collective-permute-done.1.refs_2_ = bf16[64,2816]{1,0:T(8,128)(2,1)S(1)} collective-permute-done((bf16[64,2816]{1,0:T(8,128)(2,1)S(1)}, bf16[64,2816]{1,0:T(8,128)(2,1)S(1)}, u32[]{:S(2)}, u32[]{:S(2)}) %collective-permute-start.1) | collective-permute-done | bytes 360480 | tf_op jit(solution)/shard_map/ppermute | solution.py:437
  17.0 6.9 %collective-permute-start.3 = (bf16[64,2816]{1,0:T(8,128)(2,1)S(1)}, bf16[64,2816]{1,0:T(8,128)(2,1)S(1)}, u32[]{:S(2)}, u32[]{:S(2)}) collective-permute-start(bf16[64,2816]{1,0:T(8,128)(2,1)S(1)} %collective-permute-done.1.refs_2_), channel_id=1, source_target_pairs={{2,3},{1,0},{6,7},{5,4},{10,11},{9,8},{14,15},{13,12},{18,19},{17,... | collective-permute-start | bytes 1081352 | tf_op jit(solution)/shard_map/ppermute | solution.py:437
  24.0 8.3 %shard_map.63.refs_2_.refs_1_.active = bf16[2816,4096]{1,0:T(8,128)(2,1)S(1)} custom-call(s32[22]{0:T(128)} %listed.3, bf16[3072,4096]{1,0:T(8,128)(2,1)} %trailing.1), custom_call_target="tpu_custom_call" | custom-call | bytes 23068672 | tf_op jit(solution)/shard_map/pallas_call | solution.py:98
  32.2 2.9 %shard_map.65 = bf16[128,2048]{1,0:T(8,128)(2,1)S(1)} custom-call(s32[3]{0:T(128)S(1)} %pad_add_fusion.place, bf16[64,2816]{1,0:T(8,128)(2,1)S(1)} %shard_map.58.refs_0_, bf16[64,2816]{1,0:T(8,128)(2,1)S(1)} %collective-permute-done.refs_1_, bf16[2816,4096]{1,0:T(8,128)(2,1)S(1)} %shard_map.63.refs_2_.refs_1_.active), custom_call_target="tpu_custom_call" | custom-call | flops 1476395008 | bytes 11534336 | tf_op jit(solution)/shard_map/pallas_call | solution.py:187
  36.1 1.7 %shard_map.59 = (bf16[256,2816]{1,0:T(8,128)(2,1)S(1)}, f32[128,256]{1,0:T(8,128)S(1)}, f32[128,256]{1,0:T(8,128)S(1)}) custom-call(s32[3]{0:T(128)S(1)} %pad_add_fusion.place, bf16[64,2816]{1,0:T(8,128)(2,1)S(1)} %shard_map.58.refs_0_, bf16[64,2816]{1,0:T(8,128)(2,1)S(1)} %collective-permute-done.refs_1_, ...), custom_call_target="tpu_custom_call" | custom-call | flops 369098752 | bytes 2883584 | tf_op jit(solution)/shard_map/pallas_call | solution.py:136
  37.9 2.9 %shard_map.64.keep = f32[128,2048]{1,0:T(8,128)S(1)} custom-call(s32[3]{0:T(128)S(1)} %pad_add_fusion.place, bf16[64,2816]{1,0:T(8,128)(2,1)S(1)} %shard_map.58.refs_0_, bf16[64,2816]{1,0:T(8,128)(2,1)S(1)} %collective-permute-done.refs_1_, bf16[2816,4096]{1,0:T(8,128)(2,1)S(1)} %shard_map.63.refs_2_.refs_1_.active), custom_call_target="tpu_custom_call" | custom-call | flops 1476395008 | bytes 11534336 | tf_op jit(solution)/shard_map/pallas_call | solution.py:187
  40.8 2.2 %collective-permute-start.7 = (f32[128,256]{1,0:T(8,128)S(1)}, f32[128,256]{1,0:T(8,128)S(1)}, u32[]{:S(2)}, u32[]{:S(2)}) collective-permute-start(f32[128,256]{1,0:T(8,128)S(1)} %add.36), channel_id=1, source_target_pairs={{0,24},{4,28},{8,16},{12,20},{16,8},{20,12},{24,0},{28,4},{1,25},{... | collective-permute-start | bytes 393224 | tf_op jit(solution)/shard_map/ppermute | solution.py:217
  43.5 2.9 %shard_map.68 = bf16[128,2048]{1,0:T(8,128)(2,1)S(1)} custom-call(s32[3]{0:T(128)S(1)} %pad_add_fusion.place, bf16[256,2816]{1,0:T(8,128)(2,1)S(1)} %get-tuple-element.30.full.refs_0_, bf16[2816,4096]{1,0:T(8,128)(2,1)S(1)} %shard_map.63.refs_2_.refs_1_.active), custom_call_target="tpu_custom_call" | custom-call | flops 1476395008 | bytes 11534336 | tf_op jit(solution)/shard_map/pallas_call | solution.py:187
  46.4 1.4 %collective-permute-start.15 = (bf16[128,2048]{1,0:T(8,128)(2,1)S(1)}, bf16[128,2048]{1,0:T(8,128)(2,1)S(1)}, u32[]{:S(2)}, u32[]{:S(2)}) collective-permute-start(bf16[128,2048]{1,0:T(8,128)(2,1)S(1)} %shard_map.68), channel_id=1, source_target_pairs={{0,4},{4,0},{8,12},{12,8},{16,20},{20,16},{24,28},{28,24},{1,5},{5... | collective-permute-start | bytes 1572872 | tf_op jit(solution)/shard_map/ppermute | solution.py:217
  48.4 1.3 %collective-permute-start.10 = (bf16[128,512]{1,0:T(8,128)(2,1)S(1)}, bf16[128,512]{1,0:T(8,128)(2,1)S(1)}, u32[]{:S(2)}, u32[]{:S(2)}) collective-permute-start(bf16[128,512]{1,0:T(8,128)(2,1)S(1)} %get-tuple-element.34), channel_id=1, source_target_pairs={{0,8},{4,12},{8,0},{12,4},{16,24},{20,28},{24,16},{28,20},{1,9},{5... | collective-permute-start | bytes 393224 | tf_op jit(solution)/shard_map/ppermute | solution.py:217
  53.5 2.6 %collective-permute-done.11 = bf16[128,512]{1,0:T(8,128)(2,1)S(1)} collective-permute-done((bf16[128,512]{1,0:T(8,128)(2,1)S(1)}, bf16[128,512]{1,0:T(8,128)(2,1)S(1)}, u32[]{:S(2)}, u32[]{:S(2)}) %collective-permute-start.11) | collective-permute-done | bytes 131104 | tf_op jit(solution)/shard_map/ppermute | solution.py:217
  57.2 1.4 %collective-permute-start.13 = (bf16[1,128,512]{2,1,0:T(8,128)(2,1)S(1)}, bf16[1,128,512]{2,1,0:T(8,128)(2,1)S(1)}, u32[]{:S(2)}, u32[]{:S(2)}) collective-permute-start(bf16[1,128,512]{2,1,0:T(8,128)(2,1)S(1)} %fusion), channel_id=1, source_target_pairs={{0,8},{4,12},{8,0},{12,4},{16,24},{20,28},{24,16},{28,20},{1,9},{5... | collective-permute-start | bytes 393224 | tf_op jit(solution)/shard_map/ppermute | solution.py:217
  58.6 3.0 %shard_map.67.keep = f32[128,2048]{1,0:T(8,128)S(1)} custom-call(s32[3]{0:T(128)S(1)} %pad_add_fusion.place, bf16[256,2816]{1,0:T(8,128)(2,1)S(1)} %get-tuple-element.30.full.refs_0_, bf16[2816,4096]{1,0:T(8,128)(2,1)S(1)} %shard_map.63.refs_2_.refs_1_.active), custom_call_target="tpu_custom_call" | custom-call | flops 1476395008 | bytes 11534336 | tf_op jit(solution)/shard_map/pallas_call | solution.py:187
  62.5 1.3 %collective-permute-start.17 = (bf16[128,512]{1,0:T(8,128)(2,1)S(1)}, bf16[128,512]{1,0:T(8,128)(2,1)S(1)}, u32[]{:S(2)}, u32[]{:S(2)}) collective-permute-start(bf16[128,512]{1,0:T(8,128)(2,1)S(1)} %get-tuple-element.39), channel_id=1, source_target_pairs={{0,16},{4,20},{8,24},{12,28},{16,0},{20,4},{24,8},{28,12},{1,17},{... | collective-permute-start | bytes 393224 | tf_op jit(solution)/shard_map/ppermute | solution.py:217
  65.4 5.3 %shard_map.60 = (f32[128,384]{1,0:T(8,128)S(1)}, f32[128,128]{1,0:T(8,128)S(1)}) custom-call(s32[3]{0:T(128)S(1)} %pad_add_fusion.place, f32[128,256]{1,0:T(8,128)S(1)} %add_add_fusion.mine, f32[128,256]{1,0:T(8,128)S(1)} %collective-permute-done.8.theirs), custom_call_target="tpu_custom_call" | custom-call | flops 167772160 | bytes 20971520 | tf_op jit(solution)/shard_map/pallas_call | solution.py:339
  72.0 1.3 %collective-permute-start.20 = (bf16[128,512]{1,0:T(8,128)(2,1)S(1)}, bf16[128,512]{1,0:T(8,128)(2,1)S(1)}, u32[]{:S(2)}, u32[]{:S(2)}) collective-permute-start(bf16[128,512]{1,0:T(8,128)(2,1)S(1)} %add_convert_fusion.refs_0_), channel_id=1, source_target_pairs={{0,16},{4,20},{8,24},{12,28},{16,0},{20,4},{24,8},{28,12},{1,17},{... | collective-permute-start | bytes 393224 | tf_op jit(solution)/shard_map/ppermute | solution.py:217
  73.6 5.1 %shard_map.61 = (f32[256,256]{1,0:T(8,128)}, bf16[2,256,256]{2,1,0:T(8,128)(2,1)S(1)}, bf16[2,256,256]{2,1,0:T(8,128)(2,1)S(1)}) custom-call(f32[128,384]{1,0:T(8,128)S(1)} %get-tuple-element.27.first, f32[128,128]{1,0:T(8,128)S(1)} %get-tuple-element.28.rest), custom_call_target="tpu_custom_call" | custom-call | flops 167772160 | bytes 20971520 | tf_op jit(solution)/shard_map/pallas_call | solution.py:348
  78.8 2.9 %collective-permute-done.20.refs_2_ = bf16[128,512]{1,0:T(8,128)(2,1)S(1)} collective-permute-done((bf16[128,512]{1,0:T(8,128)(2,1)S(1)}, bf16[128,512]{1,0:T(8,128)(2,1)S(1)}, u32[]{:S(2)}, u32[]{:S(2)}) %collective-permute-start.20) | collective-permute-done | bytes 131104 | tf_op jit(solution)/shard_map/ppermute | solution.py:217
  81.7 2.6 %shard_map.70 = (f32[2048,256]{1,0:T(8,128)S(1)}, bf16[256,2048]{1,0:T(8,128)(2,1)S(1)}) custom-call(s32[3]{0:T(128)S(1)} %pad_add_fusion.place, bf16[2,256,256]{2,1,0:T(8,128)(2,1)S(1)} %get-tuple-element.31.inverse, bf16[2,256,256]{2,1,0:T(8,128)(2,1)S(1)} %get-tuple-element.32.turned, bf16[4,128,512]{2,1,0:T(8,128)(2,1)S(1)} %pad_maximum_fusion.one, ...), custom_call_target="tpu_custom_call" | custom-call | flops 1342177280 | bytes 4194304 | tf_op jit(solution)/shard_map/pallas_call | solution.py:378
  84.3 1.7 %collective-permute-start.23 = (f32[2048,256]{1,0:T(8,128)S(1)}, f32[2048,256]{1,0:T(8,128)S(1)}, u32[]{:S(2)}, u32[]{:S(2)}) collective-permute-start(f32[2048,256]{1,0:T(8,128)S(1)} %get-tuple-element.42.top), channel_id=1, source_target_pairs={{0,4},{4,0},{8,12},{12,8},{16,20},{20,16},{24,28},{28,24},{1,5},{5... | collective-permute-start | bytes 6291464 | tf_op jit(solution)/shard_map/ppermute | solution.py:217
  86.6 5.9 %shard_map.71 = (f32[4096,256]{1,0:T(8,128)}, bf16[2816,4096]{1,0:T(8,128)(2,1)}) custom-call(s32[3]{0:T(128)S(1)} %pad_add_fusion.place, bf16[2816,256]{1,0:T(8,128)(2,1)S(1)} %shard_map.62.panel, bf16[256,2048]{1,0:T(8,128)(2,1)S(1)} %get-tuple-element.41.coeff, f32[2048,256]{1,0:T(8,128)S(1)} %get-tuple-element.42.top, ...), custom_call_target="tpu_custom_call" | custom-call | flops 2952790016 | bytes 11534336 | tf_op jit(solution)/shard_map/pallas_call | solution.py:421
  92.6 6.1 %shard_map.72 = (f32[4096,256]{1,0:T(8,128)}, bf16[2816,4096]{1,0:T(8,128)(2,1)}) custom-call(s32[3]{0:T(128)S(1)} %pad_add_fusion.place, bf16[2816,256]{1,0:T(8,128)(2,1)S(1)} %shard_map.62.panel, bf16[256,2048]{1,0:T(8,128)(2,1)S(1)} %collective-permute-done.22.coeff, ...), custom_call_target="tpu_custom_call", output_to_operand_aliasing={{0}: (5, {}), {1}: (6, {})} | custom-call | flops 2952790016 | bytes 11534336 | tf_op jit(solution)/shard_map/pallas_call | solution.py:421
  (46 shorter events, 12.8 us)
Async XLA Ops:
  1.7 15.2 %collective-permute-start.1 = (bf16[64,2816]{1,0:T(8,128)(2,1)S(1)}, bf16[64,2816]{1,0:T(8,128)(2,1)S(1)}, u32[]{:S(2)}, u32[]{:S(2)}) collective-permute-start(bf16[64,2816]{1,0:T(8,128)(2,1)S(1)} %shard_map.58.refs_0_), channel_id=1, source_target_pairs={{0,2},{1,3},{2,0},{3,1},{4,6},{5,7},{6,4},{7,5},{8,10},{9,11},{10,... | collective-permute-start | bytes 1081352 | tf_op jit(solution)/shard_map/ppermute | solution.py:437
  1.8 30.4 %collective-permute-start = (bf16[64,2816]{1,0:T(8,128)(2,1)S(1)}, bf16[64,2816]{1,0:T(8,128)(2,1)S(1)}, u32[]{:S(2)}, u32[]{:S(2)}) collective-permute-start(bf16[64,2816]{1,0:T(8,128)(2,1)S(1)} %shard_map.58.refs_0_), channel_id=1, source_target_pairs={{0,1},{1,0},{2,3},{3,2},{4,5},{5,4},{6,7},{7,6},{8,9},{9,8},{10,11... | collective-permute-start | bytes 1081352 | tf_op jit(solution)/shard_map/ppermute | solution.py:437
  3.2 32.9 %collective-permute-start.2 = (bf16[64,2816]{1,0:T(8,128)(2,1)S(1)}, bf16[64,2816]{1,0:T(8,128)(2,1)S(1)}, u32[]{:S(2)}, u32[]{:S(2)}) collective-permute-start(bf16[64,2816]{1,0:T(8,128)(2,1)S(1)} %shard_map.58.refs_0_), channel_id=1, source_target_pairs={{1,2},{2,1},{5,6},{6,5},{9,10},{10,9},{13,14},{14,13},{17,18},{18,... | collective-permute-start | bytes 1081352 | tf_op jit(solution)/shard_map/ppermute | solution.py:437
  17.0 19.1 %collective-permute-start.3 = (bf16[64,2816]{1,0:T(8,128)(2,1)S(1)}, bf16[64,2816]{1,0:T(8,128)(2,1)S(1)}, u32[]{:S(2)}, u32[]{:S(2)}) collective-permute-start(bf16[64,2816]{1,0:T(8,128)(2,1)S(1)} %collective-permute-done.1.refs_2_), channel_id=1, source_target_pairs={{2,3},{1,0},{6,7},{5,4},{10,11},{9,8},{14,15},{13,12},{18,19},{17,... | collective-permute-start | bytes 1081352 | tf_op jit(solution)/shard_map/ppermute | solution.py:437
  35.1 12.6 %collective-permute-start.9 = (bf16[128,2048]{1,0:T(8,128)(2,1)S(1)}, bf16[128,2048]{1,0:T(8,128)(2,1)S(1)}, u32[]{:S(2)}, u32[]{:S(2)}) collective-permute-start(bf16[128,2048]{1,0:T(8,128)(2,1)S(1)} %shard_map.65), channel_id=1, source_target_pairs={{0,4},{4,0},{8,12},{12,8},{16,20},{20,16},{24,28},{28,24},{1,5},{5... | collective-permute-start | bytes 1572872 | tf_op jit(solution)/shard_map/ppermute | solution.py:217
  37.8 3.0 %collective-permute-start.4 = (f32[128,256]{1,0:T(8,128)S(1)}, f32[128,256]{1,0:T(8,128)S(1)}, u32[]{:S(2)}, u32[]{:S(2)}) collective-permute-start(f32[128,256]{1,0:T(8,128)S(1)} %get-tuple-element.26), channel_id=1, source_target_pairs={{0,4},{4,0},{8,12},{12,8},{16,20},{20,16},{24,28},{28,24},{1,5},{5... | collective-permute-start | bytes 393224 | tf_op jit(solution)/shard_map/ppermute | solution.py:217
  40.8 8.9 %collective-permute-start.7 = (f32[128,256]{1,0:T(8,128)S(1)}, f32[128,256]{1,0:T(8,128)S(1)}, u32[]{:S(2)}, u32[]{:S(2)}) collective-permute-start(f32[128,256]{1,0:T(8,128)S(1)} %add.36), channel_id=1, source_target_pairs={{0,24},{4,28},{8,16},{12,20},{16,8},{20,12},{24,0},{28,4},{1,25},{... | collective-permute-start | bytes 393224 | tf_op jit(solution)/shard_map/ppermute | solution.py:217
  43.0 7.9 %collective-permute-start.6 = (f32[128,256]{1,0:T(8,128)S(1)}, f32[128,256]{1,0:T(8,128)S(1)}, u32[]{:S(2)}, u32[]{:S(2)}) collective-permute-start(f32[128,256]{1,0:T(8,128)S(1)} %add.36), channel_id=1, source_target_pairs={{0,16},{4,20},{8,24},{12,28},{16,0},{20,4},{24,8},{28,12},{1,17},{... | collective-permute-start | bytes 393224 | tf_op jit(solution)/shard_map/ppermute | solution.py:217
  43.2 7.9 %collective-permute-start.5 = (f32[128,256]{1,0:T(8,128)S(1)}, f32[128,256]{1,0:T(8,128)S(1)}, u32[]{:S(2)}, u32[]{:S(2)}) collective-permute-start(f32[128,256]{1,0:T(8,128)S(1)} %add.36), channel_id=1, source_target_pairs={{0,8},{4,12},{8,0},{12,4},{16,24},{20,28},{24,16},{28,20},{1,9},{5... | collective-permute-start | bytes 393224 | tf_op jit(solution)/shard_map/ppermute | solution.py:217
  46.4 15.3 %collective-permute-start.15 = (bf16[128,2048]{1,0:T(8,128)(2,1)S(1)}, bf16[128,2048]{1,0:T(8,128)(2,1)S(1)}, u32[]{:S(2)}, u32[]{:S(2)}) collective-permute-start(bf16[128,2048]{1,0:T(8,128)(2,1)S(1)} %shard_map.68), channel_id=1, source_target_pairs={{0,4},{4,0},{8,12},{12,8},{16,20},{20,16},{24,28},{28,24},{1,5},{5... | collective-permute-start | bytes 1572872 | tf_op jit(solution)/shard_map/ppermute | solution.py:217
  48.4 5.1 %collective-permute-start.10 = (bf16[128,512]{1,0:T(8,128)(2,1)S(1)}, bf16[128,512]{1,0:T(8,128)(2,1)S(1)}, u32[]{:S(2)}, u32[]{:S(2)}) collective-permute-start(bf16[128,512]{1,0:T(8,128)(2,1)S(1)} %get-tuple-element.34), channel_id=1, source_target_pairs={{0,8},{4,12},{8,0},{12,4},{16,24},{20,28},{24,16},{28,20},{1,9},{5... | collective-permute-start | bytes 393224 | tf_op jit(solution)/shard_map/ppermute | solution.py:217
  49.7 6.5 %collective-permute-start.11 = (bf16[128,512]{1,0:T(8,128)(2,1)S(1)}, bf16[128,512]{1,0:T(8,128)(2,1)S(1)}, u32[]{:S(2)}, u32[]{:S(2)}) collective-permute-start(bf16[128,512]{1,0:T(8,128)(2,1)S(1)} %get-tuple-element.35), channel_id=1, source_target_pairs={{0,16},{4,20},{8,24},{12,28},{16,0},{20,4},{24,8},{28,12},{1,17},{... | collective-permute-start | bytes 393224 | tf_op jit(solution)/shard_map/ppermute | solution.py:217
  50.9 6.2 %collective-permute-start.12 = (bf16[128,512]{1,0:T(8,128)(2,1)S(1)}, bf16[128,512]{1,0:T(8,128)(2,1)S(1)}, u32[]{:S(2)}, u32[]{:S(2)}) collective-permute-start(bf16[128,512]{1,0:T(8,128)(2,1)S(1)} %get-tuple-element.36), channel_id=1, source_target_pairs={{0,24},{4,28},{8,16},{12,20},{16,8},{20,12},{24,0},{28,4},{1,25},{... | collective-permute-start | bytes 393224 | tf_op jit(solution)/shard_map/ppermute | solution.py:217
  51.2 14.3 %collective-permute-start.8 = (f32[128,256]{1,0:T(8,128)S(1)}, f32[128,256]{1,0:T(8,128)S(1)}, u32[]{:S(2)}, u32[]{:S(2)}) collective-permute-start(f32[128,256]{1,0:T(8,128)S(1)} %add_add_fusion.mine), channel_id=1, source_target_pairs={{0,4},{4,0},{8,12},{12,8},{16,20},{20,16},{24,28},{28,24},{1,5},{5... | collective-permute-start | bytes 393224 | tf_op jit(solution)/shard_map/ppermute | solution.py:217
  57.2 7.8 %collective-permute-start.13 = (bf16[1,128,512]{2,1,0:T(8,128)(2,1)S(1)}, bf16[1,128,512]{2,1,0:T(8,128)(2,1)S(1)}, u32[]{:S(2)}, u32[]{:S(2)}) collective-permute-start(bf16[1,128,512]{2,1,0:T(8,128)(2,1)S(1)} %fusion), channel_id=1, source_target_pairs={{0,8},{4,12},{8,0},{12,4},{16,24},{20,28},{24,16},{28,20},{1,9},{5... | collective-permute-start | bytes 393224 | tf_op jit(solution)/shard_map/ppermute | solution.py:217
  62.3 8.5 %collective-permute-start.16 = (bf16[128,512]{1,0:T(8,128)(2,1)S(1)}, bf16[128,512]{1,0:T(8,128)(2,1)S(1)}, u32[]{:S(2)}, u32[]{:S(2)}) collective-permute-start(bf16[128,512]{1,0:T(8,128)(2,1)S(1)} %get-tuple-element.38), channel_id=1, source_target_pairs={{0,8},{4,12},{8,0},{12,4},{16,24},{20,28},{24,16},{28,20},{1,9},{5... | collective-permute-start | bytes 393224 | tf_op jit(solution)/shard_map/ppermute | solution.py:217
  62.5 8.3 %collective-permute-start.17 = (bf16[128,512]{1,0:T(8,128)(2,1)S(1)}, bf16[128,512]{1,0:T(8,128)(2,1)S(1)}, u32[]{:S(2)}, u32[]{:S(2)}) collective-permute-start(bf16[128,512]{1,0:T(8,128)(2,1)S(1)} %get-tuple-element.39), channel_id=1, source_target_pairs={{0,16},{4,20},{8,24},{12,28},{16,0},{20,4},{24,8},{28,12},{1,17},{... | collective-permute-start | bytes 393224 | tf_op jit(solution)/shard_map/ppermute | solution.py:217
  63.9 6.9 %collective-permute-start.18 = (bf16[128,512]{1,0:T(8,128)(2,1)S(1)}, bf16[128,512]{1,0:T(8,128)(2,1)S(1)}, u32[]{:S(2)}, u32[]{:S(2)}) collective-permute-start(bf16[128,512]{1,0:T(8,128)(2,1)S(1)} %get-tuple-element.40), channel_id=1, source_target_pairs={{0,24},{4,28},{8,16},{12,20},{16,8},{20,12},{24,0},{28,4},{1,25},{... | collective-permute-start | bytes 393224 | tf_op jit(solution)/shard_map/ppermute | solution.py:217
  65.1 13.7 %collective-permute-start.14 = (bf16[2,128,512]{2,1,0:T(8,128)(2,1)S(1)}, bf16[2,128,512]{2,1,0:T(8,128)(2,1)S(1)}, u32[]{:S(2)}, u32[]{:S(2)}) collective-permute-start(bf16[2,128,512]{2,1,0:T(8,128)(2,1)S(1)} %pad_maximum_fusion.1), channel_id=1, source_target_pairs={{0,16},{4,20},{8,24},{12,28},{16,0},{20,4},{24,8},{28,12},{1,17},{... | collective-permute-start | bytes 786440 | tf_op jit(solution)/shard_map/ppermute | solution.py:217
  70.9 7.9 %collective-permute-start.21 = (bf16[128,512]{1,0:T(8,128)(2,1)S(1)}, bf16[128,512]{1,0:T(8,128)(2,1)S(1)}, u32[]{:S(2)}, u32[]{:S(2)}) collective-permute-start(bf16[128,512]{1,0:T(8,128)(2,1)S(1)} %add_convert_fusion.refs_0_), channel_id=1, source_target_pairs={{0,24},{4,28},{8,16},{12,20},{16,8},{20,12},{24,0},{28,4},{1,25},{... | collective-permute-start | bytes 393224 | tf_op jit(solution)/shard_map/ppermute | solution.py:217
  72.0 9.7 %collective-permute-start.20 = (bf16[128,512]{1,0:T(8,128)(2,1)S(1)}, bf16[128,512]{1,0:T(8,128)(2,1)S(1)}, u32[]{:S(2)}, u32[]{:S(2)}) collective-permute-start(bf16[128,512]{1,0:T(8,128)(2,1)S(1)} %add_convert_fusion.refs_0_), channel_id=1, source_target_pairs={{0,16},{4,20},{8,24},{12,28},{16,0},{20,4},{24,8},{28,12},{1,17},{... | collective-permute-start | bytes 393224 | tf_op jit(solution)/shard_map/ppermute | solution.py:217
  73.3 8.4 %collective-permute-start.19 = (bf16[128,512]{1,0:T(8,128)(2,1)S(1)}, bf16[128,512]{1,0:T(8,128)(2,1)S(1)}, u32[]{:S(2)}, u32[]{:S(2)}) collective-permute-start(bf16[128,512]{1,0:T(8,128)(2,1)S(1)} %add_convert_fusion.refs_0_), channel_id=1, source_target_pairs={{0,8},{4,12},{8,0},{12,4},{16,24},{20,28},{24,16},{28,20},{1,9},{5... | collective-permute-start | bytes 393224 | tf_op jit(solution)/shard_map/ppermute | solution.py:217
  84.3 8.2 %collective-permute-start.23 = (f32[2048,256]{1,0:T(8,128)S(1)}, f32[2048,256]{1,0:T(8,128)S(1)}, u32[]{:S(2)}, u32[]{:S(2)}) collective-permute-start(f32[2048,256]{1,0:T(8,128)S(1)} %get-tuple-element.42.top), channel_id=1, source_target_pairs={{0,4},{4,0},{8,12},{12,8},{16,20},{20,16},{24,28},{28,24},{1,5},{5... | collective-permute-start | bytes 6291464 | tf_op jit(solution)/shard_map/ppermute | solution.py:217
  86.1 6.5 %collective-permute-start.22 = (bf16[256,2048]{1,0:T(8,128)(2,1)S(1)}, bf16[256,2048]{1,0:T(8,128)(2,1)S(1)}, u32[]{:S(2)}, u32[]{:S(2)}) collective-permute-start(bf16[256,2048]{1,0:T(8,128)(2,1)S(1)} %get-tuple-element.41.coeff), channel_id=1, source_target_pairs={{0,4},{4,0},{8,12},{12,8},{16,20},{20,16},{24,28},{28,24},{1,5},{5... | collective-permute-start | bytes 3145736 | tf_op jit(solution)/shard_map/ppermute | solution.py:217

commit v5 on v4

--- a/solution.py
+++ b/solution.py
@@ -293,9 +293,10 @@
         band = jnp.concatenate(band, 0)
         done.append(band)
         if end < count:
-            change = exact(band[:, :size], band, ((0,), (0,)))
+            change = exact(band[:, :size].T[8 * end :, :], band, ((1,), (0,)))
             for q in range(end, count):
-                x[q] = [x[q][n] - change[8 * q : 8 * q + 8, 128 * n : 128 * n + 128] for n in lanes]
+                k = 8 * (q - end)
+                x[q] = [x[q][n] - change[k : k + 8, 128 * n : 128 * n + 128] for n in lanes]
     return jnp.concatenate(done, 0)
 
 

time: 99.2 us -> 99 us (level)
  no operation moved by 1% of the time
where the time goes in v5:
time: 99 us; the launch traced here: 98.6 us
  Pallas kernels  48.9 us (49%)
  starting transfers between devices  29.4 us (30%)
  waiting for transfers between devices  18.9 us (19%)
  between operations  1.04 us (1%)
    ppermute x20, starting transfers between devices, swap(): return lax.ppermute(value, 'row', [(i, i ^ bit) for i in range(rows)])  17.9 us
    pallas_call x2, Pallas kernels, update(): call(functools.partial(update_kernel, chips, mine), (shape((columns, size...  11.9 us
    pallas_call x4, Pallas kernels, cross(): call(functools.partial(cross_kernel, prepare, 4, mine), shape((deep, colu...  11.7 us
    ppermute x4, starting transfers between devices, shift(): return lax.ppermute(value, 'col', pairs)  11.5 us
    ppermute x4, waiting for transfers between devices, shift(): return lax.ppermute(value, 'col', pairs)  10.6 us
    ppermute x20, waiting for transfers between devices, swap(): return lax.ppermute(value, 'row', [(i, i ^ bit) for i in range(rows)])  8.29 us
    pallas_call x1, Pallas kernels, load(): call(load_kernel, pltpu.VMEM((rows, columns), BF16), [HBM, HBM], VMEM, 8,...  8.27 us
    pallas_call x1, Pallas kernels, factor_first(): call(factor_first_kernel, (shape((h, 3 * h), F32), shape((h, h), F32)), [...  5.06 us
  transfers between devices with their start and end apart: 24, of which 5 were waited for; matrix products, arithmetic and copies ran while one was open for 0% of the time, Pallas kernels for 40%

profile of v5, /device:TPU:17, one launch (start us, length us, event | category | flops | bytes accessed | tf_op | source)
XLA Modules:
  0.0 98.6 jit_solution(10410138436713391449)
XLA Ops:
  1.8 1.4 %collective-permute-start = (bf16[64,2816]{1,0:T(8,128)(2,1)S(1)}, bf16[64,2816]{1,0:T(8,128)(2,1)S(1)}, u32[]{:S(2)}, u32[]{:S(2)}) collective-permute-start(bf16[64,2816]{1,0:T(8,128)(2,1)S(1)} %shard_map.58.refs_0_), channel_id=1, source_target_pairs={{0,1},{1,0},{2,3},{3,2},{4,5},{5,4},{6,7},{7,6},{8,9},{9,8},{10,11... | collective-permute-start | bytes 1081352 | tf_op jit(solution)/shard_map/ppermute | solution.py:438
  3.2 3.2 %collective-permute-start.2 = (bf16[64,2816]{1,0:T(8,128)(2,1)S(1)}, bf16[64,2816]{1,0:T(8,128)(2,1)S(1)}, u32[]{:S(2)}, u32[]{:S(2)}) collective-permute-start(bf16[64,2816]{1,0:T(8,128)(2,1)S(1)} %shard_map.58.refs_0_), channel_id=1, source_target_pairs={{1,2},{2,1},{5,6},{6,5},{9,10},{10,9},{13,14},{14,13},{17,18},{18,... | collective-permute-start | bytes 1081352 | tf_op jit(solution)/shard_map/ppermute | solution.py:438
  6.4 10.6 %collective-permute-done.1.refs_2_ = bf16[64,2816]{1,0:T(8,128)(2,1)S(1)} collective-permute-done((bf16[64,2816]{1,0:T(8,128)(2,1)S(1)}, bf16[64,2816]{1,0:T(8,128)(2,1)S(1)}, u32[]{:S(2)}, u32[]{:S(2)}) %collective-permute-start.1) | collective-permute-done | bytes 360480 | tf_op jit(solution)/shard_map/ppermute | solution.py:438
  17.0 6.9 %collective-permute-start.3 = (bf16[64,2816]{1,0:T(8,128)(2,1)S(1)}, bf16[64,2816]{1,0:T(8,128)(2,1)S(1)}, u32[]{:S(2)}, u32[]{:S(2)}) collective-permute-start(bf16[64,2816]{1,0:T(8,128)(2,1)S(1)} %collective-permute-done.1.refs_2_), channel_id=1, source_target_pairs={{2,3},{1,0},{6,7},{5,4},{10,11},{9,8},{14,15},{13,12},{18,19},{17,... | collective-permute-start | bytes 1081352 | tf_op jit(solution)/shard_map/ppermute | solution.py:438
  24.0 8.3 %shard_map.63.refs_2_.refs_1_.active = bf16[2816,4096]{1,0:T(8,128)(2,1)S(1)} custom-call(s32[22]{0:T(128)} %listed.3, bf16[3072,4096]{1,0:T(8,128)(2,1)} %trailing.1), custom_call_target="tpu_custom_call" | custom-call | bytes 23068672 | tf_op jit(solution)/shard_map/pallas_call | solution.py:98
  32.2 2.9 %shard_map.65 = bf16[128,2048]{1,0:T(8,128)(2,1)S(1)} custom-call(s32[3]{0:T(128)S(1)} %pad_add_fusion.place, bf16[64,2816]{1,0:T(8,128)(2,1)S(1)} %shard_map.58.refs_0_, bf16[64,2816]{1,0:T(8,128)(2,1)S(1)} %collective-permute-done.refs_1_, bf16[2816,4096]{1,0:T(8,128)(2,1)S(1)} %shard_map.63.refs_2_.refs_1_.active), custom_call_target="tpu_custom_call" | custom-call | flops 1476395008 | bytes 11534336 | tf_op jit(solution)/shard_map/pallas_call | solution.py:187
  36.1 1.7 %shard_map.59 = (bf16[256,2816]{1,0:T(8,128)(2,1)S(1)}, f32[128,256]{1,0:T(8,128)S(1)}, f32[128,256]{1,0:T(8,128)S(1)}) custom-call(s32[3]{0:T(128)S(1)} %pad_add_fusion.place, bf16[64,2816]{1,0:T(8,128)(2,1)S(1)} %shard_map.58.refs_0_, bf16[64,2816]{1,0:T(8,128)(2,1)S(1)} %collective-permute-done.refs_1_, ...), custom_call_target="tpu_custom_call" | custom-call | flops 369098752 | bytes 2883584 | tf_op jit(solution)/shard_map/pallas_call | solution.py:136
  37.9 2.9 %shard_map.64.keep = f32[128,2048]{1,0:T(8,128)S(1)} custom-call(s32[3]{0:T(128)S(1)} %pad_add_fusion.place, bf16[64,2816]{1,0:T(8,128)(2,1)S(1)} %shard_map.58.refs_0_, bf16[64,2816]{1,0:T(8,128)(2,1)S(1)} %collective-permute-done.refs_1_, bf16[2816,4096]{1,0:T(8,128)(2,1)S(1)} %shard_map.63.refs_2_.refs_1_.active), custom_call_target="tpu_custom_call" | custom-call | flops 1476395008 | bytes 11534336 | tf_op jit(solution)/shard_map/pallas_call | solution.py:187
  40.8 2.2 %collective-permute-start.7 = (f32[128,256]{1,0:T(8,128)S(1)}, f32[128,256]{1,0:T(8,128)S(1)}, u32[]{:S(2)}, u32[]{:S(2)}) collective-permute-start(f32[128,256]{1,0:T(8,128)S(1)} %add.36), channel_id=1, source_target_pairs={{0,24},{4,28},{8,16},{12,20},{16,8},{20,12},{24,0},{28,4},{1,25},{... | collective-permute-start | bytes 393224 | tf_op jit(solution)/shard_map/ppermute | solution.py:217
  43.5 2.9 %shard_map.68 = bf16[128,2048]{1,0:T(8,128)(2,1)S(1)} custom-call(s32[3]{0:T(128)S(1)} %pad_add_fusion.place, bf16[256,2816]{1,0:T(8,128)(2,1)S(1)} %get-tuple-element.30.full.refs_0_, bf16[2816,4096]{1,0:T(8,128)(2,1)S(1)} %shard_map.63.refs_2_.refs_1_.active), custom_call_target="tpu_custom_call" | custom-call | flops 1476395008 | bytes 11534336 | tf_op jit(solution)/shard_map/pallas_call | solution.py:187
  46.4 1.4 %collective-permute-start.15 = (bf16[128,2048]{1,0:T(8,128)(2,1)S(1)}, bf16[128,2048]{1,0:T(8,128)(2,1)S(1)}, u32[]{:S(2)}, u32[]{:S(2)}) collective-permute-start(bf16[128,2048]{1,0:T(8,128)(2,1)S(1)} %shard_map.68), channel_id=1, source_target_pairs={{0,4},{4,0},{8,12},{12,8},{16,20},{20,16},{24,28},{28,24},{1,5},{5... | collective-permute-start | bytes 1572872 | tf_op jit(solution)/shard_map/ppermute | solution.py:217
  48.4 1.3 %collective-permute-start.10 = (bf16[128,512]{1,0:T(8,128)(2,1)S(1)}, bf16[128,512]{1,0:T(8,128)(2,1)S(1)}, u32[]{:S(2)}, u32[]{:S(2)}) collective-permute-start(bf16[128,512]{1,0:T(8,128)(2,1)S(1)} %get-tuple-element.34), channel_id=1, source_target_pairs={{0,8},{4,12},{8,0},{12,4},{16,24},{20,28},{24,16},{28,20},{1,9},{5... | collective-permute-start | bytes 393224 | tf_op jit(solution)/shard_map/ppermute | solution.py:217
  53.5 2.6 %collective-permute-done.11 = bf16[128,512]{1,0:T(8,128)(2,1)S(1)} collective-permute-done((bf16[128,512]{1,0:T(8,128)(2,1)S(1)}, bf16[128,512]{1,0:T(8,128)(2,1)S(1)}, u32[]{:S(2)}, u32[]{:S(2)}) %collective-permute-start.11) | collective-permute-done | bytes 131104 | tf_op jit(solution)/shard_map/ppermute | solution.py:217
  57.2 1.4 %collective-permute-start.13 = (bf16[1,128,512]{2,1,0:T(8,128)(2,1)S(1)}, bf16[1,128,512]{2,1,0:T(8,128)(2,1)S(1)}, u32[]{:S(2)}, u32[]{:S(2)}) collective-permute-start(bf16[1,128,512]{2,1,0:T(8,128)(2,1)S(1)} %fusion), channel_id=1, source_target_pairs={{0,8},{4,12},{8,0},{12,4},{16,24},{20,28},{24,16},{28,20},{1,9},{5... | collective-permute-start | bytes 393224 | tf_op jit(solution)/shard_map/ppermute | solution.py:217
  58.6 3.0 %shard_map.67.keep = f32[128,2048]{1,0:T(8,128)S(1)} custom-call(s32[3]{0:T(128)S(1)} %pad_add_fusion.place, bf16[256,2816]{1,0:T(8,128)(2,1)S(1)} %get-tuple-element.30.full.refs_0_, bf16[2816,4096]{1,0:T(8,128)(2,1)S(1)} %shard_map.63.refs_2_.refs_1_.active), custom_call_target="tpu_custom_call" | custom-call | flops 1476395008 | bytes 11534336 | tf_op jit(solution)/shard_map/pallas_call | solution.py:187
  62.5 1.3 %collective-permute-start.17 = (bf16[128,512]{1,0:T(8,128)(2,1)S(1)}, bf16[128,512]{1,0:T(8,128)(2,1)S(1)}, u32[]{:S(2)}, u32[]{:S(2)}) collective-permute-start(bf16[128,512]{1,0:T(8,128)(2,1)S(1)} %get-tuple-element.39), channel_id=1, source_target_pairs={{0,16},{4,20},{8,24},{12,28},{16,0},{20,4},{24,8},{28,12},{1,17},{... | collective-permute-start | bytes 393224 | tf_op jit(solution)/shard_map/ppermute | solution.py:217
  65.4 5.1 %shard_map.60 = (f32[128,384]{1,0:T(8,128)S(1)}, f32[128,128]{1,0:T(8,128)S(1)}) custom-call(s32[3]{0:T(128)S(1)} %pad_add_fusion.place, f32[128,256]{1,0:T(8,128)S(1)} %add_add_fusion.mine, f32[128,256]{1,0:T(8,128)S(1)} %collective-permute-done.8.theirs), custom_call_target="tpu_custom_call" | custom-call | flops 167772160 | bytes 20971520 | tf_op jit(solution)/shard_map/pallas_call | solution.py:340
  71.7 1.3 %collective-permute-start.20 = (bf16[128,512]{1,0:T(8,128)(2,1)S(1)}, bf16[128,512]{1,0:T(8,128)(2,1)S(1)}, u32[]{:S(2)}, u32[]{:S(2)}) collective-permute-start(bf16[128,512]{1,0:T(8,128)(2,1)S(1)} %add_convert_fusion.refs_0_), channel_id=1, source_target_pairs={{0,16},{4,20},{8,24},{12,28},{16,0},{20,4},{24,8},{28,12},{1,17},{... | collective-permute-start | bytes 393224 | tf_op jit(solution)/shard_map/ppermute | solution.py:217
  73.3 4.9 %shard_map.61 = (f32[256,256]{1,0:T(8,128)}, bf16[2,256,256]{2,1,0:T(8,128)(2,1)S(1)}, bf16[2,256,256]{2,1,0:T(8,128)(2,1)S(1)}) custom-call(f32[128,384]{1,0:T(8,128)S(1)} %get-tuple-element.27.first, f32[128,128]{1,0:T(8,128)S(1)} %get-tuple-element.28.rest), custom_call_target="tpu_custom_call" | custom-call | flops 167772160 | bytes 20971520 | tf_op jit(solution)/shard_map/pallas_call | solution.py:349
  78.3 3.4 %collective-permute-done.20.refs_2_ = bf16[128,512]{1,0:T(8,128)(2,1)S(1)} collective-permute-done((bf16[128,512]{1,0:T(8,128)(2,1)S(1)}, bf16[128,512]{1,0:T(8,128)(2,1)S(1)}, u32[]{:S(2)}, u32[]{:S(2)}) %collective-permute-start.20) | collective-permute-done | bytes 131104 | tf_op jit(solution)/shard_map/ppermute | solution.py:217
  81.7 2.6 %shard_map.70 = (f32[2048,256]{1,0:T(8,128)S(1)}, bf16[256,2048]{1,0:T(8,128)(2,1)S(1)}) custom-call(s32[3]{0:T(128)S(1)} %pad_add_fusion.place, bf16[2,256,256]{2,1,0:T(8,128)(2,1)S(1)} %get-tuple-element.31.inverse, bf16[2,256,256]{2,1,0:T(8,128)(2,1)S(1)} %get-tuple-element.32.turned, bf16[4,128,512]{2,1,0:T(8,128)(2,1)S(1)} %pad_maximum_fusion.one, ...), custom_call_target="tpu_custom_call" | custom-call | flops 1342177280 | bytes 4194304 | tf_op jit(solution)/shard_map/pallas_call | solution.py:379
  84.3 1.7 %collective-permute-start.23 = (f32[2048,256]{1,0:T(8,128)S(1)}, f32[2048,256]{1,0:T(8,128)S(1)}, u32[]{:S(2)}, u32[]{:S(2)}) collective-permute-start(f32[2048,256]{1,0:T(8,128)S(1)} %get-tuple-element.42.top), channel_id=1, source_target_pairs={{0,4},{4,0},{8,12},{12,8},{16,20},{20,16},{24,28},{28,24},{1,5},{5... | collective-permute-start | bytes 6291464 | tf_op jit(solution)/shard_map/ppermute | solution.py:217
  86.6 5.9 %shard_map.71 = (f32[4096,256]{1,0:T(8,128)}, bf16[2816,4096]{1,0:T(8,128)(2,1)}) custom-call(s32[3]{0:T(128)S(1)} %pad_add_fusion.place, bf16[2816,256]{1,0:T(8,128)(2,1)S(1)} %shard_map.62.panel, bf16[256,2048]{1,0:T(8,128)(2,1)S(1)} %get-tuple-element.41.coeff, f32[2048,256]{1,0:T(8,128)S(1)} %get-tuple-element.42.top, ...), custom_call_target="tpu_custom_call" | custom-call | flops 2952790016 | bytes 11534336 | tf_op jit(solution)/shard_map/pallas_call | solution.py:422
  92.6 5.9 %shard_map.72 = (f32[4096,256]{1,0:T(8,128)}, bf16[2816,4096]{1,0:T(8,128)(2,1)}) custom-call(s32[3]{0:T(128)S(1)} %pad_add_fusion.place, bf16[2816,256]{1,0:T(8,128)(2,1)S(1)} %shard_map.62.panel, bf16[256,2048]{1,0:T(8,128)(2,1)S(1)} %collective-permute-done.22.coeff, ...), custom_call_target="tpu_custom_call", output_to_operand_aliasing={{0}: (5, {}), {1}: (6, {})} | custom-call | flops 2952790016 | bytes 11534336 | tf_op jit(solution)/shard_map/pallas_call | solution.py:422
  (46 shorter events, 12.8 us)
Async XLA Ops:
  1.7 15.2 %collective-permute-start.1 = (bf16[64,2816]{1,0:T(8,128)(2,1)S(1)}, bf16[64,2816]{1,0:T(8,128)(2,1)S(1)}, u32[]{:S(2)}, u32[]{:S(2)}) collective-permute-start(bf16[64,2816]{1,0:T(8,128)(2,1)S(1)} %shard_map.58.refs_0_), channel_id=1, source_target_pairs={{0,2},{1,3},{2,0},{3,1},{4,6},{5,7},{6,4},{7,5},{8,10},{9,11},{10,... | collective-permute-start | bytes 1081352 | tf_op jit(solution)/shard_map/ppermute | solution.py:438
  1.8 30.4 %collective-permute-start = (bf16[64,2816]{1,0:T(8,128)(2,1)S(1)}, bf16[64,2816]{1,0:T(8,128)(2,1)S(1)}, u32[]{:S(2)}, u32[]{:S(2)}) collective-permute-start(bf16[64,2816]{1,0:T(8,128)(2,1)S(1)} %shard_map.58.refs_0_), channel_id=1, source_target_pairs={{0,1},{1,0},{2,3},{3,2},{4,5},{5,4},{6,7},{7,6},{8,9},{9,8},{10,11... | collective-permute-start | bytes 1081352 | tf_op jit(solution)/shard_map/ppermute | solution.py:438
  3.2 32.9 %collective-permute-start.2 = (bf16[64,2816]{1,0:T(8,128)(2,1)S(1)}, bf16[64,2816]{1,0:T(8,128)(2,1)S(1)}, u32[]{:S(2)}, u32[]{:S(2)}) collective-permute-start(bf16[64,2816]{1,0:T(8,128)(2,1)S(1)} %shard_map.58.refs_0_), channel_id=1, source_target_pairs={{1,2},{2,1},{5,6},{6,5},{9,10},{10,9},{13,14},{14,13},{17,18},{18,... | collective-permute-start | bytes 1081352 | tf_op jit(solution)/shard_map/ppermute | solution.py:438
  17.0 19.1 %collective-permute-start.3 = (bf16[64,2816]{1,0:T(8,128)(2,1)S(1)}, bf16[64,2816]{1,0:T(8,128)(2,1)S(1)}, u32[]{:S(2)}, u32[]{:S(2)}) collective-permute-start(bf16[64,2816]{1,0:T(8,128)(2,1)S(1)} %collective-permute-done.1.refs_2_), channel_id=1, source_target_pairs={{2,3},{1,0},{6,7},{5,4},{10,11},{9,8},{14,15},{13,12},{18,19},{17,... | collective-permute-start | bytes 1081352 | tf_op jit(solution)/shard_map/ppermute | solution.py:438
  35.1 12.6 %collective-permute-start.9 = (bf16[128,2048]{1,0:T(8,128)(2,1)S(1)}, bf16[128,2048]{1,0:T(8,128)(2,1)S(1)}, u32[]{:S(2)}, u32[]{:S(2)}) collective-permute-start(bf16[128,2048]{1,0:T(8,128)(2,1)S(1)} %shard_map.65), channel_id=1, source_target_pairs={{0,4},{4,0},{8,12},{12,8},{16,20},{20,16},{24,28},{28,24},{1,5},{5... | collective-permute-start | bytes 1572872 | tf_op jit(solution)/shard_map/ppermute | solution.py:217
  37.8 3.0 %collective-permute-start.4 = (f32[128,256]{1,0:T(8,128)S(1)}, f32[128,256]{1,0:T(8,128)S(1)}, u32[]{:S(2)}, u32[]{:S(2)}) collective-permute-start(f32[128,256]{1,0:T(8,128)S(1)} %get-tuple-element.26), channel_id=1, source_target_pairs={{0,4},{4,0},{8,12},{12,8},{16,20},{20,16},{24,28},{28,24},{1,5},{5... | collective-permute-start | bytes 393224 | tf_op jit(solution)/shard_map/ppermute | solution.py:217
  40.8 8.9 %collective-permute-start.7 = (f32[128,256]{1,0:T(8,128)S(1)}, f32[128,256]{1,0:T(8,128)S(1)}, u32[]{:S(2)}, u32[]{:S(2)}) collective-permute-start(f32[128,256]{1,0:T(8,128)S(1)} %add.36), channel_id=1, source_target_pairs={{0,24},{4,28},{8,16},{12,20},{16,8},{20,12},{24,0},{28,4},{1,25},{... | collective-permute-start | bytes 393224 | tf_op jit(solution)/shard_map/ppermute | solution.py:217
  43.0 7.9 %collective-permute-start.6 = (f32[128,256]{1,0:T(8,128)S(1)}, f32[128,256]{1,0:T(8,128)S(1)}, u32[]{:S(2)}, u32[]{:S(2)}) collective-permute-start(f32[128,256]{1,0:T(8,128)S(1)} %add.36), channel_id=1, source_target_pairs={{0,16},{4,20},{8,24},{12,28},{16,0},{20,4},{24,8},{28,12},{1,17},{... | collective-permute-start | bytes 393224 | tf_op jit(solution)/shard_map/ppermute | solution.py:217
  43.2 7.9 %collective-permute-start.5 = (f32[128,256]{1,0:T(8,128)S(1)}, f32[128,256]{1,0:T(8,128)S(1)}, u32[]{:S(2)}, u32[]{:S(2)}) collective-permute-start(f32[128,256]{1,0:T(8,128)S(1)} %add.36), channel_id=1, source_target_pairs={{0,8},{4,12},{8,0},{12,4},{16,24},{20,28},{24,16},{28,20},{1,9},{5... | collective-permute-start | bytes 393224 | tf_op jit(solution)/shard_map/ppermute | solution.py:217
  46.4 15.3 %collective-permute-start.15 = (bf16[128,2048]{1,0:T(8,128)(2,1)S(1)}, bf16[128,2048]{1,0:T(8,128)(2,1)S(1)}, u32[]{:S(2)}, u32[]{:S(2)}) collective-permute-start(bf16[128,2048]{1,0:T(8,128)(2,1)S(1)} %shard_map.68), channel_id=1, source_target_pairs={{0,4},{4,0},{8,12},{12,8},{16,20},{20,16},{24,28},{28,24},{1,5},{5... | collective-permute-start | bytes 1572872 | tf_op jit(solution)/shard_map/ppermute | solution.py:217
  48.4 5.1 %collective-permute-start.10 = (bf16[128,512]{1,0:T(8,128)(2,1)S(1)}, bf16[128,512]{1,0:T(8,128)(2,1)S(1)}, u32[]{:S(2)}, u32[]{:S(2)}) collective-permute-start(bf16[128,512]{1,0:T(8,128)(2,1)S(1)} %get-tuple-element.34), channel_id=1, source_target_pairs={{0,8},{4,12},{8,0},{12,4},{16,24},{20,28},{24,16},{28,20},{1,9},{5... | collective-permute-start | bytes 393224 | tf_op jit(solution)/shard_map/ppermute | solution.py:217
  49.7 6.5 %collective-permute-start.11 = (bf16[128,512]{1,0:T(8,128)(2,1)S(1)}, bf16[128,512]{1,0:T(8,128)(2,1)S(1)}, u32[]{:S(2)}, u32[]{:S(2)}) collective-permute-start(bf16[128,512]{1,0:T(8,128)(2,1)S(1)} %get-tuple-element.35), channel_id=1, source_target_pairs={{0,16},{4,20},{8,24},{12,28},{16,0},{20,4},{24,8},{28,12},{1,17},{... | collective-permute-start | bytes 393224 | tf_op jit(solution)/shard_map/ppermute | solution.py:217
  50.9 6.2 %collective-permute-start.12 = (bf16[128,512]{1,0:T(8,128)(2,1)S(1)}, bf16[128,512]{1,0:T(8,128)(2,1)S(1)}, u32[]{:S(2)}, u32[]{:S(2)}) collective-permute-start(bf16[128,512]{1,0:T(8,128)(2,1)S(1)} %get-tuple-element.36), channel_id=1, source_target_pairs={{0,24},{4,28},{8,16},{12,20},{16,8},{20,12},{24,0},{28,4},{1,25},{... | collective-permute-start | bytes 393224 | tf_op jit(solution)/shard_map/ppermute | solution.py:217
  51.2 14.3 %collective-permute-start.8 = (f32[128,256]{1,0:T(8,128)S(1)}, f32[128,256]{1,0:T(8,128)S(1)}, u32[]{:S(2)}, u32[]{:S(2)}) collective-permute-start(f32[128,256]{1,0:T(8,128)S(1)} %add_add_fusion.mine), channel_id=1, source_target_pairs={{0,4},{4,0},{8,12},{12,8},{16,20},{20,16},{24,28},{28,24},{1,5},{5... | collective-permute-start | bytes 393224 | tf_op jit(solution)/shard_map/ppermute | solution.py:217
  57.2 7.8 %collective-permute-start.13 = (bf16[1,128,512]{2,1,0:T(8,128)(2,1)S(1)}, bf16[1,128,512]{2,1,0:T(8,128)(2,1)S(1)}, u32[]{:S(2)}, u32[]{:S(2)}) collective-permute-start(bf16[1,128,512]{2,1,0:T(8,128)(2,1)S(1)} %fusion), channel_id=1, source_target_pairs={{0,8},{4,12},{8,0},{12,4},{16,24},{20,28},{24,16},{28,20},{1,9},{5... | collective-permute-start | bytes 393224 | tf_op jit(solution)/shard_map/ppermute | solution.py:217
  62.3 8.2 %collective-permute-start.16 = (bf16[128,512]{1,0:T(8,128)(2,1)S(1)}, bf16[128,512]{1,0:T(8,128)(2,1)S(1)}, u32[]{:S(2)}, u32[]{:S(2)}) collective-permute-start(bf16[128,512]{1,0:T(8,128)(2,1)S(1)} %get-tuple-element.38), channel_id=1, source_target_pairs={{0,8},{4,12},{8,0},{12,4},{16,24},{20,28},{24,16},{28,20},{1,9},{5... | collective-permute-start | bytes 393224 | tf_op jit(solution)/shard_map/ppermute | solution.py:217
  62.5 8.0 %collective-permute-start.17 = (bf16[128,512]{1,0:T(8,128)(2,1)S(1)}, bf16[128,512]{1,0:T(8,128)(2,1)S(1)}, u32[]{:S(2)}, u32[]{:S(2)}) collective-permute-start(bf16[128,512]{1,0:T(8,128)(2,1)S(1)} %get-tuple-element.39), channel_id=1, source_target_pairs={{0,16},{4,20},{8,24},{12,28},{16,0},{20,4},{24,8},{28,12},{1,17},{... | collective-permute-start | bytes 393224 | tf_op jit(solution)/shard_map/ppermute | solution.py:217
  63.9 6.7 %collective-permute-start.18 = (bf16[128,512]{1,0:T(8,128)(2,1)S(1)}, bf16[128,512]{1,0:T(8,128)(2,1)S(1)}, u32[]{:S(2)}, u32[]{:S(2)}) collective-permute-start(bf16[128,512]{1,0:T(8,128)(2,1)S(1)} %get-tuple-element.40), channel_id=1, source_target_pairs={{0,24},{4,28},{8,16},{12,20},{16,8},{20,12},{24,0},{28,4},{1,25},{... | collective-permute-start | bytes 393224 | tf_op jit(solution)/shard_map/ppermute | solution.py:217
  65.1 13.1 %collective-permute-start.14 = (bf16[2,128,512]{2,1,0:T(8,128)(2,1)S(1)}, bf16[2,128,512]{2,1,0:T(8,128)(2,1)S(1)}, u32[]{:S(2)}, u32[]{:S(2)}) collective-permute-start(bf16[2,128,512]{2,1,0:T(8,128)(2,1)S(1)} %pad_maximum_fusion.1), channel_id=1, source_target_pairs={{0,16},{4,20},{8,24},{12,28},{16,0},{20,4},{24,8},{28,12},{1,17},{... | collective-permute-start | bytes 786440 | tf_op jit(solution)/shard_map/ppermute | solution.py:217
  70.6 7.7 %collective-permute-start.21 = (bf16[128,512]{1,0:T(8,128)(2,1)S(1)}, bf16[128,512]{1,0:T(8,128)(2,1)S(1)}, u32[]{:S(2)}, u32[]{:S(2)}) collective-permute-start(bf16[128,512]{1,0:T(8,128)(2,1)S(1)} %add_convert_fusion.refs_0_), channel_id=1, source_target_pairs={{0,24},{4,28},{8,16},{12,20},{16,8},{20,12},{24,0},{28,4},{1,25},{... | collective-permute-start | bytes 393224 | tf_op jit(solution)/shard_map/ppermute | solution.py:217
  71.7 10.0 %collective-permute-start.20 = (bf16[128,512]{1,0:T(8,128)(2,1)S(1)}, bf16[128,512]{1,0:T(8,128)(2,1)S(1)}, u32[]{:S(2)}, u32[]{:S(2)}) collective-permute-start(bf16[128,512]{1,0:T(8,128)(2,1)S(1)} %add_convert_fusion.refs_0_), channel_id=1, source_target_pairs={{0,16},{4,20},{8,24},{12,28},{16,0},{20,4},{24,8},{28,12},{1,17},{... | collective-permute-start | bytes 393224 | tf_op jit(solution)/shard_map/ppermute | solution.py:217
  73.0 8.7 %collective-permute-start.19 = (bf16[128,512]{1,0:T(8,128)(2,1)S(1)}, bf16[128,512]{1,0:T(8,128)(2,1)S(1)}, u32[]{:S(2)}, u32[]{:S(2)}) collective-permute-start(bf16[128,512]{1,0:T(8,128)(2,1)S(1)} %add_convert_fusion.refs_0_), channel_id=1, source_target_pairs={{0,8},{4,12},{8,0},{12,4},{16,24},{20,28},{24,16},{28,20},{1,9},{5... | collective-permute-start | bytes 393224 | tf_op jit(solution)/shard_map/ppermute | solution.py:217
  84.3 8.2 %collective-permute-start.23 = (f32[2048,256]{1,0:T(8,128)S(1)}, f32[2048,256]{1,0:T(8,128)S(1)}, u32[]{:S(2)}, u32[]{:S(2)}) collective-permute-start(f32[2048,256]{1,0:T(8,128)S(1)} %get-tuple-element.42.top), channel_id=1, source_target_pairs={{0,4},{4,0},{8,12},{12,8},{16,20},{20,16},{24,28},{28,24},{1,5},{5... | collective-permute-start | bytes 6291464 | tf_op jit(solution)/shard_map/ppermute | solution.py:217
  86.1 6.5 %collective-permute-start.22 = (bf16[256,2048]{1,0:T(8,128)(2,1)S(1)}, bf16[256,2048]{1,0:T(8,128)(2,1)S(1)}, u32[]{:S(2)}, u32[]{:S(2)}) collective-permute-start(bf16[256,2048]{1,0:T(8,128)(2,1)S(1)} %get-tuple-element.41.coeff), channel_id=1, source_target_pairs={{0,4},{4,0},{8,12},{12,8},{16,20},{20,16},{24,28},{28,24},{1,5},{5... | collective-permute-start | bytes 3145736 | tf_op jit(solution)/shard_map/ppermute | solution.py:217

commit v6 on v5

--- a/solution.py
+++ b/solution.py
@@ -167,50 +167,47 @@
         lhs[k * across : (k + 1) * across, :] = full[pl.ds(pl.multiple_of(q * across, across), across), :]
 
 
-def cross_kernel(prepare, steps, mine, place, *refs):
+def cross_send_kernel(prepare, steps, place, *refs):
     *sources, active, out, lhs = refs
-    side = place[1] if mine else 1 - place[1]
     wide = out.shape[1] // steps
     prepare(place, sources, lhs)
 
-    def body(i, _):
-        source = pl.ds(pl.multiple_of(side * out.shape[1] + i * wide, wide), wide)
-        where = pl.ds(pl.multiple_of(i * wide, wide), wide)
-        out[:, where] = dot(lhs[...], active[:, source], ((1,), (0,))).astype(out.dtype)
-        return 0
-
-    lax.fori_loop(0, steps, body, 0)
-
-
-def cross(prepare, mine, deep, place, sources, active):
+    for i in range(steps):
+        source = pl.ds(pl.multiple_of((1 - place[1]) * out.shape[1] + i * wide, wide), wide)
+        out[:, i * wide : (i + 1) * wide] = dot(lhs[...], active[:, source], ((1,), (0,))).astype(out.dtype)
+
+
+def cross_send(prepare, deep, place, sources, active):
     rows, columns = active.shape
     return call(
-        functools.partial(cross_kernel, prepare, 4, mine),
-        shape((deep, columns // 2), F32 if mine else BF16), [SMEM] + [VMEM] * (len(sources) + 1), VMEM, 8,
-        flops=deep * rows * columns, moved=rows * columns,
-        scratch=(pltpu.VMEM((deep, rows), BF16),),
+        functools.partial(cross_send_kernel, prepare, 4), shape((deep, columns // 2), BF16),
+        [SMEM] + [VMEM] * (len(sources) + 1), VMEM, 8,
+        flops=deep * rows * columns, moved=rows * columns, scratch=(pltpu.VMEM((deep, rows), BF16),),
     )(place, *sources, active)
 
 
-def share_kernel(place, keep, got, own, *outs):
-    chip = place[2]
-    wide = own.shape[1]
-
-    def total(where):
-        return keep[:, where] + got[:, where].astype(F32)
-
-    own[...] = total(pl.ds(pl.multiple_of(chip * wide, wide), wide))
-    for s, out in enumerate(outs, 1):
-        out[...] = total(pl.ds(pl.multiple_of((chip ^ s) * wide, wide), wide)).astype(BF16)
-
-
-def share(place, keep, got, chips):
-    deep, columns = keep.shape
-    wide = columns // chips
-    return call(
-        share_kernel, [shape((deep, wide), F32)] + [shape((deep, wide), BF16)] * (chips - 1),
-        [SMEM, VMEM, VMEM], [VMEM] * chips, 8, moved=8 * deep * columns,
-    )(place, keep, got)
+def cross_keep_kernel(prepare, chips, place, *refs):
+    *sources, got, active = refs[: -1 - chips]
+    outs, lhs = refs[-1 - chips : -1], refs[-1]
+    wide = outs[0].shape[1]
+    prepare(place, sources, lhs)
+    for s, out in enumerate(outs):
+        chunk = place[2] ^ s
+        source = pl.ds(pl.multiple_of((place[1] * chips + chunk) * wide, wide), wide)
+        where = pl.ds(pl.multiple_of(chunk * wide, wide), wide)
+        total = dot(lhs[...], active[:, source], ((1,), (0,))) + got[:, where].astype(F32)
+        out[...] = total.astype(out.dtype)
+
+
+def cross_keep(prepare, deep, place, sources, got, active, chips):
+    rows, columns = active.shape
+    dims = (deep, columns // (2 * chips))
+    return call(
+        functools.partial(cross_keep_kernel, prepare, chips),
+        [shape(dims, F32)] + [shape(dims, BF16)] * (chips - 1),
+        [SMEM] + [VMEM] * (len(sources) + 2), [VMEM] * chips, 8,
+        flops=deep * rows * columns, moved=rows * columns, scratch=(pltpu.VMEM((deep, rows), BF16),),
+    )(place, *sources, got, active)
 
 
 def swap(value, bit, rows):
@@ -228,9 +225,7 @@
     return [1 << k for k in range(1, rows.bit_length() - 1)]
 
 
-def reduce_cross(place, keep, got, rows):
-    chips = rows // 2
-    own, *outs = share(place, keep, got, chips)
+def reduce_cross(own, outs, rows):
     parts = [own] + [swap(v, 2 * s, rows) for s, v in enumerate(outs, 1)]
     return tree(parts).astype(BF16)
 
@@ -456,9 +451,9 @@
     active = load(tile_list, trailing)
 
     def both(prepare, deep, sources):
-        send = swap(cross(prepare, False, deep, place, sources, active), 1, nrow)
-        keep = cross(prepare, True, deep, place, sources, active)
-        return reduce_cross(place, keep, send, nrow)
+        got = swap(cross_send(prepare, deep, place, sources, active), 1, nrow)
+        own, *outs = cross_keep(prepare, deep, place, sources, got, active, chips)
+        return reduce_cross(own, outs, nrow)
 
     one = gather_slow(both(pair_lhs, across, blocks[:2]), nrow)
     full, keep, send = gram(place, blocks, ncol)

time: 99 us -> 99.1 us (level)
  local copies, waits for them, and re-layouts: 0 us -> 17.7 us
  waiting for transfers between devices: 18.9 us -> 7.94 us
  Pallas kernels: 48.9 us -> 45.2 us
  starting transfers between devices: 29.4 us -> 26 us
    unnamed x0 -> x6, local copies, waits for them, and re-layouts: none -> 17.7 us
    ppermute x4, waiting for transfers between devices: 10.6 us -> 0.01 us  [shift(): return lax.ppermute(value, 'col', pairs)]
    ppermute x4, starting transfers between devices: 11.5 us -> 5.9 us  [shift(): return lax.ppermute(value, 'col', pairs)]
    pallas_call x6 -> x4, Pallas kernels: 13 us -> 9.1 us  [the longest x2 4.55 us: cross_keep(): call(functools.partial(cross_keep_kernel, prepare, chips), [shape(dims, F...]
    ppermute x20, starting transfers between devices: 17.9 us -> 20.1 us  [swap(): return lax.ppermute(value, 'row', [(i, i ^ bit) for i in range(rows)])]
  transfers between devices with their start and end apart: 24 -> 24, of which waited for: 5 -> 4; matrix products, arithmetic and copies ran while one was open for 0% -> 0% of each run, Pallas kernels for 40% -> 36%
where the time goes in v6:
time: 99.1 us; the launch traced here: 98.2 us
  Pallas kernels  45.2 us (46%)
  starting transfers between devices  26 us (26%)
  local copies, waits for them, and re-layouts  17.7 us (18%)
  waiting for transfers between devices  7.94 us (8%)
  between operations  1.03 us (1%)
    ppermute x20, starting transfers between devices, swap(): return lax.ppermute(value, 'row', [(i, i ^ bit) for i in range(rows)])  20.1 us
    unnamed x6, local copies, waits for them, and re-layouts  17.7 us
    pallas_call x2, Pallas kernels, update(): call(functools.partial(update_kernel, chips, mine), (shape((columns, size...  11.9 us
    pallas_call x1, Pallas kernels, load(): call(load_kernel, pltpu.VMEM((rows, columns), BF16), [HBM, HBM], VMEM, 8,...  8.27 us
    ppermute x20, waiting for transfers between devices, swap(): return lax.ppermute(value, 'row', [(i, i ^ bit) for i in range(rows)])  7.93 us
    ppermute x4, starting transfers between devices, shift(): return lax.ppermute(value, 'col', pairs)  5.9 us
    pallas_call x1, Pallas kernels, factor_first(): call(factor_first_kernel, (shape((h, 3 * h), F32), shape((h, h), F32)), [...  5.07 us
    pallas_call x1, Pallas kernels, factor_last(): call(factor_last_kernel, (shape((size, size), F32), both, both), [VMEM, V...  4.89 us
  transfers between devices with their start and end apart: 24, of which 4 were waited for; matrix products, arithmetic and copies ran while one was open for 0% of the time, Pallas kernels for 36%

profile of v6, /device:TPU:17, one launch (start us, length us, event | category | flops | bytes accessed | tf_op | source)
XLA Modules:
  0.0 98.2 jit_solution(12922518866713175841)
XLA Ops:
  1.8 1.4 %collective-permute-start = (bf16[64,2816]{1,0:T(8,128)(2,1)S(1)}, bf16[64,2816]{1,0:T(8,128)(2,1)S(1)}, u32[]{:S(2)}, u32[]{:S(2)}) collective-permute-start(bf16[64,2816]{1,0:T(8,128)(2,1)S(1)} %shard_map.58.refs_0_), channel_id=1, source_target_pairs={{0,1},{1,0},{2,3},{3,2},{4,5},{5,4},{6,7},{7,6},{8,9},{9,8},{10,11... | collective-permute-start | bytes 1081352 | tf_op jit(solution)/shard_map/ppermute | solution.py:433
  3.2 3.2 %collective-permute-start.2 = (bf16[64,2816]{1,0:T(8,128)(2,1)S(1)}, bf16[64,2816]{1,0:T(8,128)(2,1)S(1)}, u32[]{:S(2)}, u32[]{:S(2)}) collective-permute-start(bf16[64,2816]{1,0:T(8,128)(2,1)S(1)} %shard_map.58.refs_0_), channel_id=1, source_target_pairs={{1,2},{2,1},{5,6},{6,5},{9,10},{10,9},{13,14},{14,13},{17,18},{18,... | collective-permute-start | bytes 1081352 | tf_op jit(solution)/shard_map/ppermute | solution.py:433
  6.4 8.3 %shard_map.63.refs_2_.refs_3_.refs_1_.active = bf16[2816,4096]{1,0:T(8,128)(2,1)S(1)} custom-call(s32[22]{0:T(128)} %listed.3, bf16[3072,4096]{1,0:T(8,128)(2,1)} %trailing.1), custom_call_target="tpu_custom_call" | custom-call | bytes 23068672 | tf_op jit(solution)/shard_map/pallas_call | solution.py:98
  14.7 8.2 %copy-done = bf16[2816,4096]{1,0:T(8,128)(2,1)} copy-done((bf16[2816,4096]{1,0:T(8,128)(2,1)}, bf16[2816,4096]{1,0:T(8,128)(2,1)S(1)}, u32[]{:S(2)}) %copy-start) | copy-done | bytes 23068696
  24.3 7.6 %copy-done.1 = bf16[2816,4096]{1,0:T(8,128)(2,1)S(1)} copy-done((bf16[2816,4096]{1,0:T(8,128)(2,1)S(1)}, bf16[2816,4096]{1,0:T(8,128)(2,1)}, u32[]{:S(2)}) %copy-start.1) | copy-done | bytes 23068696
  31.9 2.3 %shard_map.64 = bf16[128,2048]{1,0:T(8,128)(2,1)S(1)} custom-call(s32[3]{0:T(128)S(1)} %pad_add_fusion.place, bf16[64,2816]{1,0:T(8,128)(2,1)S(1)} %shard_map.58.refs_0_, bf16[64,2816]{1,0:T(8,128)(2,1)S(1)} %collective-permute-done.refs_1_, bf16[2816,4096]{1,0:T(8,128)(2,1)S(1)} %copy-done.1), custom_call_target="tpu_custom_call" | custom-call | flops 1476395008 | bytes 11534336 | tf_op jit(solution)/shard_map/pallas_call | solution.py:182
  34.1 1.6 %collective-permute-start.9 = (bf16[128,2048]{1,0:T(8,128)(2,1)S(1)}, bf16[128,2048]{1,0:T(8,128)(2,1)S(1)}, u32[]{:S(2)}, u32[]{:S(2)}) collective-permute-start(bf16[128,2048]{1,0:T(8,128)(2,1)S(1)} %shard_map.64), channel_id=1, source_target_pairs={{0,4},{4,0},{8,12},{12,8},{16,20},{20,16},{24,28},{28,24},{1,5},{5... | collective-permute-start | bytes 1572872 | tf_op jit(solution)/shard_map/ppermute | solution.py:214
  35.7 1.7 %shard_map.59 = (bf16[256,2816]{1,0:T(8,128)(2,1)S(1)}, f32[128,256]{1,0:T(8,128)S(1)}, f32[128,256]{1,0:T(8,128)S(1)}) custom-call(s32[3]{0:T(128)S(1)} %pad_add_fusion.place, bf16[64,2816]{1,0:T(8,128)(2,1)S(1)} %shard_map.58.refs_0_, bf16[64,2816]{1,0:T(8,128)(2,1)S(1)} %collective-permute-done.refs_1_, ...), custom_call_target="tpu_custom_call" | custom-call | flops 369098752 | bytes 2883584 | tf_op jit(solution)/shard_map/pallas_call | solution.py:136
  37.5 1.9 %copy-done.2 = bf16[2816,4096]{1,0:T(8,128)(2,1)S(1)} copy-done((bf16[2816,4096]{1,0:T(8,128)(2,1)S(1)}, bf16[2816,4096]{1,0:T(8,128)(2,1)}, u32[]{:S(2)}) %copy-start.2) | copy-done | bytes 23068696
  39.4 2.3 %shard_map.66 = bf16[128,2048]{1,0:T(8,128)(2,1)S(1)} custom-call(s32[3]{0:T(128)S(1)} %pad_add_fusion.place, bf16[256,2816]{1,0:T(8,128)(2,1)S(1)} %get-tuple-element.30.full.refs_0_, bf16[2816,4096]{1,0:T(8,128)(2,1)S(1)} %copy-done.2), custom_call_target="tpu_custom_call" | custom-call | flops 1476395008 | bytes 11534336 | tf_op jit(solution)/shard_map/pallas_call | solution.py:182
  41.7 1.6 %collective-permute-start.15 = (bf16[128,2048]{1,0:T(8,128)(2,1)S(1)}, bf16[128,2048]{1,0:T(8,128)(2,1)S(1)}, u32[]{:S(2)}, u32[]{:S(2)}) collective-permute-start(bf16[128,2048]{1,0:T(8,128)(2,1)S(1)} %shard_map.66), channel_id=1, source_target_pairs={{0,4},{4,0},{8,12},{12,8},{16,20},{20,16},{24,28},{28,24},{1,5},{5... | collective-permute-start | bytes 1572872 | tf_op jit(solution)/shard_map/ppermute | solution.py:214
  43.3 2.2 %collective-permute-start.7 = (f32[128,256]{1,0:T(8,128)S(1)}, f32[128,256]{1,0:T(8,128)S(1)}, u32[]{:S(2)}, u32[]{:S(2)}) collective-permute-start(f32[128,256]{1,0:T(8,128)S(1)} %add.36), channel_id=1, source_target_pairs={{0,24},{4,28},{8,16},{12,20},{16,8},{20,12},{24,0},{28,4},{1,25},{... | collective-permute-start | bytes 393224 | tf_op jit(solution)/shard_map/ppermute | solution.py:214
  46.0 2.3 %shard_map.65 = (f32[128,512]{1,0:T(8,128)S(1)}, bf16[128,512]{1,0:T(8,128)(2,1)S(1)}, bf16[128,512]{1,0:T(8,128)(2,1)S(1)}, bf16[128,512]{1,0:T(8,128)(2,1)S(1)}) custom-call(s32[3]{0:T(128)S(1)} %pad_add_fusion.place, bf16[64,2816]{1,0:T(8,128)(2,1)S(1)} %shard_map.58.refs_0_, bf16[64,2816]{1,0:T(8,128)(2,1)S(1)} %collective-permute-done.refs_1_, ...), custom_call_target="tpu_custom_call" | custom-call | flops 1476395008 | bytes 11534336 | tf_op jit(solution)/shard_map/pallas_call | solution.py:205
  50.8 1.7 %collective-permute-done.6 = f32[128,256]{1,0:T(8,128)S(1)} collective-permute-done((f32[128,256]{1,0:T(8,128)S(1)}, f32[128,256]{1,0:T(8,128)S(1)}, u32[]{:S(2)}, u32[]{:S(2)}) %collective-permute-start.6) | collective-permute-done | bytes 131104 | tf_op jit(solution)/shard_map/ppermute | solution.py:214
  53.4 1.5 %collective-permute-start.8 = (f32[128,256]{1,0:T(8,128)S(1)}, f32[128,256]{1,0:T(8,128)S(1)}, u32[]{:S(2)}, u32[]{:S(2)}) collective-permute-start(f32[128,256]{1,0:T(8,128)S(1)} %add_add_fusion.mine), channel_id=1, source_target_pairs={{0,4},{4,0},{8,12},{12,8},{16,20},{20,16},{24,28},{28,24},{1,5},{5... | collective-permute-start | bytes 393224 | tf_op jit(solution)/shard_map/ppermute | solution.py:214
  55.0 2.9 %collective-permute-done.12 = bf16[128,512]{1,0:T(8,128)(2,1)S(1)} collective-permute-done((bf16[128,512]{1,0:T(8,128)(2,1)S(1)}, bf16[128,512]{1,0:T(8,128)(2,1)S(1)}, u32[]{:S(2)}, u32[]{:S(2)}) %collective-permute-start.12) | collective-permute-done | bytes 131104 | tf_op jit(solution)/shard_map/ppermute | solution.py:214
  59.3 2.3 %shard_map.67 = (f32[128,512]{1,0:T(8,128)S(1)}, bf16[128,512]{1,0:T(8,128)(2,1)S(1)}, bf16[128,512]{1,0:T(8,128)(2,1)S(1)}, bf16[128,512]{1,0:T(8,128)(2,1)S(1)}) custom-call(s32[3]{0:T(128)S(1)} %pad_add_fusion.place, bf16[256,2816]{1,0:T(8,128)(2,1)S(1)} %get-tuple-element.30.full.refs_0_, bf16[128,2048]{1,0:T(8,128)(2,1)S(1)} %collective-permute-done.15.refs_1_, ...), custom_call_target="tpu_custom_call" | custom-call | flops 1476395008 | bytes 11534336 | tf_op jit(solution)/shard_map/pallas_call | solution.py:205
  65.0 5.1 %shard_map.60 = (f32[128,384]{1,0:T(8,128)S(1)}, f32[128,128]{1,0:T(8,128)S(1)}) custom-call(s32[3]{0:T(128)S(1)} %pad_add_fusion.place, f32[128,256]{1,0:T(8,128)S(1)} %add_add_fusion.mine, f32[128,256]{1,0:T(8,128)S(1)} %collective-permute-done.8.theirs), custom_call_target="tpu_custom_call" | custom-call | flops 167772160 | bytes 20971520 | tf_op jit(solution)/shard_map/pallas_call | solution.py:335
  72.9 4.9 %shard_map.61 = (f32[256,256]{1,0:T(8,128)}, bf16[2,256,256]{2,1,0:T(8,128)(2,1)S(1)}, bf16[2,256,256]{2,1,0:T(8,128)(2,1)S(1)}) custom-call(f32[128,384]{1,0:T(8,128)S(1)} %get-tuple-element.27.first, f32[128,128]{1,0:T(8,128)S(1)} %get-tuple-element.28.rest), custom_call_target="tpu_custom_call" | custom-call | flops 167772160 | bytes 20971520 | tf_op jit(solution)/shard_map/pallas_call | solution.py:344
  77.9 3.1 %collective-permute-done.20.refs_2_ = bf16[128,512]{1,0:T(8,128)(2,1)S(1)} collective-permute-done((bf16[128,512]{1,0:T(8,128)(2,1)S(1)}, bf16[128,512]{1,0:T(8,128)(2,1)S(1)}, u32[]{:S(2)}, u32[]{:S(2)}) %collective-permute-start.20) | collective-permute-done | bytes 131104 | tf_op jit(solution)/shard_map/ppermute | solution.py:214
  81.0 2.8 %shard_map.68 = (f32[2048,256]{1,0:T(8,128)S(1)}, bf16[256,2048]{1,0:T(8,128)(2,1)S(1)}) custom-call(s32[3]{0:T(128)S(1)} %pad_add_fusion.place, bf16[2,256,256]{2,1,0:T(8,128)(2,1)S(1)} %get-tuple-element.31.inverse, bf16[2,256,256]{2,1,0:T(8,128)(2,1)S(1)} %get-tuple-element.32.turned, bf16[4,128,512]{2,1,0:T(8,128)(2,1)S(1)} %pad_maximum_fusion.one, ...), custom_call_target="tpu_custom_call" | custom-call | flops 1342177280 | bytes 4194304 | tf_op jit(solution)/shard_map/pallas_call | solution.py:374
  83.8 1.8 %collective-permute-start.23 = (f32[2048,256]{1,0:T(8,128)S(1)}, f32[2048,256]{1,0:T(8,128)S(1)}, u32[]{:S(2)}, u32[]{:S(2)}) collective-permute-start(f32[2048,256]{1,0:T(8,128)S(1)} %get-tuple-element.42.top), channel_id=1, source_target_pairs={{0,4},{4,0},{8,12},{12,8},{16,20},{20,16},{24,28},{28,24},{1,5},{5... | collective-permute-start | bytes 6291464 | tf_op jit(solution)/shard_map/ppermute | solution.py:214
  86.2 5.9 %shard_map.69 = (f32[4096,256]{1,0:T(8,128)}, bf16[2816,4096]{1,0:T(8,128)(2,1)}) custom-call(s32[3]{0:T(128)S(1)} %pad_add_fusion.place, bf16[2816,256]{1,0:T(8,128)(2,1)S(1)} %shard_map.62.panel, bf16[256,2048]{1,0:T(8,128)(2,1)S(1)} %get-tuple-element.41.coeff, f32[2048,256]{1,0:T(8,128)S(1)} %get-tuple-element.42.top, bf16[2816,4096]{1,0:T(8,128)(2,1)S(1)} %copy-done.2), custom_call_target="tpu_custom_call" | custom-call | flops 2952790016 | bytes 11534336 | tf_op jit(solution)/shard_map/pallas_call | solution.py:417
  92.1 5.9 %shard_map.70 = (f32[4096,256]{1,0:T(8,128)}, bf16[2816,4096]{1,0:T(8,128)(2,1)}) custom-call(s32[3]{0:T(128)S(1)} %pad_add_fusion.place, bf16[2816,256]{1,0:T(8,128)(2,1)S(1)} %shard_map.62.panel, bf16[256,2048]{1,0:T(8,128)(2,1)S(1)} %collective-permute-done.22.coeff, ...), custom_call_target="tpu_custom_call", output_to_operand_aliasing={{0}: (5, {}), {1}: (6, {})} | custom-call | flops 2952790016 | bytes 11534336 | tf_op jit(solution)/shard_map/pallas_call | solution.py:417
  (50 shorter events, 14.8 us)
Async XLA Ops:
  1.7 21.2 %collective-permute-start.1 = (bf16[64,2816]{1,0:T(8,128)(2,1)S(1)}, bf16[64,2816]{1,0:T(8,128)(2,1)S(1)}, u32[]{:S(2)}, u32[]{:S(2)}) collective-permute-start(bf16[64,2816]{1,0:T(8,128)(2,1)S(1)} %shard_map.58.refs_0_), channel_id=1, source_target_pairs={{0,2},{1,3},{2,0},{3,1},{4,6},{5,7},{6,4},{7,5},{8,10},{9,11},{10,... | collective-permute-start | bytes 1081352 | tf_op jit(solution)/shard_map/ppermute | solution.py:433
  1.8 22.5 %collective-permute-start = (bf16[64,2816]{1,0:T(8,128)(2,1)S(1)}, bf16[64,2816]{1,0:T(8,128)(2,1)S(1)}, u32[]{:S(2)}, u32[]{:S(2)}) collective-permute-start(bf16[64,2816]{1,0:T(8,128)(2,1)S(1)} %shard_map.58.refs_0_), channel_id=1, source_target_pairs={{0,1},{1,0},{2,3},{3,2},{4,5},{5,4},{6,7},{7,6},{8,9},{9,8},{10,11... | collective-permute-start | bytes 1081352 | tf_op jit(solution)/shard_map/ppermute | solution.py:433
  3.2 32.5 %collective-permute-start.2 = (bf16[64,2816]{1,0:T(8,128)(2,1)S(1)}, bf16[64,2816]{1,0:T(8,128)(2,1)S(1)}, u32[]{:S(2)}, u32[]{:S(2)}) collective-permute-start(bf16[64,2816]{1,0:T(8,128)(2,1)S(1)} %shard_map.58.refs_0_), channel_id=1, source_target_pairs={{1,2},{2,1},{5,6},{6,5},{9,10},{10,9},{13,14},{14,13},{17,18},{18,... | collective-permute-start | bytes 1081352 | tf_op jit(solution)/shard_map/ppermute | solution.py:433
  23.0 12.8 %collective-permute-start.3 = (bf16[64,2816]{1,0:T(8,128)(2,1)S(1)}, bf16[64,2816]{1,0:T(8,128)(2,1)S(1)}, u32[]{:S(2)}, u32[]{:S(2)}) collective-permute-start(bf16[64,2816]{1,0:T(8,128)(2,1)S(1)} %collective-permute-done.1.refs_2_), channel_id=1, source_target_pairs={{2,3},{1,0},{6,7},{5,4},{10,11},{9,8},{14,15},{13,12},{18,19},{17,... | collective-permute-start | bytes 1081352 | tf_op jit(solution)/shard_map/ppermute | solution.py:433
  34.1 11.9 %collective-permute-start.9 = (bf16[128,2048]{1,0:T(8,128)(2,1)S(1)}, bf16[128,2048]{1,0:T(8,128)(2,1)S(1)}, u32[]{:S(2)}, u32[]{:S(2)}) collective-permute-start(bf16[128,2048]{1,0:T(8,128)(2,1)S(1)} %shard_map.64), channel_id=1, source_target_pairs={{0,4},{4,0},{8,12},{12,8},{16,20},{20,16},{24,28},{28,24},{1,5},{5... | collective-permute-start | bytes 1572872 | tf_op jit(solution)/shard_map/ppermute | solution.py:214
  37.4 5.9 %collective-permute-start.4 = (f32[128,256]{1,0:T(8,128)S(1)}, f32[128,256]{1,0:T(8,128)S(1)}, u32[]{:S(2)}, u32[]{:S(2)}) collective-permute-start(f32[128,256]{1,0:T(8,128)S(1)} %get-tuple-element.26), channel_id=1, source_target_pairs={{0,4},{4,0},{8,12},{12,8},{16,20},{20,16},{24,28},{28,24},{1,5},{5... | collective-permute-start | bytes 393224 | tf_op jit(solution)/shard_map/ppermute | solution.py:214
  41.7 17.6 %collective-permute-start.15 = (bf16[128,2048]{1,0:T(8,128)(2,1)S(1)}, bf16[128,2048]{1,0:T(8,128)(2,1)S(1)}, u32[]{:S(2)}, u32[]{:S(2)}) collective-permute-start(bf16[128,2048]{1,0:T(8,128)(2,1)S(1)} %shard_map.66), channel_id=1, source_target_pairs={{0,4},{4,0},{8,12},{12,8},{16,20},{20,16},{24,28},{28,24},{1,5},{5... | collective-permute-start | bytes 1572872 | tf_op jit(solution)/shard_map/ppermute | solution.py:214
  43.3 6.3 %collective-permute-start.7 = (f32[128,256]{1,0:T(8,128)S(1)}, f32[128,256]{1,0:T(8,128)S(1)}, u32[]{:S(2)}, u32[]{:S(2)}) collective-permute-start(f32[128,256]{1,0:T(8,128)S(1)} %add.36), channel_id=1, source_target_pairs={{0,24},{4,28},{8,16},{12,20},{16,8},{20,12},{24,0},{28,4},{1,25},{... | collective-permute-start | bytes 393224 | tf_op jit(solution)/shard_map/ppermute | solution.py:214
  45.5 7.0 %collective-permute-start.6 = (f32[128,256]{1,0:T(8,128)S(1)}, f32[128,256]{1,0:T(8,128)S(1)}, u32[]{:S(2)}, u32[]{:S(2)}) collective-permute-start(f32[128,256]{1,0:T(8,128)S(1)} %add.36), channel_id=1, source_target_pairs={{0,16},{4,20},{8,24},{12,28},{16,0},{20,4},{24,8},{28,12},{1,17},{... | collective-permute-start | bytes 393224 | tf_op jit(solution)/shard_map/ppermute | solution.py:214
  45.8 7.5 %collective-permute-start.5 = (f32[128,256]{1,0:T(8,128)S(1)}, f32[128,256]{1,0:T(8,128)S(1)}, u32[]{:S(2)}, u32[]{:S(2)}) collective-permute-start(f32[128,256]{1,0:T(8,128)S(1)} %add.36), channel_id=1, source_target_pairs={{0,8},{4,12},{8,0},{12,4},{16,24},{20,28},{24,16},{28,20},{1,9},{5... | collective-permute-start | bytes 393224 | tf_op jit(solution)/shard_map/ppermute | solution.py:214
  48.3 6.7 %collective-permute-start.10 = (bf16[128,512]{1,0:T(8,128)(2,1)S(1)}, bf16[128,512]{1,0:T(8,128)(2,1)S(1)}, u32[]{:S(2)}, u32[]{:S(2)}) collective-permute-start(bf16[128,512]{1,0:T(8,128)(2,1)S(1)} %get-tuple-element.34), channel_id=1, source_target_pairs={{0,8},{4,12},{8,0},{12,4},{16,24},{20,28},{24,16},{28,20},{1,9},{5... | collective-permute-start | bytes 393224 | tf_op jit(solution)/shard_map/ppermute | solution.py:214
  49.6 5.5 %collective-permute-start.11 = (bf16[128,512]{1,0:T(8,128)(2,1)S(1)}, bf16[128,512]{1,0:T(8,128)(2,1)S(1)}, u32[]{:S(2)}, u32[]{:S(2)}) collective-permute-start(bf16[128,512]{1,0:T(8,128)(2,1)S(1)} %get-tuple-element.35), channel_id=1, source_target_pairs={{0,16},{4,20},{8,24},{12,28},{16,0},{20,4},{24,8},{28,12},{1,17},{... | collective-permute-start | bytes 393224 | tf_op jit(solution)/shard_map/ppermute | solution.py:214
  52.5 5.4 %collective-permute-start.12 = (bf16[128,512]{1,0:T(8,128)(2,1)S(1)}, bf16[128,512]{1,0:T(8,128)(2,1)S(1)}, u32[]{:S(2)}, u32[]{:S(2)}) collective-permute-start(bf16[128,512]{1,0:T(8,128)(2,1)S(1)} %get-tuple-element.36), channel_id=1, source_target_pairs={{0,24},{4,28},{8,16},{12,20},{16,8},{20,12},{24,0},{28,4},{1,25},{... | collective-permute-start | bytes 393224 | tf_op jit(solution)/shard_map/ppermute | solution.py:214
  53.4 11.7 %collective-permute-start.8 = (f32[128,256]{1,0:T(8,128)S(1)}, f32[128,256]{1,0:T(8,128)S(1)}, u32[]{:S(2)}, u32[]{:S(2)}) collective-permute-start(f32[128,256]{1,0:T(8,128)S(1)} %add_add_fusion.mine), channel_id=1, source_target_pairs={{0,4},{4,0},{8,12},{12,8},{16,20},{20,16},{24,28},{28,24},{1,5},{5... | collective-permute-start | bytes 393224 | tf_op jit(solution)/shard_map/ppermute | solution.py:214
  58.0 6.3 %collective-permute-start.13 = (bf16[1,128,512]{2,1,0:T(8,128)(2,1)S(1)}, bf16[1,128,512]{2,1,0:T(8,128)(2,1)S(1)}, u32[]{:S(2)}, u32[]{:S(2)}) collective-permute-start(bf16[1,128,512]{2,1,0:T(8,128)(2,1)S(1)} %fusion), channel_id=1, source_target_pairs={{0,8},{4,12},{8,0},{12,4},{16,24},{20,28},{24,16},{28,20},{1,9},{5... | collective-permute-start | bytes 393224 | tf_op jit(solution)/shard_map/ppermute | solution.py:214
  61.6 8.5 %collective-permute-start.16 = (bf16[128,512]{1,0:T(8,128)(2,1)S(1)}, bf16[128,512]{1,0:T(8,128)(2,1)S(1)}, u32[]{:S(2)}, u32[]{:S(2)}) collective-permute-start(bf16[128,512]{1,0:T(8,128)(2,1)S(1)} %get-tuple-element.38), channel_id=1, source_target_pairs={{0,8},{4,12},{8,0},{12,4},{16,24},{20,28},{24,16},{28,20},{1,9},{5... | collective-permute-start | bytes 393224 | tf_op jit(solution)/shard_map/ppermute | solution.py:214
  61.9 8.2 %collective-permute-start.17 = (bf16[128,512]{1,0:T(8,128)(2,1)S(1)}, bf16[128,512]{1,0:T(8,128)(2,1)S(1)}, u32[]{:S(2)}, u32[]{:S(2)}) collective-permute-start(bf16[128,512]{1,0:T(8,128)(2,1)S(1)} %get-tuple-element.39), channel_id=1, source_target_pairs={{0,16},{4,20},{8,24},{12,28},{16,0},{20,4},{24,8},{28,12},{1,17},{... | collective-permute-start | bytes 393224 | tf_op jit(solution)/shard_map/ppermute | solution.py:214
  63.1 7.0 %collective-permute-start.18 = (bf16[128,512]{1,0:T(8,128)(2,1)S(1)}, bf16[128,512]{1,0:T(8,128)(2,1)S(1)}, u32[]{:S(2)}, u32[]{:S(2)}) collective-permute-start(bf16[128,512]{1,0:T(8,128)(2,1)S(1)} %get-tuple-element.40), channel_id=1, source_target_pairs={{0,24},{4,28},{8,16},{12,20},{16,8},{20,12},{24,0},{28,4},{1,25},{... | collective-permute-start | bytes 393224 | tf_op jit(solution)/shard_map/ppermute | solution.py:214
  64.3 13.5 %collective-permute-start.14 = (bf16[2,128,512]{2,1,0:T(8,128)(2,1)S(1)}, bf16[2,128,512]{2,1,0:T(8,128)(2,1)S(1)}, u32[]{:S(2)}, u32[]{:S(2)}) collective-permute-start(bf16[2,128,512]{2,1,0:T(8,128)(2,1)S(1)} %pad_maximum_fusion.1), channel_id=1, source_target_pairs={{0,16},{4,20},{8,24},{12,28},{16,0},{20,4},{24,8},{28,12},{1,17},{... | collective-permute-start | bytes 786440 | tf_op jit(solution)/shard_map/ppermute | solution.py:214
  70.2 7.7 %collective-permute-start.21 = (bf16[128,512]{1,0:T(8,128)(2,1)S(1)}, bf16[128,512]{1,0:T(8,128)(2,1)S(1)}, u32[]{:S(2)}, u32[]{:S(2)}) collective-permute-start(bf16[128,512]{1,0:T(8,128)(2,1)S(1)} %add_convert_fusion.refs_0_), channel_id=1, source_target_pairs={{0,24},{4,28},{8,16},{12,20},{16,8},{20,12},{24,0},{28,4},{1,25},{... | collective-permute-start | bytes 393224 | tf_op jit(solution)/shard_map/ppermute | solution.py:214
  71.1 9.9 %collective-permute-start.20 = (bf16[128,512]{1,0:T(8,128)(2,1)S(1)}, bf16[128,512]{1,0:T(8,128)(2,1)S(1)}, u32[]{:S(2)}, u32[]{:S(2)}) collective-permute-start(bf16[128,512]{1,0:T(8,128)(2,1)S(1)} %add_convert_fusion.refs_0_), channel_id=1, source_target_pairs={{0,16},{4,20},{8,24},{12,28},{16,0},{20,4},{24,8},{28,12},{1,17},{... | collective-permute-start | bytes 393224 | tf_op jit(solution)/shard_map/ppermute | solution.py:214
  72.3 8.6 %collective-permute-start.19 = (bf16[128,512]{1,0:T(8,128)(2,1)S(1)}, bf16[128,512]{1,0:T(8,128)(2,1)S(1)}, u32[]{:S(2)}, u32[]{:S(2)}) collective-permute-start(bf16[128,512]{1,0:T(8,128)(2,1)S(1)} %add_convert_fusion.refs_0_), channel_id=1, source_target_pairs={{0,8},{4,12},{8,0},{12,4},{16,24},{20,28},{24,16},{28,20},{1,9},{5... | collective-permute-start | bytes 393224 | tf_op jit(solution)/shard_map/ppermute | solution.py:214
  83.8 8.3 %collective-permute-start.23 = (f32[2048,256]{1,0:T(8,128)S(1)}, f32[2048,256]{1,0:T(8,128)S(1)}, u32[]{:S(2)}, u32[]{:S(2)}) collective-permute-start(f32[2048,256]{1,0:T(8,128)S(1)} %get-tuple-element.42.top), channel_id=1, source_target_pairs={{0,4},{4,0},{8,12},{12,8},{16,20},{20,16},{24,28},{28,24},{1,5},{5... | collective-permute-start | bytes 6291464 | tf_op jit(solution)/shard_map/ppermute | solution.py:214
  85.7 6.5 %collective-permute-start.22 = (bf16[256,2048]{1,0:T(8,128)(2,1)S(1)}, bf16[256,2048]{1,0:T(8,128)(2,1)S(1)}, u32[]{:S(2)}, u32[]{:S(2)}) collective-permute-start(bf16[256,2048]{1,0:T(8,128)(2,1)S(1)} %get-tuple-element.41.coeff), channel_id=1, source_target_pairs={{0,4},{4,0},{8,12},{12,8},{16,20},{20,16},{24,28},{28,24},{1,5},{5... | collective-permute-start | bytes 3145736 | tf_op jit(solution)/shard_map/ppermute | solution.py:214
  (3 other events, 23.4 us)
